TPU v7x, 512 devices: a whole 4x4x16 slice. The times are simulated.
512 devices in a mesh: occ: 64 (over x, z), vir: 8 (over y, core).
Axes of the slice: x: 4, y: 4, z: 16, core: 2. Of those that a mesh axis runs over, the one named last changes fastest.
Arguments:
- t2_tiles: float32 [64, 8, 4, 128, 256], P('occ', 'vir'), may hold values from -6 to 6
- cycle_ints: float32 [64, 8, 4, 256, 128], P('occ', 'vir'), may hold values from -0.21875 to 0.21875
- cycle_left: int32 [64, 8, 96], P('occ', 'vir'), may hold values from 0 to 3
- cycle_right: int32 [64, 8, 96], P('occ', 'vir'), may hold values from 0 to 3
- cycle_dest: int32 [64, 8, 96], P('occ', 'vir'), may hold values from 0 to 127, as said below
- lam_ladder: float32 [16384, 4096], P('occ', 'vir'), may hold values from -6 to 6
- ladder_ints: float32 [4096, 1024], P('vir'), may hold values from -0.09375 to 0.09375
- ladder_mask: int32 [128, 32], P('occ', 'vir'), may hold values 0 or 1
- partner_slot: int32 [64, 2], P('occ'), may hold values from 0 to 1, as said below
- denom: float32 [16384, 1024], P('occ', 'vir'), may hold values from 1 to 8
Outputs:
- increment: float32 [16384, 1024], P('occ', 'vir')
Inputs may be any that keep to these rules, and one draw needn't show every extreme that they name: One device's tasks name each owner (cycle_dest // 2) at most 3 times; in each vir column one owner is named exactly 3 times by every device. `partner_slot`: each row is a permutation of the 2 slots.
All inputs are finite; a program needn't handle non-finite values. No bound on the sum of `ladder_mask` on one device may be relied on, other than what follows from the above.
Results may differ from a plain program's by a relative error of at most 0.0001.
Values sent between devices are 32-bit elements; how exact they have to be, the bound alone decides.
No kernel may reach another device: no remote copies, remote signals or barrier semaphores. Data moves between devices by JAX's collectives and lax.ppermute only.
A program may use at most 128 MiB of HBM per device.

v0:
```python
import jax
import jax.numpy as jnp
from jax import lax
from jax.sharding import PartitionSpec as P

CAP = 3


def partner_2(array, axis, distance):
    return lax.ppermute(array, axis, [(i, i ^ 1 << distance) for i in range(lax.axis_size(axis))])


def body(
    t2_tiles,
    cycle_ints,
    cycle_left,
    cycle_right,
    cycle_dest,
    lam_ladder,
    ladder_ints,
    ladder_mask,
    partner_slot,
    denom,
):
    highest = lax.Precision.HIGHEST
    owned = partner_slot.shape[1]
    edge = denom.shape[1]
    blocks = ladder_mask.shape[1]
    n_occ = lax.axis_size("occ")
    shaped = lam_ladder.reshape(owned, edge, blocks, edge)
    masked = (shaped * ladder_mask.astype(jnp.float32)[:, None, :, None]).reshape(
        owned * edge, blocks * edge
    )
    partial_ladder = jnp.dot(masked, ladder_ints, precision=highest)
    ladder = lax.psum_scatter(partial_ladder, "vir", scatter_dimension=1, tiled=True)
    left_tiles = t2_tiles[0, 0]
    right_tiles = cycle_ints[0, 0]
    lefts = cycle_left[0, 0]
    rights = cycle_right[0, 0]
    dests = cycle_dest[0, 0]
    count = dests.shape[0]

    def task_block(pair):
        lidx, ridx = pair
        return jnp.einsum("btk,bkc->btc", left_tiles[lidx], right_tiles[ridx], precision=highest)

    partials = lax.map(task_block, (lefts.reshape(-1, 8), rights.reshape(-1, 8))).reshape(
        count, edge, edge
    )
    owners = dests // owned
    slots = dests % owned
    onehot = (owners[:, None] == jnp.arange(n_occ, dtype=jnp.int32)[None, :]).astype(jnp.int32)
    before = jnp.cumsum(onehot, axis=0) - onehot
    rank = jnp.sum(before * onehot, axis=1)
    position = owners * CAP + rank
    slot_task = (
        jax.ops.segment_sum(
            jnp.arange(count, dtype=jnp.int32) + 1, position, num_segments=n_occ * CAP
        )
        - 1
    )
    valid = slot_task >= 0
    index = jnp.maximum(slot_task, 0)
    send_tiles = (partials[index] * valid.astype(jnp.float32)[:, None, None]).reshape(
        n_occ, CAP, edge, edge
    )
    send_slots = jnp.where(valid, slots[index], owned).reshape(n_occ, CAP)
    got_tiles, got_slots = (
        lax.all_to_all(send_tiles, "occ", split_axis=0, concat_axis=0, tiled=True),
        lax.all_to_all(send_slots, "occ", split_axis=0, concat_axis=0, tiled=True),
    )
    select = (got_slots[:, :, None] == jnp.arange(owned, dtype=jnp.int32)[None, None, :]).astype(
        jnp.float32
    )
    cycle = jnp.einsum("ncij,ncs->sij", got_tiles, select, precision=highest)
    resid = ladder.reshape(owned, edge, edge) + cycle
    moved = resid
    for bit in range(n_occ.bit_length() - 1):
        moved = partner_2(moved, "occ", bit)
    partner = moved[partner_slot[0]][:, ::-1, ::-1]
    sym = (resid + partner).reshape(owned * edge, edge)
    return sym / denom


def solution(mesh):
    in_specs = (
        P("occ", "vir", None, None, None),
        P("occ", "vir", None, None, None),
        P("occ", "vir", None),
        P("occ", "vir", None),
        P("occ", "vir", None),
        P("occ", "vir"),
        P("vir", None),
        P("occ", "vir"),
        P("occ", None),
        P("occ", "vir"),
    )
    out_specs = P("occ", "vir")
    return jax.shard_map(body, mesh=mesh, in_specs=in_specs, out_specs=out_specs, check_vma=False)
```

profile of v0, /device:TPU:24, one launch (start us, length us, event | category | flops | bytes accessed | tf_op | source)
XLA Modules:
  0.0 803.7 jit_solution(17789336024252845694)
XLA Ops:
  12.0 18.6 %all-to-all-start = ((s32[64,1,3]{2,1,0:T(1,128)}), s32[64,1,3]{2,1,0:T(1,128)S(1)}, u32[]{:S(2)}, u32[]{:S(2)}) async-start(s32[64,1,3]{2,1,0:T(1,128)} %bitcast.10), calls=%async_computation.1 | async-start | bytes 65536 | tf_op jit(solution)/shard_map/all_to_all | solution.py:70
  33.7 90.4 %while.10 = (s32[]{:T(128)}, f32[12,8,128,128]{3,2,1,0:T(8,128)}, s32[12,8]{1,0:T(8,128)S(1)}, f32[4,128,256]{2,1,0:T(8,128)}, s32[12,8]{1,0:T(8,128)S(1)}, /*index=5*/f32[4,256,128]{2,1,0:T(8,128)}, s32[]{:T(128)}) while((s32[]{:T(128)}, f32[12,8,128,128]{3,2,1,0:T(8,128)}, s32[12,8]{1,0:T(8,128)S(1)}, f32[4,128,256]{2,1,0:T(8,128)}, ...), condition=%wide.region_5.6_spmd, body=%wide.region_4.5_spmd.sunk | while | flops 402655296 | bytes 6824785 | solution.py:47
  33.8 1.7 gather_fusion
  35.4 2.7 gather_fusion.1
  38.1 3.2 fusion.35
  43.0 2.7 gather_fusion.1
  45.6 3.2 fusion.35
  50.5 2.7 gather_fusion.1
  53.1 3.2 fusion.35
  58.0 2.7 gather_fusion.1
  60.7 3.2 fusion.35
  65.5 2.7 gather_fusion.1
  68.2 3.2 fusion.35
  71.4 1.7 gather_fusion
  73.1 2.7 gather_fusion.1
  75.7 3.2 fusion.35
  80.6 2.7 gather_fusion.1
  83.3 3.2 fusion.35
  88.1 2.7 gather_fusion.1
  90.8 3.2 fusion.35
  95.6 2.7 gather_fusion.1
  98.3 3.2 fusion.35
  103.2 2.7 gather_fusion.1
  105.8 3.2 fusion.35
  109.0 1.7 gather_fusion
  110.7 2.7 gather_fusion.1
  113.4 3.2 fusion.35
  118.3 2.7 gather_fusion.1
  120.9 3.2 fusion.35
  124.1 13.3 %gather_fusion.3 = f32[192,128,128]{2,1,0:T(8,128)} fusion(f32[96,128,128]{2,1,0:T(8,128)} %bitcast.93, s32[1024]{0:T(1024)S(1)} %pad_clamp_fusion.3), kind=kCustom, calls=%fused_computation.3 | custom fusion | bytes 25166592 | tf_op jit(solution)/shard_map/gather | solution.py:64
  137.6 10.0 %broadcast_multiply_fusion = f32[64,3,128,128]{3,2,1,0:T(8,128)} fusion(f32[64,3,128,128]{3,2,1,0:T(8,128)} %bitcast.92, f32[64,3]{1,0:T(8,128)S(1)} %reshape.201), kind=kLoop, calls=%fused_computation.20 | loop fusion | flops 3145728 | bytes 25166592 | tf_op jit(solution)/shard_map/mul | solution.py:64
  147.6 15.5 %all-to-all-start.1 = ((f32[64,3,128,128]{3,2,1,0:T(8,128)}), f32[64,3,128,128]{3,2,1,0:T(8,128)}, u32[]{:S(2)}, u32[]{:S(2)}) async-start(f32[64,3,128,128]{3,2,1,0:T(8,128)} %broadcast_multiply_fusion), calls=%async_computation.2 | async-start | bytes 25165824 | tf_op jit(solution)/shard_map/all_to_all | solution.py:69
  163.5 3.0 fusion.13
  166.6 38.2 %reduce-scatter.2.cloned.1.call-done = f32[256,128]{1,0:T(8,128)} async-done(((f32[256,1024]{1,0:T(8,128)}), f32[256,128]{1,0:T(8,128)}) %reduce-scatter.2.cloned.1.call-update) | async-done | bytes 131088 | tf_op jit(solution)/shard_map/reduce_scatter | solution.py:35
  204.8 504.5 %all-to-all-done.1 = f32[64,3,128,128]{3,2,1,0:T(8,128)} async-done(((f32[64,3,128,128]{3,2,1,0:T(8,128)}), f32[64,3,128,128]{3,2,1,0:T(8,128)}, u32[]{:S(2)}, u32[]{:S(2)}) %all-to-all-start.1) | async-done | bytes 12582944 | tf_op jit(solution)/shard_map/all_to_all | solution.py:69
  709.4 15.2 %fusion.10 = f32[2,128,128]{2,0,1:T(2,128)S(1)} fusion(f32[64,3,128,128]{3,2,1,0:T(8,128)} %all-to-all-done.1, f32[2,128,128]{2,1,0:T(8,128)} %bitcast.95, s32[64,3]{0,1:T(4,128)S(1)} %copy.28), kind=kOutput, calls=%fused_computation.22 | convolution fusion | flops 75530624 | bytes 12845824 | tf_op jit(solution)/shard_map/ncij,ncs->sij/dot_general | solution.py:75
  724.6 3.9 collective-permute-start
  728.5 3.0 collective-permute-done
  731.5 3.8 collective-permute-start.1
  735.3 4.0 collective-permute-done.1
  739.2 7.0 collective-permute-start.2
  746.2 10.0 %collective-permute-done.2 = f32[2,128,128]{2,0,1:T(2,128)S(1)} collective-permute-done((f32[2,128,128]{2,0,1:T(2,128)S(1)}, f32[2,128,128]{2,0,1:T(2,128)S(1)}, u32[]{:S(2)}, u32[]{:S(2)}) %collective-permute-start.2) | collective-permute-done | bytes 131104 | tf_op jit(solution)/shard_map/ppermute | solution.py:10
  756.2 12.0 %collective-permute-start.3 = (f32[2,128,128]{2,0,1:T(2,128)S(1)}, f32[2,128,128]{2,0,1:T(2,128)S(1)}, u32[]{:S(2)}, u32[]{:S(2)}) collective-permute-start(f32[2,128,128]{2,0,1:T(2,128)S(1)} %collective-permute-done.2), channel_id=1, source_target_pairs={{0,64},{8,72},{16,80},{24,88},{32,96},{40,104},{48,112},{56,120},{... | collective-permute-start | bytes 393224 | tf_op jit(solution)/shard_map/ppermute | solution.py:10
  768.2 11.3 %collective-permute-done.3 = f32[2,128,128]{2,0,1:T(2,128)S(1)} collective-permute-done((f32[2,128,128]{2,0,1:T(2,128)S(1)}, f32[2,128,128]{2,0,1:T(2,128)S(1)}, u32[]{:S(2)}, u32[]{:S(2)}) %collective-permute-start.3) | collective-permute-done | bytes 131104 | tf_op jit(solution)/shard_map/ppermute | solution.py:10
  779.5 1.9 collective-permute-start.4
  781.4 5.4 collective-permute-done.4
  786.8 1.9 collective-permute-start.5
  788.7 6.4 collective-permute-done.5
  (90 shorter events, 26.0 us)
Async XLA Ops:
  6.5 157.0 %copy-start = (f32[512,1024]{1,0:T(8,128)S(1)}, f32[512,1024]{1,0:T(8,128)}, u32[]{:S(2)}) copy-start(f32[512,1024]{1,0:T(8,128)} %param.18) | copy-start | bytes 6291460
  12.0 135.6 %all-to-all-start = ((s32[64,1,3]{2,1,0:T(1,128)}), s32[64,1,3]{2,1,0:T(1,128)S(1)}, u32[]{:S(2)}, u32[]{:S(2)}) async-start(s32[64,1,3]{2,1,0:T(1,128)} %bitcast.10), calls=%async_computation.1 | async-start | bytes 65536 | tf_op jit(solution)/shard_map/all_to_all | solution.py:70
  147.6 15.8 %copy-start.3 = (s32[2,4]{1,0:T(2,128)S(1)}, s32[2,4]{1,0:T(2,128)}, u32[]{:S(2)}) copy-start(s32[2,4]{1,0:T(2,128)} %param.19) | copy-start | bytes 100
  147.6 15.9 %copy-start.1 = (f32[256,512]{1,0:T(8,128)S(1)}, f32[256,512]{1,0:T(8,128)}, u32[]{:S(2)}) copy-start(f32[256,512]{1,0:T(8,128)} %param.17) | copy-start | bytes 1572868
  147.6 561.8 %all-to-all-start.1 = ((f32[64,3,128,128]{3,2,1,0:T(8,128)}), f32[64,3,128,128]{3,2,1,0:T(8,128)}, u32[]{:S(2)}, u32[]{:S(2)}) async-start(f32[64,3,128,128]{3,2,1,0:T(8,128)} %broadcast_multiply_fusion), calls=%async_computation.2 | async-start | bytes 25165824 | tf_op jit(solution)/shard_map/all_to_all | solution.py:69
  163.1 625.6 %copy-start.4 = (s32[1,2]{1,0:T(1,128)S(1)}, s32[1,2]{1,0:T(1,128)}, u32[]{:S(2)}) copy-start(s32[1,2]{1,0:T(1,128)} %param.20) | copy-start | bytes 28
  163.1 633.1 %copy-start.2 = (f32[256,128]{1,0:T(8,128)S(1)}, f32[256,128]{1,0:T(8,128)}, u32[]{:S(2)}) copy-start(f32[256,128]{1,0:T(8,128)} %param.21) | copy-start | bytes 393220
  163.1 41.7 %reduce-scatter.2.cloned.1.call-start = ((), (), s32[]{:S(2)}) async-start(), calls=%async_computation.3 | async-start | bytes 1179648 | tf_op jit(solution)/shard_map/reduce_scatter | solution.py:35
  724.6 6.9 collective-permute-start
  731.5 7.7 collective-permute-start.1
  739.2 17.0 %collective-permute-start.2 = (f32[2,128,128]{2,0,1:T(2,128)S(1)}, f32[2,128,128]{2,0,1:T(2,128)S(1)}, u32[]{:S(2)}, u32[]{:S(2)}) collective-permute-start(f32[2,128,128]{2,0,1:T(2,128)S(1)} %collective-permute-done.1), channel_id=1, source_target_pairs={{0,32},{8,40},{16,48},{24,56},{32,0},{40,8},{48,16},{56,24},{64,96... | collective-permute-start | bytes 393224 | tf_op jit(solution)/shard_map/ppermute | solution.py:10
  756.2 23.3 %collective-permute-start.3 = (f32[2,128,128]{2,0,1:T(2,128)S(1)}, f32[2,128,128]{2,0,1:T(2,128)S(1)}, u32[]{:S(2)}, u32[]{:S(2)}) collective-permute-start(f32[2,128,128]{2,0,1:T(2,128)S(1)} %collective-permute-done.2), channel_id=1, source_target_pairs={{0,64},{8,72},{16,80},{24,88},{32,96},{40,104},{48,112},{56,120},{... | collective-permute-start | bytes 393224 | tf_op jit(solution)/shard_map/ppermute | solution.py:10
  779.5 7.3 collective-permute-start.4
  786.8 8.4 %collective-permute-start.5 = (f32[2,128,128]{2,0,1:T(2,128)S(1)}, f32[2,128,128]{2,0,1:T(2,128)S(1)}, u32[]{:S(2)}, u32[]{:S(2)}) collective-permute-start(f32[2,128,128]{2,0,1:T(2,128)S(1)} %collective-permute-done.4), channel_id=1, source_target_pairs={{0,256},{8,264},{16,272},{24,280},{32,288},{40,296},{48,304},{56,3... | collective-permute-start | bytes 393224 | tf_op jit(solution)/shard_map/ppermute | solution.py:10
Sparse Core Ops, SparseCore 0:
  166.8 37.9 reduce-scatter.1
where the time goes:
time: 805 us; the launch traced here: 804 us
  waiting for transfers between devices  583 us (72%)
  local copies, waits for them, and re-layouts  69.4 us (9%)
  starting transfers between devices  64.7 us (8%)
  matrix products  56.2 us (7%)
  other arithmetic  16.6 us (2%)
  between operations  13.7 us (2%)
    all_to_all x1, waiting for transfers between devices, body(): lax.all_to_all(send_tiles, 'occ', split_axis=0, concat_axis=0, tiled=True)  505 us
    ppermute x6, waiting for transfers between devices, partner_2(): lax.ppermute(array, axis, [(i, i ^ 1 << distance) for i in range(lax.axis...  40 us
    reduce_scatter x1, waiting for transfers between devices, body(): lax.psum_scatter(partial_ladder, 'vir', scatter_dimension=1, tiled=True)  38.2 us
    dot_general x12, matrix products, task_block(): jnp.einsum('btk,bkc->btc', left_tiles[lidx], right_tiles[ridx], precision...  38 us
    gather x12, local copies, waits for them, and re-layouts, task_block(): right_tiles[ridx]  31.9 us
    ppermute x6, starting transfers between devices, partner_2(): lax.ppermute(array, axis, [(i, i ^ 1 << distance) for i in range(lax.axis...  30.4 us
    gather x12, local copies, waits for them, and re-layouts, task_block(): left_tiles[lidx]  19.9 us
    all_to_all x1, starting transfers between devices, body(): lax.all_to_all(send_slots, 'occ', split_axis=0, concat_axis=0, tiled=True)  18.6 us
  transfers between devices with their start and end apart: 9, of which 8 were waited for; matrix products, arithmetic and copies ran while one was open for 15% of the time, Pallas kernels for 0%

commit v1 on v0

v1 whole, which is shorter than its diff:
```python
import jax
import jax.numpy as jnp
from jax import lax
from jax.experimental import pallas as pl
from jax.experimental.pallas import tpu as pltpu
from jax.sharding import Mesh
from jax.sharding import PartitionSpec as P

CAP = 3
EDGE = 128
OWN = 2
XT = 4
NX = 4
NZ = 16
TASKS = 96
ENTRIES = NX * NZ * CAP
PAIRS = XT * XT
TABLE = 8
ROWS = PAIRS * EDGE + TABLE
NEAR = (0, 1, -1, 2)
HIGHEST = lax.Precision.HIGHEST
SMEM = pltpu.SMEM
VMEM = pltpu.VMEM


def products_kernel(lefts, rights, dests, t2_ref, ints_ref, out_ref, count):
    n_owner = NX * NZ

    def clear(i, c):
        count[i] = 0
        return c

    lax.fori_loop(0, n_owner, clear, 0)
    where = (
        lax.broadcasted_iota(jnp.int32, (TABLE, EDGE), 0) * EDGE
        + lax.broadcasted_iota(jnp.int32, (TABLE, EDGE), 1)
    )

    def place(t, table):
        dest = dests[t]
        owner = dest // OWN
        rank = count[owner]
        count[owner] = rank + 1
        entry = (dest - owner * OWN) * PAIRS + lefts[t] * XT + rights[t]
        return jnp.where(where == owner * CAP + rank, entry, table)

    table = lax.fori_loop(0, TASKS, place, jnp.full((TABLE, EDGE), -1, jnp.int32))
    out_ref[PAIRS * EDGE :, :] = table.astype(jnp.float32)
    right = jnp.concatenate([ints_ref[r] for r in range(XT)], axis=1)
    for l in range(XT):
        tile = jnp.dot(
            t2_ref[l], right, precision=HIGHEST, preferred_element_type=jnp.float32
        )
        for r in range(XT):
            out_ref[pl.ds((l * XT + r) * EDGE, EDGE), :] = tile[:, r * EDGE : (r + 1) * EDGE]


def ladder_kernel(mask, lam_ref, ints_ref, out_ref):
    blocks = lam_ref.shape[1] // EDGE
    for s in range(OWN):
        rows = [
            lam_ref[pl.ds(s * EDGE, EDGE), pl.ds(b * EDGE, EDGE)]
            * mask[s, b].astype(jnp.float32)
            for b in range(blocks)
        ]
        part = jnp.dot(
            jnp.concatenate(rows, axis=1),
            ints_ref[...],
            precision=HIGHEST,
            preferred_element_type=jnp.float32,
        )
        for q in range(out_ref.shape[0]):
            out_ref[q, pl.ds(s * EDGE, EDGE), :] = part[:, q * EDGE : (q + 1) * EDGE]


def gather_kernel(where, t0, t1, t2, t3, p0, p1, p2, p3, o0, o1, o2, o3):
    base = where[0] * NZ
    z = where[1]
    sign = where[2]
    tables = (t0, t1, t2, t3)
    tiles = (p0, p1, p2, p3)
    for near, out in zip(NEAR, (o0, o1, o2, o3)):

        def dest(a, c, near=near, out=out):
            target = lax.rem(z + sign * (near + 4 * a) + 4 * NZ, NZ)
            start = (base + target) * CAP
            acc = [jnp.zeros((EDGE, EDGE), jnp.float32) for _ in range(OWN)]
            for table, tile in zip(tables, tiles):
                for k in range(CAP):
                    entry = table[start + k]
                    slot = lax.shift_right_arithmetic(entry, 4)
                    code = jnp.bitwise_and(jnp.maximum(entry, 0), PAIRS - 1)
                    at = pl.multiple_of(code * EDGE, EDGE)
                    val = tile[pl.ds(at, EDGE), :]
                    for s in range(OWN):
                        acc[s] = acc[s] + val * (slot == s).astype(jnp.float32)
            for s in range(OWN):
                out[a, pl.ds(s * EDGE, EDGE), :] = acc[s]
            return c

        lax.fori_loop(0, 4, dest, 0)


def signed(axis_size, distance):
    pairs = []
    for i in range(axis_size):
        for c in range(2):
            step = distance if c == 0 else -distance
            pairs.append((i * 2 + c, (i + step) % axis_size * 2 + c))
    return pairs


def move(array, axis, size, distance):
    return lax.ppermute(array, (axis, "c"), signed(size, distance))


def vm(n):
    return [pl.BlockSpec(memory_space=VMEM)] * n


def sm(n):
    return [pl.BlockSpec(memory_space=SMEM)] * n


def body(
    t2_tiles,
    cycle_ints,
    cycle_left,
    cycle_right,
    cycle_dest,
    lam_ladder,
    ladder_ints,
    ladder_mask,
    partner_slot,
    denom,
):
    f32 = jnp.float32
    x = lax.axis_index("x")
    z = lax.axis_index("z")
    c = lax.axis_index("c")
    payload = pl.pallas_call(
        products_kernel,
        out_shape=jax.ShapeDtypeStruct((ROWS, EDGE), f32),
        in_specs=sm(3) + vm(2),
        out_specs=pl.BlockSpec(memory_space=VMEM),
        scratch_shapes=[pltpu.SMEM((NX * NZ,), jnp.int32)],
        name="products",
    )(cycle_left[0, 0], cycle_right[0, 0], cycle_dest[0, 0], t2_tiles[0, 0], cycle_ints[0, 0])
    got_a = move(payload, "x", NX, 1)
    got_b = move(payload, "x", NX, -1)
    got_c = move(got_a, "x", NX, 1)
    partial = pl.pallas_call(
        ladder_kernel,
        out_shape=jax.ShapeDtypeStruct((8, OWN * EDGE, EDGE), f32),
        in_specs=sm(1) + vm(2),
        out_specs=pl.BlockSpec(memory_space=VMEM),
        name="ladder",
    )(ladder_mask, lam_ladder, ladder_ints)
    spread = lax.all_to_all(partial, ("y", "c"), split_axis=0, concat_axis=0, tiled=True)
    ladder = jnp.sum(spread, axis=0)

    arrays = (payload, got_a, got_b, got_c)
    tables = [a[PAIRS * EDGE :].reshape(-1)[:ENTRIES].astype(jnp.int32) for a in arrays]
    place = jnp.stack([x, z, 1 - 2 * c]).astype(jnp.int32)
    near = pl.pallas_call(
        gather_kernel,
        out_shape=[jax.ShapeDtypeStruct((4, OWN * EDGE, EDGE), f32)] * 4,
        in_specs=sm(5) + vm(4),
        out_specs=vm(4),
        name="gather",
    )(place, *tables, *arrays)
    moved = [move(near[j], "z", NZ, NEAR[j]) for j in (1, 2, 3)]
    far = [near[0][a] + moved[0][a] + moved[1][a] + moved[2][a] for a in range(4)]
    far = [far[0]] + [move(far[a], "z", NZ, 4 * a) for a in (1, 3, 2)]
    resid = (ladder + far[0] + far[1] + far[2] + far[3]).reshape(OWN, EDGE, EDGE)
    n_occ = NX * NZ
    other = lax.ppermute(resid, ("x", "z"), [(i, n_occ - 1 - i) for i in range(n_occ)])
    partner = other[partner_slot[0]][:, ::-1, ::-1]
    return (resid + partner).reshape(OWN * EDGE, EDGE) / denom


def solution(mesh):
    grid = Mesh(mesh.devices.reshape(NX, NZ, 4, 2), ("x", "z", "y", "c"))
    occ = ("x", "z")
    vir = ("y", "c")
    in_specs = (
        P(occ, vir, None, None, None),
        P(occ, vir, None, None, None),
        P(occ, vir, None),
        P(occ, vir, None),
        P(occ, vir, None),
        P(occ, vir),
        P(vir, None),
        P(occ, vir),
        P(occ, None),
        P(occ, vir),
    )
    return jax.shard_map(
        body, mesh=grid, in_specs=in_specs, out_specs=P(occ, vir), check_vma=False
    )
```

time: 805 us -> 144 us (0.18)
  waiting for transfers between devices: 583 us -> 53.5 us
  local copies, waits for them, and re-layouts: 69.4 us -> 2.11 us
  matrix products: 56.2 us -> 0 us
  Pallas kernels: 0 us -> 15.9 us
  between operations: 13.7 us -> 0.19 us
  other arithmetic: 16.6 us -> 5.86 us
    all_to_all x2 -> x1, waiting for transfers between devices: 505 us -> 0.01 us  [body(): lax.all_to_all(partial, ('y', 'c'), split_axis=0, concat_axis=0, tiled=True)]
    gather x28 -> x1, local copies, waits for them, and re-layouts: 67.3 us -> 0.56 us  [body(): partner = other[partner_slot[0]][:, ::-1, ::-1]]
    dot_general x14 -> x0, matrix products: 56.2 us -> none  [the longest x12 38 us: task_block(): jnp.einsum('btk,bkc->btc', left_tiles[lidx], right_tiles[ridx], precision...]
    reduce_scatter x1 -> x0, waiting for transfers between devices: 38.2 us -> none  [body(): lax.psum_scatter(partial_ladder, 'vir', scatter_dimension=1, tiled=True)]
    ppermute x6 -> x10, starting transfers between devices: 30.4 us -> 56 us  [the longest x9 46.2 us: move(): return lax.ppermute(array, (axis, 'c'), signed(size, distance))]
    all_to_all x2 -> x1, starting transfers between devices: 34.1 us -> 9.08 us  [body(): lax.all_to_all(partial, ('y', 'c'), split_axis=0, concat_axis=0, tiled=True)]
    pallas_call x0 -> x3, Pallas kernels: none -> 15.9 us  [the longest x1 5.88 us: body(): pl.pallas_call(gather_kernel, out_shape=[jax.ShapeDtypeStruct((4, OWN * E...]
    ppermute x6 -> x10, waiting for transfers between devices: 40 us -> 53.4 us  [the longest x9 43.5 us: move(): return lax.ppermute(array, (axis, 'c'), signed(size, distance))]
  transfers between devices with their start and end apart: 9 -> 11, of which waited for: 8 -> 6; matrix products, arithmetic and copies ran while one was open for 15% -> 4% of each run, Pallas kernels for 0% -> 7%
where the time goes in v1:
time: 144 us; the launch traced here: 143 us
  starting transfers between devices  65.1 us (45%)
  waiting for transfers between devices  53.5 us (37%)
  Pallas kernels  15.9 us (11%)
  other arithmetic  5.86 us (4%)
  local copies, waits for them, and re-layouts  2.11 us (1%)
    ppermute x9, starting transfers between devices, move(): return lax.ppermute(array, (axis, 'c'), signed(size, distance))  46.2 us
    ppermute x9, waiting for transfers between devices, move(): return lax.ppermute(array, (axis, 'c'), signed(size, distance))  43.5 us
    ppermute x1, waiting for transfers between devices, body(): lax.ppermute(resid, ('x', 'z'), [(i, n_occ - 1 - i) for i in range(n_occ)])  9.92 us
    ppermute x1, starting transfers between devices, body(): lax.ppermute(resid, ('x', 'z'), [(i, n_occ - 1 - i) for i in range(n_occ)])  9.82 us
    all_to_all x1, starting transfers between devices, body(): lax.all_to_all(partial, ('y', 'c'), split_axis=0, concat_axis=0, tiled=True)  9.08 us
    pallas_call x1, Pallas kernels, body(): pl.pallas_call(gather_kernel, out_shape=[jax.ShapeDtypeStruct((4, OWN * E...  5.88 us
    pallas_call x1, Pallas kernels, body(): pl.pallas_call(products_kernel, out_shape=jax.ShapeDtypeStruct((ROWS, EDG...  5.23 us
    pallas_call x1, Pallas kernels, body(): pl.pallas_call(ladder_kernel, out_shape=jax.ShapeDtypeStruct((8, OWN * ED...  4.78 us
  transfers between devices with their start and end apart: 11, of which 6 were waited for; matrix products, arithmetic and copies ran while one was open for 4% of the time, Pallas kernels for 7%

profile of v1, /device:TPU:24, one launch (start us, length us, event | category | flops | bytes accessed | tf_op | source)
XLA Modules:
  0.0 142.6 jit_solution(838285022508464702)
XLA Ops:
  0.0 5.2 %products.1.p0 = f32[2056,128]{1,0:T(8,128)} custom-call(s32[96]{0:T(128)} %bitcast.43, s32[96]{0:T(128)} %bitcast.44, s32[96]{0:T(128)} %bitcast.45, f32[4,128,256]{2,1,0:T(8,128)} %bitcast.41, f32[4,256,128]{2,1,0:T(8,128)} %bitcast.42), custom_call_target="tpu_custom_call" | custom-call | tf_op jit(solution)/shard_map/products/pallas_call | solution.py:141
  5.2 3.4 %collective-permute-start = (f32[2056,128]{1,0:T(8,128)}, f32[2056,128]{1,0:T(8,128)S(1)}, u32[]{:S(2)}, u32[]{:S(2)}) collective-permute-start(f32[2056,128]{1,0:T(8,128)} %products.1.p0), channel_id=1, source_target_pairs={{0,128},{1,385},{128,256},{129,1},{256,384},{257,129},{384,0},{385... | collective-permute-start | bytes 3158024 | tf_op jit(solution)/shard_map/ppermute | solution.py:114
  8.6 3.7 %collective-permute-start.1 = (f32[2056,128]{1,0:T(8,128)}, f32[2056,128]{1,0:T(8,128)S(1)}, u32[]{:S(2)}, u32[]{:S(2)}) collective-permute-start(f32[2056,128]{1,0:T(8,128)} %products.1.p0), channel_id=1, source_target_pairs={{0,384},{1,129},{128,0},{129,257},{256,128},{257,385},{384,256},{3... | collective-permute-start | bytes 3158024 | tf_op jit(solution)/shard_map/ppermute | solution.py:114
  12.3 4.8 %ladder.1 = f32[8,256,128]{2,1,0:T(8,128)} custom-call(s32[2,4]{1,0:T(2,128)} %mask.1, f32[256,512]{1,0:T(8,128)} %lam_ref.1, f32[512,1024]{1,0:T(8,128)} %ints_ref.1), custom_call_target="tpu_custom_call" | custom-call | tf_op jit(solution)/shard_map/ladder/pallas_call | solution.py:152
  17.1 9.1 %all-to-all-start = ((f32[8,256,128]{2,1,0:T(8,128)}), f32[8,256,128]{2,1,0:T(8,128)S(1)}, u32[]{:S(2)}, u32[]{:S(2)}) async-start(f32[8,256,128]{2,1,0:T(8,128)} %ladder.1), calls=%async_computation | async-start | bytes 2097152 | tf_op jit(solution)/shard_map/all_to_all | solution.py:159
  26.1 0.7 slice_bitcast_fusion.3
  26.8 4.5 %collective-permute-done.p1 = f32[2056,128]{1,0:T(8,128)S(1)} collective-permute-done((f32[2056,128]{1,0:T(8,128)}, f32[2056,128]{1,0:T(8,128)S(1)}, u32[]{:S(2)}, u32[]{:S(2)}) %collective-permute-start) | collective-permute-done | bytes 1052704 | tf_op jit(solution)/shard_map/ppermute | solution.py:114
  31.3 0.0 copy-start
  31.3 3.6 %collective-permute-start.2 = (f32[2056,128]{1,0:T(8,128)S(1)}, f32[2056,128]{1,0:T(8,128)}, u32[]{:S(2)}, u32[]{:S(2)}) collective-permute-start(f32[2056,128]{1,0:T(8,128)S(1)} %collective-permute-done.p1), channel_id=1, source_target_pairs={{0,128},{1,385},{128,256},{129,1},{256,384},{257,129},{384,0},{385... | collective-permute-start | bytes 3158024 | tf_op jit(solution)/shard_map/ppermute | solution.py:114
  34.9 0.6 slice_convert_fusion.3.t0
  35.5 0.7 pad_add_fusion.where
  36.1 0.6 slice_convert_fusion.2.t1
  36.7 0.0 collective-permute-done.1.p2
  36.7 0.0 copy-start.1
  36.7 0.6 slice_convert_fusion.1.t2
  37.4 12.3 %collective-permute-done.2.p3 = f32[2056,128]{1,0:T(8,128)} collective-permute-done((f32[2056,128]{1,0:T(8,128)S(1)}, f32[2056,128]{1,0:T(8,128)}, u32[]{:S(2)}, u32[]{:S(2)}) %collective-permute-start.2) | collective-permute-done | bytes 1052704 | tf_op jit(solution)/shard_map/ppermute | solution.py:114
  49.6 0.7 slice_bitcast_fusion
  50.3 0.6 slice_convert_fusion.t3
  50.9 0.0 copy-done
  50.9 0.0 copy-done.1
  50.9 5.9 %gather.7 = (f32[4,256,128]{2,1,0:T(8,128)}, f32[4,256,128]{2,1,0:T(8,128)}, f32[4,256,128]{2,1,0:T(8,128)}, f32[4,256,128]{2,1,0:T(8,128)}) custom-call(s32[3]{0:T(128)} %pad_add_fusion.where, s32[192]{0:T(256)} %slice_convert_fusion.3.t0, s32[192]{0:T(256)} %slice_convert_fusion.2.t1, s32[192]{0:T(256)} %slice_convert_fusion.1.t2, ...), custom_call_target="tpu_custom_call" | custom-call | tf_op jit(solution)/shard_map/gather/pallas_call | solution.py:165
  56.8 3.8 %collective-permute-start.3 = (f32[4,256,128]{2,1,0:T(8,128)}, f32[4,256,128]{2,1,0:T(8,128)S(1)}, u32[]{:S(2)}, u32[]{:S(2)}) collective-permute-start(f32[4,256,128]{2,1,0:T(8,128)} %get-tuple-element.10), channel_id=1, source_target_pairs={{0,8},{1,121},{8,16},{9,1},{16,24},{17,9},{24,32},{25,17},{32,40},... | collective-permute-start | bytes 1572872 | tf_op jit(solution)/shard_map/ppermute | solution.py:114
  60.6 9.5 %collective-permute-start.4 = (f32[4,256,128]{2,1,0:T(8,128)}, f32[4,256,128]{2,1,0:T(8,128)S(1)}, u32[]{:S(2)}, u32[]{:S(2)}) collective-permute-start(f32[4,256,128]{2,1,0:T(8,128)} %get-tuple-element.11), channel_id=1, source_target_pairs={{0,120},{1,9},{8,0},{9,17},{16,8},{17,25},{24,16},{25,33},{32,24},... | collective-permute-start | bytes 1572872 | tf_op jit(solution)/shard_map/ppermute | solution.py:114
  70.1 1.9 %collective-permute-start.5 = (f32[4,256,128]{2,1,0:T(8,128)}, f32[4,256,128]{2,1,0:T(8,128)S(1)}, u32[]{:S(2)}, u32[]{:S(2)}) collective-permute-start(f32[4,256,128]{2,1,0:T(8,128)} %get-tuple-element.12), channel_id=1, source_target_pairs={{0,16},{1,113},{8,24},{9,121},{16,32},{17,1},{24,40},{25,9},{32,48... | collective-permute-start | bytes 1572872 | tf_op jit(solution)/shard_map/ppermute | solution.py:114
  72.1 8.8 %collective-permute-done.3 = f32[4,256,128]{2,1,0:T(8,128)S(1)} collective-permute-done((f32[4,256,128]{2,1,0:T(8,128)}, f32[4,256,128]{2,1,0:T(8,128)S(1)}, u32[]{:S(2)}, u32[]{:S(2)}) %collective-permute-start.3) | collective-permute-done | bytes 524320 | tf_op jit(solution)/shard_map/ppermute | solution.py:114
  80.8 6.9 %collective-permute-done.4 = f32[4,256,128]{2,1,0:T(8,128)S(1)} collective-permute-done((f32[4,256,128]{2,1,0:T(8,128)}, f32[4,256,128]{2,1,0:T(8,128)S(1)}, u32[]{:S(2)}, u32[]{:S(2)}) %collective-permute-start.4) | collective-permute-done | bytes 524320 | tf_op jit(solution)/shard_map/ppermute | solution.py:114
  87.7 0.0 collective-permute-done.5
  87.7 1.1 fusion.2
  88.8 3.5 %collective-permute-start.6 = (f32[256,128]{1,0:T(8,128)S(1)}, f32[256,128]{1,0:T(8,128)S(1)}, u32[]{:S(2)}, u32[]{:S(2)}) collective-permute-start(f32[256,128]{1,0:T(8,128)S(1)} %get-tuple-element.13), channel_id=1, source_target_pairs={{0,32},{1,97},{8,40},{9,105},{16,48},{17,113},{24,56},{25,121},{32... | collective-permute-start | bytes 393224 | tf_op jit(solution)/shard_map/ppermute | solution.py:114
  92.3 6.3 %collective-permute-start.7 = (f32[256,128]{1,0:T(8,128)S(1)}, f32[256,128]{1,0:T(8,128)S(1)}, u32[]{:S(2)}, u32[]{:S(2)}) collective-permute-start(f32[256,128]{1,0:T(8,128)S(1)} %get-tuple-element.15), channel_id=1, source_target_pairs={{0,96},{1,33},{8,104},{9,41},{16,112},{17,49},{24,120},{25,57},{32... | collective-permute-start | bytes 393224 | tf_op jit(solution)/shard_map/ppermute | solution.py:114
  98.6 0.0 copy-start.3
  98.6 10.6 %collective-permute-start.8 = (f32[256,128]{1,0:T(8,128)S(1)}, f32[256,128]{1,0:T(8,128)S(1)}, u32[]{:S(2)}, u32[]{:S(2)}) collective-permute-start(f32[256,128]{1,0:T(8,128)S(1)} %get-tuple-element.14), channel_id=1, source_target_pairs={{0,64},{1,65},{8,72},{9,73},{16,80},{17,81},{24,88},{25,89},{32,96... | collective-permute-start | bytes 393224 | tf_op jit(solution)/shard_map/ppermute | solution.py:114
  109.3 0.0 all-to-all-done
  109.3 0.1 reduce_sum.9
  109.3 0.0 copy-start.2
  109.3 0.0 collective-permute-done.6
  109.4 0.0 collective-permute-done.7
  109.4 11.1 %collective-permute-done.8 = f32[256,128]{1,0:T(8,128)S(1)} collective-permute-done((f32[256,128]{1,0:T(8,128)S(1)}, f32[256,128]{1,0:T(8,128)S(1)}, u32[]{:S(2)}, u32[]{:S(2)}) %collective-permute-start.8) | collective-permute-done | bytes 131104 | tf_op jit(solution)/shard_map/ppermute | solution.py:114
  120.4 1.0 fusion.7
  121.4 9.8 %collective-permute-start.9 = (f32[2,128,128]{2,1,0:T(8,128)S(1)}, f32[2,128,128]{2,1,0:T(8,128)S(1)}, u32[]{:S(2)}, u32[]{:S(2)}) collective-permute-start(f32[2,128,128]{2,1,0:T(8,128)S(1)} %bitcast.39), channel_id=1, source_target_pairs={{0,504},{8,496},{16,488},{24,480},{32,472},{40,464},{48,456},{56,4... | collective-permute-start | bytes 393224 | tf_op jit(solution)/shard_map/ppermute | solution.py:177
  131.2 0.0 copy-done.3
  131.2 9.9 %collective-permute-done.9 = f32[2,128,128]{2,1,0:T(8,128)S(1)} collective-permute-done((f32[2,128,128]{2,1,0:T(8,128)S(1)}, f32[2,128,128]{2,1,0:T(8,128)S(1)}, u32[]{:S(2)}, u32[]{:S(2)}) %collective-permute-start.9) | collective-permute-done | bytes 131104 | tf_op jit(solution)/shard_map/ppermute | solution.py:177
  141.2 0.6 gather_fusion
  141.7 0.2 rev.3
  141.9 0.0 copy-done.2
  141.9 0.7 bitcast_divide_fusion
  (5 shorter events, 0.0 us)
Async XLA Ops:
  5.2 26.1 %collective-permute-start = (f32[2056,128]{1,0:T(8,128)}, f32[2056,128]{1,0:T(8,128)S(1)}, u32[]{:S(2)}, u32[]{:S(2)}) collective-permute-start(f32[2056,128]{1,0:T(8,128)} %products.1.p0), channel_id=1, source_target_pairs={{0,128},{1,385},{128,256},{129,1},{256,384},{257,129},{384,0},{385... | collective-permute-start | bytes 3158024 | tf_op jit(solution)/shard_map/ppermute | solution.py:114
  8.6 28.1 %collective-permute-start.1 = (f32[2056,128]{1,0:T(8,128)}, f32[2056,128]{1,0:T(8,128)S(1)}, u32[]{:S(2)}, u32[]{:S(2)}) collective-permute-start(f32[2056,128]{1,0:T(8,128)} %products.1.p0), channel_id=1, source_target_pairs={{0,384},{1,129},{128,0},{129,257},{256,128},{257,385},{384,256},{3... | collective-permute-start | bytes 3158024 | tf_op jit(solution)/shard_map/ppermute | solution.py:114
  17.1 92.2 %all-to-all-start = ((f32[8,256,128]{2,1,0:T(8,128)}), f32[8,256,128]{2,1,0:T(8,128)S(1)}, u32[]{:S(2)}, u32[]{:S(2)}) async-start(f32[8,256,128]{2,1,0:T(8,128)} %ladder.1), calls=%async_computation | async-start | bytes 2097152 | tf_op jit(solution)/shard_map/all_to_all | solution.py:159
  31.3 19.6 %copy-start = (f32[2056,128]{1,0:T(8,128)}, f32[2056,128]{1,0:T(8,128)S(1)}, u32[]{:S(2)}) copy-start(f32[2056,128]{1,0:T(8,128)S(1)} %collective-permute-done.p1) | copy-start | bytes 3158020
  31.3 18.3 %collective-permute-start.2 = (f32[2056,128]{1,0:T(8,128)S(1)}, f32[2056,128]{1,0:T(8,128)}, u32[]{:S(2)}, u32[]{:S(2)}) collective-permute-start(f32[2056,128]{1,0:T(8,128)S(1)} %collective-permute-done.p1), channel_id=1, source_target_pairs={{0,128},{1,385},{128,256},{129,1},{256,384},{257,129},{384,0},{385... | collective-permute-start | bytes 3158024 | tf_op jit(solution)/shard_map/ppermute | solution.py:114
  36.7 14.2 %copy-start.1 = (f32[2056,128]{1,0:T(8,128)}, f32[2056,128]{1,0:T(8,128)S(1)}, u32[]{:S(2)}) copy-start(f32[2056,128]{1,0:T(8,128)S(1)} %collective-permute-done.1.p2) | copy-start | bytes 3158020
  56.8 24.0 %collective-permute-start.3 = (f32[4,256,128]{2,1,0:T(8,128)}, f32[4,256,128]{2,1,0:T(8,128)S(1)}, u32[]{:S(2)}, u32[]{:S(2)}) collective-permute-start(f32[4,256,128]{2,1,0:T(8,128)} %get-tuple-element.10), channel_id=1, source_target_pairs={{0,8},{1,121},{8,16},{9,1},{16,24},{17,9},{24,32},{25,17},{32,40},... | collective-permute-start | bytes 1572872 | tf_op jit(solution)/shard_map/ppermute | solution.py:114
  60.6 27.1 %collective-permute-start.4 = (f32[4,256,128]{2,1,0:T(8,128)}, f32[4,256,128]{2,1,0:T(8,128)S(1)}, u32[]{:S(2)}, u32[]{:S(2)}) collective-permute-start(f32[4,256,128]{2,1,0:T(8,128)} %get-tuple-element.11), channel_id=1, source_target_pairs={{0,120},{1,9},{8,0},{9,17},{16,8},{17,25},{24,16},{25,33},{32,24},... | collective-permute-start | bytes 1572872 | tf_op jit(solution)/shard_map/ppermute | solution.py:114
  70.1 17.6 %collective-permute-start.5 = (f32[4,256,128]{2,1,0:T(8,128)}, f32[4,256,128]{2,1,0:T(8,128)S(1)}, u32[]{:S(2)}, u32[]{:S(2)}) collective-permute-start(f32[4,256,128]{2,1,0:T(8,128)} %get-tuple-element.12), channel_id=1, source_target_pairs={{0,16},{1,113},{8,24},{9,121},{16,32},{17,1},{24,40},{25,9},{32,48... | collective-permute-start | bytes 1572872 | tf_op jit(solution)/shard_map/ppermute | solution.py:114
  88.8 20.5 %collective-permute-start.6 = (f32[256,128]{1,0:T(8,128)S(1)}, f32[256,128]{1,0:T(8,128)S(1)}, u32[]{:S(2)}, u32[]{:S(2)}) collective-permute-start(f32[256,128]{1,0:T(8,128)S(1)} %get-tuple-element.13), channel_id=1, source_target_pairs={{0,32},{1,97},{8,40},{9,105},{16,48},{17,113},{24,56},{25,121},{32... | collective-permute-start | bytes 393224 | tf_op jit(solution)/shard_map/ppermute | solution.py:114
  92.3 17.0 %collective-permute-start.7 = (f32[256,128]{1,0:T(8,128)S(1)}, f32[256,128]{1,0:T(8,128)S(1)}, u32[]{:S(2)}, u32[]{:S(2)}) collective-permute-start(f32[256,128]{1,0:T(8,128)S(1)} %get-tuple-element.15), channel_id=1, source_target_pairs={{0,96},{1,33},{8,104},{9,41},{16,112},{17,49},{24,120},{25,57},{32... | collective-permute-start | bytes 393224 | tf_op jit(solution)/shard_map/ppermute | solution.py:114
  98.6 32.6 %copy-start.3 = (s32[1,2]{1,0:T(1,128)S(1)}, s32[1,2]{1,0:T(1,128)}, u32[]{:S(2)}) copy-start(s32[1,2]{1,0:T(1,128)} %param.18) | copy-start | bytes 28
  98.6 21.8 %collective-permute-start.8 = (f32[256,128]{1,0:T(8,128)S(1)}, f32[256,128]{1,0:T(8,128)S(1)}, u32[]{:S(2)}, u32[]{:S(2)}) collective-permute-start(f32[256,128]{1,0:T(8,128)S(1)} %get-tuple-element.14), channel_id=1, source_target_pairs={{0,64},{1,65},{8,72},{9,73},{16,80},{17,81},{24,88},{25,89},{32,96... | collective-permute-start | bytes 393224 | tf_op jit(solution)/shard_map/ppermute | solution.py:114
  109.3 32.6 %copy-start.2 = (f32[256,128]{1,0:T(8,128)S(1)}, f32[256,128]{1,0:T(8,128)}, u32[]{:S(2)}) copy-start(f32[256,128]{1,0:T(8,128)} %param.19) | copy-start | bytes 393220
  121.4 19.8 %collective-permute-start.9 = (f32[2,128,128]{2,1,0:T(8,128)S(1)}, f32[2,128,128]{2,1,0:T(8,128)S(1)}, u32[]{:S(2)}, u32[]{:S(2)}) collective-permute-start(f32[2,128,128]{2,1,0:T(8,128)S(1)} %bitcast.39), channel_id=1, source_target_pairs={{0,504},{8,496},{16,488},{24,480},{32,472},{40,464},{48,456},{56,4... | collective-permute-start | bytes 393224 | tf_op jit(solution)/shard_map/ppermute | solution.py:177

commit v2 on v1

--- a/solution.py
+++ b/solution.py
@@ -1,3 +1,5 @@
+import functools
+
 import jax
 import jax.numpy as jnp
 from jax import lax
@@ -17,6 +19,8 @@
 PAIRS = XT * XT
 TABLE = 8
 ROWS = PAIRS * EDGE + TABLE
+HIGH = 4
+LOW = 4
 NEAR = (0, 1, -1, 2)
 HIGHEST = lax.Precision.HIGHEST
 SMEM = pltpu.SMEM
@@ -73,32 +77,57 @@
             out_ref[q, pl.ds(s * EDGE, EDGE), :] = part[:, q * EDGE : (q + 1) * EDGE]
 
 
-def gather_kernel(where, t0, t1, t2, t3, p0, p1, p2, p3, o0, o1, o2, o3):
-    base = where[0] * NZ
-    z = where[1]
-    sign = where[2]
-    tables = (t0, t1, t2, t3)
-    tiles = (p0, p1, p2, p3)
-    for near, out in zip(NEAR, (o0, o1, o2, o3)):
-
-        def dest(a, c, near=near, out=out):
-            target = lax.rem(z + sign * (near + 4 * a) + 4 * NZ, NZ)
-            start = (base + target) * CAP
-            acc = [jnp.zeros((EDGE, EDGE), jnp.float32) for _ in range(OWN)]
-            for table, tile in zip(tables, tiles):
-                for k in range(CAP):
-                    entry = table[start + k]
-                    slot = lax.shift_right_arithmetic(entry, 4)
-                    code = jnp.bitwise_and(jnp.maximum(entry, 0), PAIRS - 1)
-                    at = pl.multiple_of(code * EDGE, EDGE)
-                    val = tile[pl.ds(at, EDGE), :]
-                    for s in range(OWN):
-                        acc[s] = acc[s] + val * (slot == s).astype(jnp.float32)
+def flipped(value):
+    last = value.shape[0] // 8 - 1
+    lane = EDGE - 1 - lax.broadcasted_iota(jnp.int32, (8, EDGE), 1)
+    row = 7 - lax.broadcasted_iota(jnp.int32, (8, EDGE), 0)
+    parts = []
+    for i in range(last + 1):
+        part = value[(last - i) * 8 : (last - i + 1) * 8]
+        part = jnp.take_along_axis(part, lane, axis=1, mode="promise_in_bounds")
+        part = jnp.take_along_axis(part, row, axis=0, mode="promise_in_bounds")
+        parts.append(part)
+    return jnp.concatenate(parts, axis=0)
+
+
+def gather_kernel(sources, more, place, slots, *refs):
+    tables = refs[:sources]
+    tiles = refs[sources : 2 * sources]
+    refs = refs[2 * sources :]
+    befores = refs[:4] if more else (None,) * 4
+    outs = refs[-4:]
+    base = place[0] * NZ
+    z = place[1]
+    sign = place[2]
+    for near, before, out in zip(NEAR, befores, outs):
+        low = jnp.bitwise_and(z + sign * near + NZ, LOW - 1)
+
+        def dest(a, carry, low=low, before=before, out=out):
+            target = a * LOW + low
+            owner = base + target
+            sums = []
+            for flip in range(2):
+                start = (NX * NZ - 1 - owner if flip else owner) * CAP
+                acc = [jnp.zeros((EDGE, EDGE), jnp.float32) for _ in range(OWN)]
+                for table, tile in zip(tables, tiles):
+                    for k in range(CAP):
+                        entry = table[start + k]
+                        slot = lax.shift_right_arithmetic(entry, 4)
+                        code = jnp.bitwise_and(jnp.maximum(entry, 0), PAIRS - 1)
+                        val = tile[pl.ds(pl.multiple_of(code * EDGE, EDGE), EDGE), :]
+                        for s in range(OWN):
+                            want = slots[target * OWN + s] if flip else s
+                            acc[s] = acc[s] + val * (slot == want).astype(jnp.float32)
+                sums.append(acc)
             for s in range(OWN):
-                out[a, pl.ds(s * EDGE, EDGE), :] = acc[s]
-            return c
-
-        lax.fori_loop(0, 4, dest, 0)
+                rows = pl.ds(s * EDGE, EDGE)
+                total = sums[0][s] + flipped(sums[1][s])
+                if before is not None:
+                    total = total + before[a, rows, :]
+                out[a, rows, :] = total
+            return carry
+
+        lax.fori_loop(0, HIGH, dest, 0)
 
 
 def signed(axis_size, distance):
@@ -110,8 +139,23 @@
     return pairs
 
 
-def move(array, axis, size, distance):
-    return lax.ppermute(array, (axis, "c"), signed(size, distance))
+def move_x(array, distance):
+    return lax.ppermute(array, ("x", "c"), signed(NX, distance))
+
+
+def move_z(array, distance):
+    return lax.ppermute(array, ("h", "l", "c"), signed(NZ, distance))
+
+
+def gather(place, slots, tables, arrays, before=()):
+    n = len(arrays)
+    return pl.pallas_call(
+        functools.partial(gather_kernel, n, len(before) > 0),
+        out_shape=[jax.ShapeDtypeStruct((HIGH, OWN * EDGE, EDGE), jnp.float32)] * 4,
+        in_specs=sm(2 + n) + vm(n + len(before)),
+        out_specs=vm(4),
+        name="gather_more" if before else "gather",
+    )(place, slots, *tables, *arrays, *before)
 
 
 def vm(n):
@@ -136,8 +180,9 @@
 ):
     f32 = jnp.float32
     x = lax.axis_index("x")
-    z = lax.axis_index("z")
+    z = lax.axis_index(("h", "l"))
     c = lax.axis_index("c")
+    place = jnp.stack([x, z, 1 - 2 * c]).astype(jnp.int32)
     payload = pl.pallas_call(
         products_kernel,
         out_shape=jax.ShapeDtypeStruct((ROWS, EDGE), f32),
@@ -146,9 +191,9 @@
         scratch_shapes=[pltpu.SMEM((NX * NZ,), jnp.int32)],
         name="products",
     )(cycle_left[0, 0], cycle_right[0, 0], cycle_dest[0, 0], t2_tiles[0, 0], cycle_ints[0, 0])
-    got_a = move(payload, "x", NX, 1)
-    got_b = move(payload, "x", NX, -1)
-    got_c = move(got_a, "x", NX, 1)
+    got_a = move_x(payload, 1)
+    got_b = move_x(payload, -1)
+    got_c = move_x(got_a, 1)
     partial = pl.pallas_call(
         ladder_kernel,
         out_shape=jax.ShapeDtypeStruct((8, OWN * EDGE, EDGE), f32),
@@ -158,30 +203,28 @@
     )(ladder_mask, lam_ladder, ladder_ints)
     spread = lax.all_to_all(partial, ("y", "c"), split_axis=0, concat_axis=0, tiled=True)
     ladder = jnp.sum(spread, axis=0)
+    n_occ = NX * NZ
+    mirror = [(i, n_occ - 1 - i) for i in range(n_occ)]
+    other = lax.ppermute(ladder, ("x", "h", "l"), mirror).reshape(OWN, EDGE, EDGE)
+    other = other[partner_slot[0]][:, ::-1, ::-1].reshape(OWN * EDGE, EDGE)
+    ladder = ladder + other
+    own_slots = jnp.broadcast_to(partner_slot, (NZ, OWN))
+    slots = lax.all_to_all(own_slots, ("h", "l"), split_axis=0, concat_axis=0, tiled=True)
+    slots = slots.reshape(-1)
 
     arrays = (payload, got_a, got_b, got_c)
     tables = [a[PAIRS * EDGE :].reshape(-1)[:ENTRIES].astype(jnp.int32) for a in arrays]
-    place = jnp.stack([x, z, 1 - 2 * c]).astype(jnp.int32)
-    near = pl.pallas_call(
-        gather_kernel,
-        out_shape=[jax.ShapeDtypeStruct((4, OWN * EDGE, EDGE), f32)] * 4,
-        in_specs=sm(5) + vm(4),
-        out_specs=vm(4),
-        name="gather",
-    )(place, *tables, *arrays)
-    moved = [move(near[j], "z", NZ, NEAR[j]) for j in (1, 2, 3)]
-    far = [near[0][a] + moved[0][a] + moved[1][a] + moved[2][a] for a in range(4)]
-    far = [far[0]] + [move(far[a], "z", NZ, 4 * a) for a in (1, 3, 2)]
-    resid = (ladder + far[0] + far[1] + far[2] + far[3]).reshape(OWN, EDGE, EDGE)
-    n_occ = NX * NZ
-    other = lax.ppermute(resid, ("x", "z"), [(i, n_occ - 1 - i) for i in range(n_occ)])
-    partner = other[partner_slot[0]][:, ::-1, ::-1]
-    return (resid + partner).reshape(OWN * EDGE, EDGE) / denom
+    near = gather(place, slots, tables[:3], arrays[:3])
+    near = gather(place, slots, tables[3:], arrays[3:], near)
+    moved = [move_z(near[j], NEAR[j]) for j in (3, 1, 2)]
+    far = near[0] + moved[0] + moved[1] + moved[2]
+    far = lax.all_to_all(far, "h", split_axis=0, concat_axis=0, tiled=True)
+    return (ladder + far[0] + far[1] + far[2] + far[3]) / denom
 
 
 def solution(mesh):
-    grid = Mesh(mesh.devices.reshape(NX, NZ, 4, 2), ("x", "z", "y", "c"))
-    occ = ("x", "z")
+    grid = Mesh(mesh.devices.reshape(NX, HIGH, LOW, 4, 2), ("x", "h", "l", "y", "c"))
+    occ = ("x", "h", "l")
     vir = ("y", "c")
     in_specs = (
         P(occ, vir, None, None, None),

time: 144 us -> 150 us (1.042)
  Pallas kernels: 15.9 us -> 21.3 us
  starting transfers between devices: 65.1 us -> 61.6 us
  local copies, waits for them, and re-layouts: 2.11 us -> 4.27 us
    ppermute x10 -> x7, starting transfers between devices: 56 us -> 28.5 us  [the longest x3 11.3 us: move_z(): return lax.ppermute(array, ('h', 'l', 'c'), signed(NZ, distance))]
    all_to_all x0 -> x2, starting transfers between devices: none -> 24.5 us  [the longest x1 15.2 us: body(): lax.all_to_all(own_slots, ('h', 'l'), split_axis=0, concat_axis=0, tiled=...]
    pallas_call x1 -> x2, Pallas kernels: 5.88 us -> 11.3 us  [gather(): pl.pallas_call(functools.partial(gather_kernel, n, len(before) > 0), out_...]
    ppermute x10 -> x7, waiting for transfers between devices: 53.4 us -> 54.9 us  [the longest x1 32 us: body(): lax.ppermute(ladder, ('x', 'h', 'l'), mirror).reshape(OWN, EDGE, EDGE)]
  transfers between devices with their start and end apart: 11 -> 10, of which waited for: 6 -> 4; matrix products, arithmetic and copies ran while one was open for 4% -> 6% of each run, Pallas kernels for 7% -> 11%
where the time goes in v2:
time: 150 us; the launch traced here: 148 us
  starting transfers between devices  61.6 us (41%)
  waiting for transfers between devices  54.9 us (37%)
  Pallas kernels  21.3 us (14%)
  other arithmetic  6.28 us (4%)
  local copies, waits for them, and re-layouts  4.27 us (3%)
    ppermute x1, waiting for transfers between devices, body(): lax.ppermute(ladder, ('x', 'h', 'l'), mirror).reshape(OWN, EDGE, EDGE)  32 us
    ppermute x3, waiting for transfers between devices, move_z(): return lax.ppermute(array, ('h', 'l', 'c'), signed(NZ, distance))  20.4 us
    all_to_all x1, starting transfers between devices, body(): lax.all_to_all(own_slots, ('h', 'l'), split_axis=0, concat_axis=0, tiled=...  15.2 us
    ppermute x3, starting transfers between devices, move_z(): return lax.ppermute(array, ('h', 'l', 'c'), signed(NZ, distance))  11.3 us
    pallas_call x2, Pallas kernels, gather(): pl.pallas_call(functools.partial(gather_kernel, n, len(before) > 0), out_...  11.3 us
    ppermute x3, starting transfers between devices, move_x(): return lax.ppermute(array, ('x', 'c'), signed(NX, distance))  10.6 us
    all_to_all x1, starting transfers between devices, body(): far = lax.all_to_all(far, 'h', split_axis=0, concat_axis=0, tiled=True)  9.27 us
    all_to_all x1, starting transfers between devices, body(): lax.all_to_all(partial, ('y', 'c'), split_axis=0, concat_axis=0, tiled=True)  8.62 us
  transfers between devices with their start and end apart: 10, of which 4 were waited for; matrix products, arithmetic and copies ran while one was open for 6% of the time, Pallas kernels for 11%

profile of v2, /device:TPU:24, one launch (start us, length us, event | category | flops | bytes accessed | tf_op | source)
XLA Modules:
  0.0 148.5 jit_solution(12750883900599209705)
XLA Ops:
  0.0 0.0 copy-start.3
  0.0 5.3 %products.1.refs_3_ = f32[2056,128]{1,0:T(8,128)} custom-call(s32[96]{0:T(128)} %bitcast.53, s32[96]{0:T(128)} %bitcast.54, s32[96]{0:T(128)} %bitcast.55, f32[4,128,256]{2,1,0:T(8,128)} %bitcast.50, f32[4,256,128]{2,1,0:T(8,128)} %bitcast.51), custom_call_target="tpu_custom_call" | custom-call | tf_op jit(solution)/shard_map/products/pallas_call | solution.py:186
  5.3 3.4 %collective-permute-start.1 = (f32[2056,128]{1,0:T(8,128)}, f32[2056,128]{1,0:T(8,128)S(1)}, u32[]{:S(2)}, u32[]{:S(2)}) collective-permute-start(f32[2056,128]{1,0:T(8,128)} %products.1.refs_3_), channel_id=1, source_target_pairs={{0,128},{1,385},{128,256},{129,1},{256,384},{257,129},{384,0},{385... | collective-permute-start | bytes 3158024 | tf_op jit(solution)/shard_map/ppermute | solution.py:143
  8.7 3.7 %collective-permute-start.3 = (f32[2056,128]{1,0:T(8,128)}, f32[2056,128]{1,0:T(8,128)S(1)}, u32[]{:S(2)}, u32[]{:S(2)}) collective-permute-start(f32[2056,128]{1,0:T(8,128)} %products.1.refs_3_), channel_id=1, source_target_pairs={{0,384},{1,129},{128,0},{129,257},{256,128},{257,385},{384,256},{3... | collective-permute-start | bytes 3158024 | tf_op jit(solution)/shard_map/ppermute | solution.py:143
  12.3 0.0 copy-done.3
  12.3 0.6 broadcast_in_dim.2
  12.9 15.2 %all-to-all-start.1 = ((s32[16,1,2]{2,1,0:T(1,128)}), s32[16,1,2]{2,1,0:T(1,128)S(1)}, u32[]{:S(2)}, u32[]{:S(2)}) async-start(s32[16,1,2]{2,1,0:T(1,128)} %broadcast_in_dim.2), calls=%async_computation.1 | async-start | bytes 16384 | tf_op jit(solution)/shard_map/all_to_all | solution.py:212
  28.1 0.7 slice_bitcast_fusion.6
  28.8 2.6 %collective-permute-done.1.refs_4_ = f32[2056,128]{1,0:T(8,128)S(1)} collective-permute-done((f32[2056,128]{1,0:T(8,128)}, f32[2056,128]{1,0:T(8,128)S(1)}, u32[]{:S(2)}, u32[]{:S(2)}) %collective-permute-start.1) | collective-permute-done | bytes 1052704 | tf_op jit(solution)/shard_map/ppermute | solution.py:143
  31.4 0.0 copy-start
  31.4 3.6 %collective-permute-start.2 = (f32[2056,128]{1,0:T(8,128)S(1)}, f32[2056,128]{1,0:T(8,128)}, u32[]{:S(2)}, u32[]{:S(2)}) collective-permute-start(f32[2056,128]{1,0:T(8,128)S(1)} %collective-permute-done.1.refs_4_), channel_id=1, source_target_pairs={{0,128},{1,385},{128,256},{129,1},{256,384},{257,129},{384,0},{385... | collective-permute-start | bytes 3158024 | tf_op jit(solution)/shard_map/ppermute | solution.py:143
  34.9 0.5 slice_convert_fusion.2.refs_0_
  35.5 0.6 pad_add_fusion.place
  36.1 4.8 %ladder.1 = f32[8,256,128]{2,1,0:T(8,128)} custom-call(s32[2,4]{1,0:T(2,128)} %mask.1, f32[256,512]{1,0:T(8,128)} %lam_ref.1, f32[512,1024]{1,0:T(8,128)} %ints_ref.1), custom_call_target="tpu_custom_call" | custom-call | tf_op jit(solution)/shard_map/ladder/pallas_call | solution.py:197
  40.9 0.0 all-to-all-done.1
  40.9 8.6 %all-to-all-start = ((f32[8,256,128]{2,1,0:T(8,128)}), f32[8,256,128]{2,1,0:T(8,128)S(1)}, u32[]{:S(2)}, u32[]{:S(2)}) async-start(f32[8,256,128]{2,1,0:T(8,128)} %ladder.1), calls=%async_computation | async-start | bytes 2097152 | tf_op jit(solution)/shard_map/all_to_all | solution.py:204
  49.5 0.5 broadcast.35
  50.0 0.7 reduce.3
  50.7 0.6 reshape.58.slots
  51.4 0.0 copy-done
  51.4 0.6 slice_convert_fusion.1.refs_1_
  51.9 0.0 collective-permute-done.3.refs_5_
  51.9 0.0 copy-start.1
  51.9 0.6 slice_convert_fusion.refs_2_
  52.5 0.4 copy-done.1
  52.9 6.3 %gather.7 = (f32[4,256,128]{2,1,0:T(8,128)}, f32[4,256,128]{2,1,0:T(8,128)}, f32[4,256,128]{2,1,0:T(8,128)}, f32[4,256,128]{2,1,0:T(8,128)}) custom-call(s32[3]{0:T(128)} %pad_add_fusion.place, s32[32]{0:T(128)} %reshape.58.slots, s32[192]{0:T(256)} %slice_convert_fusion.2.refs_0_, s32[192]{0:T(256)} %slice_convert_fusion.1.refs_1_, ...), custom_call_target="tpu_custom_call" | custom-call | tf_op jit(solution)/shard_map/gather/pallas_call | solution.py:152
  59.3 0.0 collective-permute-done.2.refs_1_
  59.3 0.7 slice_bitcast_fusion.7
  59.9 0.6 slice_convert_fusion.3.refs_0_
  60.5 5.0 %gather_more.1 = (f32[4,256,128]{2,1,0:T(8,128)}, f32[4,256,128]{2,1,0:T(8,128)}, f32[4,256,128]{2,1,0:T(8,128)}, f32[4,256,128]{2,1,0:T(8,128)}) custom-call(s32[3]{0:T(128)} %pad_add_fusion.place, s32[32]{0:T(128)} %reshape.58.slots, s32[192]{0:T(256)} %slice_convert_fusion.3.refs_0_, f32[2056,128]{1,0:T(8,128)} %collective-permute-done.2.refs_1_, ...), custom_call_target="tpu_custom_call" | custom-call | tf_op jit(solution)/shard_map/gather_more/pallas_call | solution.py:152
  65.5 1.9 %collective-permute-start.4 = (f32[4,256,128]{2,1,0:T(8,128)}, f32[4,256,128]{2,1,0:T(8,128)S(1)}, u32[]{:S(2)}, u32[]{:S(2)}) collective-permute-start(f32[4,256,128]{2,1,0:T(8,128)} %get-tuple-element.18), channel_id=1, source_target_pairs={{0,16},{1,113},{8,24},{9,121},{16,32},{17,1},{24,40},{25,9},{32,48... | collective-permute-start | bytes 1572872 | tf_op jit(solution)/shard_map/ppermute | solution.py:147
  67.4 3.2 %collective-permute-start.5 = (f32[4,256,128]{2,1,0:T(8,128)}, f32[4,256,128]{2,1,0:T(8,128)S(1)}, u32[]{:S(2)}, u32[]{:S(2)}) collective-permute-start(f32[4,256,128]{2,1,0:T(8,128)} %get-tuple-element.19), channel_id=1, source_target_pairs={{0,8},{1,121},{8,16},{9,1},{16,24},{17,9},{24,32},{25,17},{32,40},... | collective-permute-start | bytes 1572872 | tf_op jit(solution)/shard_map/ppermute | solution.py:147
  70.6 6.2 %collective-permute-start.6 = (f32[4,256,128]{2,1,0:T(8,128)}, f32[4,256,128]{2,1,0:T(8,128)S(1)}, u32[]{:S(2)}, u32[]{:S(2)}) collective-permute-start(f32[4,256,128]{2,1,0:T(8,128)} %get-tuple-element.20), channel_id=1, source_target_pairs={{0,120},{1,9},{8,0},{9,17},{16,8},{17,25},{24,16},{25,33},{32,24},... | collective-permute-start | bytes 1572872 | tf_op jit(solution)/shard_map/ppermute | solution.py:147
  76.8 6.8 %collective-permute-done.4 = f32[4,256,128]{2,1,0:T(8,128)S(1)} collective-permute-done((f32[4,256,128]{2,1,0:T(8,128)}, f32[4,256,128]{2,1,0:T(8,128)S(1)}, u32[]{:S(2)}, u32[]{:S(2)}) %collective-permute-start.4) | collective-permute-done | bytes 524320 | tf_op jit(solution)/shard_map/ppermute | solution.py:147
  83.6 13.5 %collective-permute-done.5 = f32[4,256,128]{2,1,0:T(8,128)S(1)} collective-permute-done((f32[4,256,128]{2,1,0:T(8,128)}, f32[4,256,128]{2,1,0:T(8,128)S(1)}, u32[]{:S(2)}, u32[]{:S(2)}) %collective-permute-start.5) | collective-permute-done | bytes 524320 | tf_op jit(solution)/shard_map/ppermute | solution.py:147
  97.2 0.0 collective-permute-done.6
  97.2 1.9 %add_add_fusion = f32[4,256,128]{2,1,0:T(8,128)} fusion(f32[4,256,128]{2,1,0:T(8,128)S(1)} %collective-permute-done.6, f32[4,256,128]{2,1,0:T(8,128)S(1)} %collective-permute-done.5, f32[4,256,128]{2,1,0:T(8,128)} %get-tuple-element.17, f32[4,256,128]{2,1,0:T(8,128)S(1)} %collective-permute-done.4), kind=kLoop, calls=%fused_computation.1 | loop fusion | flops 393216 | bytes 2621440 | tf_op jit(solution)/shard_map/add | solution.py:220
  99.1 0.0 all-to-all-done
  99.1 9.3 %all-to-all-start.2 = ((f32[4,256,128]{2,1,0:T(8,128)}), f32[4,256,128]{2,1,0:T(8,128)S(1)}, u32[]{:S(2)}, u32[]{:S(2)}) async-start(f32[4,256,128]{2,1,0:T(8,128)} %add_add_fusion), calls=%async_computation.2 | async-start | bytes 1048576 | tf_op jit(solution)/shard_map/all_to_all | solution.py:221
  108.4 0.0 copy-start.2
  108.4 0.1 reduce_sum.9
  108.4 6.6 %collective-permute-start = (f32[256,128]{1,0:T(8,128)S(1)}, f32[256,128]{1,0:T(8,128)S(1)}, u32[]{:S(2)}, u32[]{:S(2)}) collective-permute-start(f32[256,128]{1,0:T(8,128)S(1)} %reduce_sum.9), channel_id=1, source_target_pairs={{0,504},{8,496},{16,488},{24,480},{32,472},{40,464},{48,456},{56,4... | collective-permute-start | bytes 393224 | tf_op jit(solution)/shard_map/ppermute | solution.py:208
  115.0 32.0 %collective-permute-done = f32[256,128]{1,0:T(8,128)S(1)} collective-permute-done((f32[256,128]{1,0:T(8,128)S(1)}, f32[256,128]{1,0:T(8,128)S(1)}, u32[]{:S(2)}, u32[]{:S(2)}) %collective-permute-start) | collective-permute-done | bytes 131104 | tf_op jit(solution)/shard_map/ppermute | solution.py:208
  147.0 0.6 gather_fusion
  147.6 0.2 rev.3
  147.7 0.0 all-to-all-done.2
  147.8 0.0 copy-done.2
  147.8 0.7 fusion.1
  (4 shorter events, 0.0 us)
Async XLA Ops:
  0.0 12.3 %copy-start.3 = (s32[1,2]{1,0:T(1,128)S(1)}, s32[1,2]{1,0:T(1,128)}, u32[]{:S(2)}) copy-start(s32[1,2]{1,0:T(1,128)} %param.18) | copy-start | bytes 28
  5.3 26.1 %collective-permute-start.1 = (f32[2056,128]{1,0:T(8,128)}, f32[2056,128]{1,0:T(8,128)S(1)}, u32[]{:S(2)}, u32[]{:S(2)}) collective-permute-start(f32[2056,128]{1,0:T(8,128)} %products.1.refs_3_), channel_id=1, source_target_pairs={{0,128},{1,385},{128,256},{129,1},{256,384},{257,129},{384,0},{385... | collective-permute-start | bytes 3158024 | tf_op jit(solution)/shard_map/ppermute | solution.py:143
  8.7 43.3 %collective-permute-start.3 = (f32[2056,128]{1,0:T(8,128)}, f32[2056,128]{1,0:T(8,128)S(1)}, u32[]{:S(2)}, u32[]{:S(2)}) collective-permute-start(f32[2056,128]{1,0:T(8,128)} %products.1.refs_3_), channel_id=1, source_target_pairs={{0,384},{1,129},{128,0},{129,257},{256,128},{257,385},{384,256},{3... | collective-permute-start | bytes 3158024 | tf_op jit(solution)/shard_map/ppermute | solution.py:143
  12.9 28.0 %all-to-all-start.1 = ((s32[16,1,2]{2,1,0:T(1,128)}), s32[16,1,2]{2,1,0:T(1,128)S(1)}, u32[]{:S(2)}, u32[]{:S(2)}) async-start(s32[16,1,2]{2,1,0:T(1,128)} %broadcast_in_dim.2), calls=%async_computation.1 | async-start | bytes 16384 | tf_op jit(solution)/shard_map/all_to_all | solution.py:212
  31.4 20.0 %copy-start = (f32[2056,128]{1,0:T(8,128)}, f32[2056,128]{1,0:T(8,128)S(1)}, u32[]{:S(2)}) copy-start(f32[2056,128]{1,0:T(8,128)S(1)} %collective-permute-done.1.refs_4_) | copy-start | bytes 3158020
  31.4 27.9 %collective-permute-start.2 = (f32[2056,128]{1,0:T(8,128)S(1)}, f32[2056,128]{1,0:T(8,128)}, u32[]{:S(2)}, u32[]{:S(2)}) collective-permute-start(f32[2056,128]{1,0:T(8,128)S(1)} %collective-permute-done.1.refs_4_), channel_id=1, source_target_pairs={{0,128},{1,385},{128,256},{129,1},{256,384},{257,129},{384,0},{385... | collective-permute-start | bytes 3158024 | tf_op jit(solution)/shard_map/ppermute | solution.py:143
  40.9 58.2 %all-to-all-start = ((f32[8,256,128]{2,1,0:T(8,128)}), f32[8,256,128]{2,1,0:T(8,128)S(1)}, u32[]{:S(2)}, u32[]{:S(2)}) async-start(f32[8,256,128]{2,1,0:T(8,128)} %ladder.1), calls=%async_computation | async-start | bytes 2097152 | tf_op jit(solution)/shard_map/all_to_all | solution.py:204
  51.9 1.0 copy-start.1
  65.5 18.1 %collective-permute-start.4 = (f32[4,256,128]{2,1,0:T(8,128)}, f32[4,256,128]{2,1,0:T(8,128)S(1)}, u32[]{:S(2)}, u32[]{:S(2)}) collective-permute-start(f32[4,256,128]{2,1,0:T(8,128)} %get-tuple-element.18), channel_id=1, source_target_pairs={{0,16},{1,113},{8,24},{9,121},{16,32},{17,1},{24,40},{25,9},{32,48... | collective-permute-start | bytes 1572872 | tf_op jit(solution)/shard_map/ppermute | solution.py:147
  67.4 29.8 %collective-permute-start.5 = (f32[4,256,128]{2,1,0:T(8,128)}, f32[4,256,128]{2,1,0:T(8,128)S(1)}, u32[]{:S(2)}, u32[]{:S(2)}) collective-permute-start(f32[4,256,128]{2,1,0:T(8,128)} %get-tuple-element.19), channel_id=1, source_target_pairs={{0,8},{1,121},{8,16},{9,1},{16,24},{17,9},{24,32},{25,17},{32,40},... | collective-permute-start | bytes 1572872 | tf_op jit(solution)/shard_map/ppermute | solution.py:147
  70.6 26.6 %collective-permute-start.6 = (f32[4,256,128]{2,1,0:T(8,128)}, f32[4,256,128]{2,1,0:T(8,128)S(1)}, u32[]{:S(2)}, u32[]{:S(2)}) collective-permute-start(f32[4,256,128]{2,1,0:T(8,128)} %get-tuple-element.20), channel_id=1, source_target_pairs={{0,120},{1,9},{8,0},{9,17},{16,8},{17,25},{24,16},{25,33},{32,24},... | collective-permute-start | bytes 1572872 | tf_op jit(solution)/shard_map/ppermute | solution.py:147
  99.1 48.6 %all-to-all-start.2 = ((f32[4,256,128]{2,1,0:T(8,128)}), f32[4,256,128]{2,1,0:T(8,128)S(1)}, u32[]{:S(2)}, u32[]{:S(2)}) async-start(f32[4,256,128]{2,1,0:T(8,128)} %add_add_fusion), calls=%async_computation.2 | async-start | bytes 1048576 | tf_op jit(solution)/shard_map/all_to_all | solution.py:221
  108.4 39.4 %copy-start.2 = (f32[256,128]{1,0:T(8,128)S(1)}, f32[256,128]{1,0:T(8,128)}, u32[]{:S(2)}) copy-start(f32[256,128]{1,0:T(8,128)} %param.19) | copy-start | bytes 393220
  108.4 38.6 %collective-permute-start = (f32[256,128]{1,0:T(8,128)S(1)}, f32[256,128]{1,0:T(8,128)S(1)}, u32[]{:S(2)}, u32[]{:S(2)}) collective-permute-start(f32[256,128]{1,0:T(8,128)S(1)} %reduce_sum.9), channel_id=1, source_target_pairs={{0,504},{8,496},{16,488},{24,480},{32,472},{40,464},{48,456},{56,4... | collective-permute-start | bytes 393224 | tf_op jit(solution)/shard_map/ppermute | solution.py:208

commit v3 on v2

v3 whole, which is shorter than its diff:
```python
import functools

import jax
import jax.numpy as jnp
from jax import lax
from jax.experimental import pallas as pl
from jax.experimental.pallas import tpu as pltpu
from jax.sharding import Mesh
from jax.sharding import PartitionSpec as P

CAP = 3
EDGE = 128
OWN = 2
XT = 4
NX = 4
NZ = 16
TASKS = 96
ENTRIES = NX * NZ * CAP
PAIRS = XT * XT
TABLE = 8
ROWS = PAIRS * EDGE + TABLE
HIGH = 4
LOW = 4
NEAR = (2, 1, -1, 0)
HIGHEST = lax.Precision.HIGHEST
SMEM = pltpu.SMEM
VMEM = pltpu.VMEM


def halves(value):
    high = value.astype(jnp.bfloat16)
    return high, (value - high.astype(jnp.float32)).astype(jnp.bfloat16)


def dot3(left, right):
    left_high, left_low = halves(left)
    right_high, right_low = halves(right)
    dot = functools.partial(jnp.dot, preferred_element_type=jnp.float32)
    return dot(left_high, right_high) + (dot(left_high, right_low) + dot(left_low, right_high))


def products_kernel(lefts, rights, dests, t2_ref, ints_ref, out_ref, count):
    for i in range(NX * NZ):
        count[i] = 0
    where = (
        lax.broadcasted_iota(jnp.int32, (TABLE, EDGE), 0) * EDGE
        + lax.broadcasted_iota(jnp.int32, (TABLE, EDGE), 1)
    )
    table = jnp.full((TABLE, EDGE), -1, jnp.int32)
    for t in range(TASKS):
        dest = dests[t]
        owner = lax.shift_right_logical(dest, 1)
        rank = count[owner]
        count[owner] = rank + 1
        entry = jnp.bitwise_and(dest, OWN - 1) * PAIRS + lefts[t] * XT + rights[t]
        table = jnp.where(where == owner * CAP + rank, entry, table)
    out_ref[PAIRS * EDGE :, :] = table.astype(jnp.float32)
    right = jnp.concatenate([ints_ref[r] for r in range(XT)], axis=1)
    for l in range(XT):
        tile = dot3(t2_ref[l], right)
        for r in range(XT):
            out_ref[pl.ds((l * XT + r) * EDGE, EDGE), :] = tile[:, r * EDGE : (r + 1) * EDGE]


def ladder_kernel(mask, lam_ref, ints_ref, out_ref):
    blocks = lam_ref.shape[1] // EDGE
    for s in range(OWN):
        rows = [
            lam_ref[pl.ds(s * EDGE, EDGE), pl.ds(b * EDGE, EDGE)]
            * mask[s, b].astype(jnp.float32)
            for b in range(blocks)
        ]
        part = dot3(jnp.concatenate(rows, axis=1), ints_ref[...])
        for q in range(out_ref.shape[0]):
            out_ref[q, pl.ds(s * EDGE, EDGE), :] = part[:, q * EDGE : (q + 1) * EDGE]


def flipped(value):
    last = value.shape[0] // 8 - 1
    lane = EDGE - 1 - lax.broadcasted_iota(jnp.int32, (8, EDGE), 1)
    row = 7 - lax.broadcasted_iota(jnp.int32, (8, EDGE), 0)
    parts = []
    for i in range(last + 1):
        part = value[(last - i) * 8 : (last - i + 1) * 8]
        part = jnp.take_along_axis(part, lane, axis=1, mode="promise_in_bounds")
        part = jnp.take_along_axis(part, row, axis=0, mode="promise_in_bounds")
        parts.append(part)
    return jnp.concatenate(parts, axis=0)


def gather_kernel(sources, nears, more, slots, *refs):
    tiles = refs[:sources]
    refs = refs[sources:]
    befores = refs[: len(nears)] if more else (None,) * len(nears)
    refs = refs[len(nears) :] if more else refs
    outs = refs[: len(nears)]
    tables, sems = refs[len(nears) :]
    copies = [
        pltpu.make_async_copy(tile.at[pl.ds(PAIRS * EDGE, TABLE)], tables.at[i], sems.at[i])
        for i, tile in enumerate(tiles)
    ]
    for copy in copies:
        copy.start()
    base = lax.axis_index("x") * NZ
    z = lax.axis_index("h") * LOW + lax.axis_index("l")
    sign = 1 - 2 * lax.axis_index("c")
    for copy in copies:
        copy.wait()
    for near, before, out in zip(nears, befores, outs):
        low = jnp.bitwise_and(z + sign * near + NZ, LOW - 1)

        def dest(a, carry, low=low, before=before, out=out):
            target = a * LOW + low
            owner = base + target
            sums = []
            for flip in range(2):
                start = (NX * NZ - 1 - owner if flip else owner) * CAP
                acc = [jnp.zeros((EDGE, EDGE), jnp.float32) for _ in range(OWN)]
                for i, tile in enumerate(tiles):
                    for k in range(CAP):
                        at = start + k
                        row = lax.shift_right_logical(at, 7)
                        lane = jnp.bitwise_and(at, EDGE - 1)
                        entry = tables[i, row, lane].astype(jnp.int32)
                        slot = lax.shift_right_arithmetic(entry, 4)
                        code = jnp.bitwise_and(jnp.maximum(entry, 0), PAIRS - 1)
                        val = tile[pl.ds(pl.multiple_of(code * EDGE, EDGE), EDGE), :]
                        for s in range(OWN):
                            want = slots[target, s] if flip else s
                            acc[s] = acc[s] + val * (slot == want).astype(jnp.float32)
                sums.append(acc)
            for s in range(OWN):
                rows = pl.ds(s * EDGE, EDGE)
                total = sums[0][s] + flipped(sums[1][s])
                if before is not None:
                    total = total + before[a, rows, :]
                out[a, rows, :] = total
            return carry

        lax.fori_loop(0, HIGH, dest, 0)


def signed(axis_size, distance):
    pairs = []
    for i in range(axis_size):
        for c in range(2):
            step = distance if c == 0 else -distance
            pairs.append((i * 2 + c, (i + step) % axis_size * 2 + c))
    return pairs


def move_x(array, distance):
    return lax.ppermute(array, ("x", "c"), signed(NX, distance))


def move_z(array, distance):
    return lax.ppermute(array, ("h", "l", "c"), signed(NZ, distance))


def gather(nears, slots, arrays, before=()):
    n = len(arrays)
    return pl.pallas_call(
        functools.partial(gather_kernel, n, nears, len(before) > 0),
        out_shape=[jax.ShapeDtypeStruct((HIGH, OWN * EDGE, EDGE), jnp.float32)] * len(nears),
        in_specs=sm(1) + vm(n + len(before)),
        out_specs=vm(len(nears)),
        scratch_shapes=[pltpu.SMEM((n, TABLE, EDGE), jnp.float32), pltpu.SemaphoreType.DMA((n,))],
        name="gather_more" if before else "gather",
    )(slots, *arrays, *before)


def vm(n):
    return [pl.BlockSpec(memory_space=VMEM)] * n


def sm(n):
    return [pl.BlockSpec(memory_space=SMEM)] * n


def body(
    t2_tiles,
    cycle_ints,
    cycle_left,
    cycle_right,
    cycle_dest,
    lam_ladder,
    ladder_ints,
    ladder_mask,
    partner_slot,
    denom,
):
    f32 = jnp.float32
    payload = pl.pallas_call(
        products_kernel,
        out_shape=jax.ShapeDtypeStruct((ROWS, EDGE), f32),
        in_specs=sm(3) + vm(2),
        out_specs=pl.BlockSpec(memory_space=VMEM),
        scratch_shapes=[pltpu.SMEM((NX * NZ,), jnp.int32)],
        name="products",
    )(cycle_left[0, 0], cycle_right[0, 0], cycle_dest[0, 0], t2_tiles[0, 0], cycle_ints[0, 0])
    got_a = move_x(payload, 1)
    got_b = move_x(payload, -1)
    partial = pl.pallas_call(
        ladder_kernel,
        out_shape=jax.ShapeDtypeStruct((8, OWN * EDGE, EDGE), f32),
        in_specs=sm(1) + vm(2),
        out_specs=pl.BlockSpec(memory_space=VMEM),
        name="ladder",
    )(ladder_mask, lam_ladder, ladder_ints)
    own_slots = jnp.broadcast_to(partner_slot, (NZ, OWN))
    slots = lax.all_to_all(own_slots, ("h", "l"), split_axis=0, concat_axis=0, tiled=True)
    got_a, got_b, slots, partial = lax.optimization_barrier((got_a, got_b, slots, partial))
    got_c = move_x(got_a, 1)

    near = gather(NEAR, slots, (payload, got_a, got_b))
    near, partial = lax.optimization_barrier((near, partial))
    spread = lax.all_to_all(partial, ("y", "c"), split_axis=0, concat_axis=0, tiled=True)
    ladder = jnp.sum(spread, axis=0)
    n_occ = NX * NZ
    mirror = [(i, n_occ - 1 - i) for i in range(n_occ)]
    other = lax.ppermute(ladder, ("x", "h", "l"), mirror)

    first = gather(NEAR[:1], slots, (got_c,), near[:1])
    moved = [move_z(first[0], NEAR[0])]
    first, others = lax.optimization_barrier((first, near[1:]))
    rest = gather(NEAR[1:], slots, (got_c,), others)
    moved += [move_z(rest[j], NEAR[1 + j]) for j in range(2)]
    far = rest[2] + moved[0] + moved[1] + moved[2]
    far, other = lax.optimization_barrier((far, other))
    far = lax.all_to_all(far, "h", split_axis=0, concat_axis=0, tiled=True)
    other = other.reshape(OWN, EDGE, EDGE)[partner_slot[0]][:, ::-1, ::-1]
    ladder = ladder + other.reshape(OWN * EDGE, EDGE)
    return (ladder + far[0] + far[1] + far[2] + far[3]) / denom


def solution(mesh):
    grid = Mesh(mesh.devices.reshape(NX, HIGH, LOW, 4, 2), ("x", "h", "l", "y", "c"))
    occ = ("x", "h", "l")
    vir = ("y", "c")
    in_specs = (
        P(occ, vir, None, None, None),
        P(occ, vir, None, None, None),
        P(occ, vir, None),
        P(occ, vir, None),
        P(occ, vir, None),
        P(occ, vir),
        P(vir, None),
        P(occ, vir),
        P(occ, None),
        P(occ, vir),
    )
    return jax.shard_map(
        body, mesh=grid, in_specs=in_specs, out_specs=P(occ, vir), check_vma=False
    )
```

time: 150 us -> 142 us (0.947)
  starting transfers between devices: 61.6 us -> 51.1 us
  waiting for transfers between devices: 54.9 us -> 61.1 us
  other arithmetic: 6.28 us -> 1.69 us
    ppermute x1, waiting for transfers between devices: 32 us -> 3.3 us  [body(): other = lax.ppermute(ladder, ('x', 'h', 'l'), mirror)]
    all_to_all x1, waiting for transfers between devices: 0.01 us -> 22.8 us  [body(): far = lax.all_to_all(far, 'h', split_axis=0, concat_axis=0, tiled=True)]
    all_to_all x1, waiting for transfers between devices: 0.01 us -> 8.41 us  [body(): lax.all_to_all(own_slots, ('h', 'l'), split_axis=0, concat_axis=0, tiled=...]
    pallas_call x2 -> x3, Pallas kernels: 11.3 us -> 15.4 us  [gather(): pl.pallas_call(functools.partial(gather_kernel, n, nears, len(before) > 0...]
    all_to_all x1, starting transfers between devices: 8.62 us -> 4.7 us  [body(): lax.all_to_all(partial, ('y', 'c'), split_axis=0, concat_axis=0, tiled=True)]
    ppermute x3, waiting for transfers between devices: 20.4 us -> 23.4 us  [move_z(): return lax.ppermute(array, ('h', 'l', 'c'), signed(NZ, distance))]
    ppermute x1, starting transfers between devices: 6.56 us -> 4.1 us  [body(): other = lax.ppermute(ladder, ('x', 'h', 'l'), mirror)]
    convert_element_type x4 -> x0, other arithmetic: 2.26 us -> none  [body(): a[PAIRS * EDGE:].reshape(-1)[:ENTRIES].astype(jnp.int32)]
  transfers between devices with their start and end apart: 10 -> 10, of which waited for: 4 -> 7; matrix products, arithmetic and copies ran while one was open for 6% -> 2% of each run, Pallas kernels for 11% -> 14%
where the time goes in v3:
time: 142 us; the launch traced here: 141 us
  waiting for transfers between devices  61.1 us (43%)
  starting transfers between devices  51.1 us (36%)
  Pallas kernels  22.4 us (16%)
  local copies, waits for them, and re-layouts  4.1 us (3%)
  other arithmetic  1.69 us (1%)
    ppermute x3, waiting for transfers between devices, move_z(): return lax.ppermute(array, ('h', 'l', 'c'), signed(NZ, distance))  23.4 us
    all_to_all x1, waiting for transfers between devices, body(): far = lax.all_to_all(far, 'h', split_axis=0, concat_axis=0, tiled=True)  22.8 us
    pallas_call x3, Pallas kernels, gather(): pl.pallas_call(functools.partial(gather_kernel, n, nears, len(before) > 0...  15.4 us
    all_to_all x1, starting transfers between devices, body(): lax.all_to_all(own_slots, ('h', 'l'), split_axis=0, concat_axis=0, tiled=...  15.2 us
    ppermute x3, starting transfers between devices, move_x(): return lax.ppermute(array, ('x', 'c'), signed(NX, distance))  9.22 us
    ppermute x3, starting transfers between devices, move_z(): return lax.ppermute(array, ('h', 'l', 'c'), signed(NZ, distance))  9.1 us
    all_to_all x1, starting transfers between devices, body(): far = lax.all_to_all(far, 'h', split_axis=0, concat_axis=0, tiled=True)  8.82 us
    all_to_all x1, waiting for transfers between devices, body(): lax.all_to_all(own_slots, ('h', 'l'), split_axis=0, concat_axis=0, tiled=...  8.41 us
  transfers between devices with their start and end apart: 10, of which 7 were waited for; matrix products, arithmetic and copies ran while one was open for 2% of the time, Pallas kernels for 14%

profile of v3, /device:TPU:24, one launch (start us, length us, event | category | flops | bytes accessed | tf_op | source)
XLA Modules:
  0.0 140.5 jit_solution(1245402473004396334)
XLA Ops:
  0.0 0.0 copy-start.5
  0.0 3.0 %products.1.refs_0_ = f32[2056,128]{1,0:T(8,128)} custom-call(s32[96]{0:T(128)} %bitcast.44, s32[96]{0:T(128)} %bitcast.45, s32[96]{0:T(128)} %bitcast.46, f32[4,128,256]{2,1,0:T(8,128)} %bitcast.40, f32[4,256,128]{2,1,0:T(8,128)} %bitcast.41), custom_call_target="tpu_custom_call" | custom-call | tf_op jit(solution)/shard_map/products/pallas_call | solution.py:193
  3.0 3.4 %collective-permute-start = (f32[2056,128]{1,0:T(8,128)}, f32[2056,128]{1,0:T(8,128)S(1)}, u32[]{:S(2)}, u32[]{:S(2)}) collective-permute-start(f32[2056,128]{1,0:T(8,128)} %products.1.refs_0_), channel_id=1, source_target_pairs={{0,128},{1,385},{128,256},{129,1},{256,384},{257,129},{384,0},{385... | collective-permute-start | bytes 3158024 | tf_op jit(solution)/shard_map/ppermute | solution.py:153
  6.4 3.7 %collective-permute-start.1 = (f32[2056,128]{1,0:T(8,128)}, f32[2056,128]{1,0:T(8,128)S(1)}, u32[]{:S(2)}, u32[]{:S(2)}) collective-permute-start(f32[2056,128]{1,0:T(8,128)} %products.1.refs_0_), channel_id=1, source_target_pairs={{0,384},{1,129},{128,0},{129,257},{256,128},{257,385},{384,256},{3... | collective-permute-start | bytes 3158024 | tf_op jit(solution)/shard_map/ppermute | solution.py:153
  10.1 0.0 copy-done.5
  10.1 0.6 broadcast_in_dim.2
  10.7 15.2 %all-to-all-start = ((s32[16,1,2]{2,1,0:T(1,128)}), s32[16,1,2]{2,1,0:T(1,128)S(1)}, u32[]{:S(2)}, u32[]{:S(2)}) async-start(s32[16,1,2]{2,1,0:T(1,128)} %broadcast_in_dim.2), calls=%async_computation | async-start | bytes 16384 | tf_op jit(solution)/shard_map/all_to_all | solution.py:211
  25.9 4.0 %ladder.1 = f32[8,256,128]{2,1,0:T(8,128)} custom-call(s32[2,4]{1,0:T(2,128)} %mask.1, f32[256,512]{1,0:T(8,128)} %lam_ref.1, f32[512,1024]{1,0:T(8,128)} %ints_ref.1), custom_call_target="tpu_custom_call" | custom-call | tf_op jit(solution)/shard_map/ladder/pallas_call | solution.py:203
  29.8 8.4 %all-to-all-done = s32[16,1,2]{2,1,0:T(1,128)S(1)} async-done(((s32[16,1,2]{2,1,0:T(1,128)}), s32[16,1,2]{2,1,0:T(1,128)S(1)}, u32[]{:S(2)}, u32[]{:S(2)}) %all-to-all-start) | async-done | bytes 160 | tf_op jit(solution)/shard_map/all_to_all | solution.py:211
  38.3 0.1 copy.14
  38.3 0.0 collective-permute-done.refs_1_
  38.3 0.0 copy-start.1
  38.3 0.0 collective-permute-done.1.refs_2_
  38.3 0.0 copy-start.2
  38.4 1.0 copy-done.2
  39.4 2.2 %collective-permute-start.2 = (f32[2056,128]{1,0:T(8,128)S(1)}, f32[2056,128]{1,0:T(8,128)S(1)}, u32[]{:S(2)}, u32[]{:S(2)}) collective-permute-start(f32[2056,128]{1,0:T(8,128)S(1)} %collective-permute-done.refs_1_), channel_id=1, source_target_pairs={{0,128},{1,385},{128,256},{129,1},{256,384},{257,129},{384,0},{385... | collective-permute-start | bytes 3158024 | tf_op jit(solution)/shard_map/ppermute | solution.py:153
  41.5 0.7 copy.15.slots
  42.2 0.0 copy-done.1
  42.2 7.2 %gather.7 = (f32[4,256,128]{2,1,0:T(8,128)}, f32[4,256,128]{2,1,0:T(8,128)}, f32[4,256,128]{2,1,0:T(8,128)}, f32[4,256,128]{2,1,0:T(8,128)}) custom-call(s32[16,2]{1,0:T(8,128)} %copy.15.slots, f32[2056,128]{1,0:T(8,128)} %products.1.refs_0_, f32[2056,128]{1,0:T(8,128)} %copy-done.1, f32[2056,128]{1,0:T(8,128)} %copy-done.2), custom_call_target="tpu_custom_call" | custom-call | tf_op jit(solution)/shard_map/gather/pallas_call | solution.py:162
  49.4 4.7 %all-to-all-start.1 = ((f32[8,256,128]{2,1,0:T(8,128)}), f32[8,256,128]{2,1,0:T(8,128)S(1)}, u32[]{:S(2)}, u32[]{:S(2)}) async-start(f32[8,256,128]{2,1,0:T(8,128)} %ladder.1), calls=%async_computation.1 | async-start | bytes 2097152 | tf_op jit(solution)/shard_map/all_to_all | solution.py:217
  54.1 3.2 %collective-permute-done.2.refs_0_ = f32[2056,128]{1,0:T(8,128)S(1)} collective-permute-done((f32[2056,128]{1,0:T(8,128)S(1)}, f32[2056,128]{1,0:T(8,128)S(1)}, u32[]{:S(2)}, u32[]{:S(2)}) %collective-permute-start.2) | collective-permute-done | bytes 1052704 | tf_op jit(solution)/shard_map/ppermute | solution.py:153
  57.3 0.0 copy-start
  57.3 1.0 copy-done
  58.3 3.3 %gather_more.2 = f32[4,256,128]{2,1,0:T(8,128)} custom-call(s32[16,2]{1,0:T(8,128)} %copy.15.slots, f32[2056,128]{1,0:T(8,128)} %copy-done, f32[4,256,128]{2,1,0:T(8,128)} %get-tuple-element.35.refs_1_), custom_call_target="tpu_custom_call" | custom-call | tf_op jit(solution)/shard_map/gather_more/pallas_call | solution.py:162
  61.6 4.9 %gather_more.3 = (f32[4,256,128]{2,1,0:T(8,128)}, f32[4,256,128]{2,1,0:T(8,128)}, f32[4,256,128]{2,1,0:T(8,128)}) custom-call(s32[16,2]{1,0:T(8,128)} %copy.15.slots, f32[2056,128]{1,0:T(8,128)} %copy-done, f32[4,256,128]{2,1,0:T(8,128)} %get-tuple-element.39.refs_1_, f32[4,256,128]{2,1,0:T(8,128)} %get-tuple-element.40.refs_2_, ...), custom_call_target="tpu_custom_call" | custom-call | tf_op jit(solution)/shard_map/gather_more/pallas_call | solution.py:162
  66.5 0.0 copy-start.3
  66.5 2.6 %collective-permute-start.4 = (f32[4,256,128]{2,1,0:T(8,128)}, f32[4,256,128]{2,1,0:T(8,128)S(1)}, u32[]{:S(2)}, u32[]{:S(2)}) collective-permute-start(f32[4,256,128]{2,1,0:T(8,128)} %get-tuple-element.43), channel_id=1, source_target_pairs={{0,8},{1,121},{8,16},{9,1},{16,24},{17,9},{24,32},{25,17},{32,40},... | collective-permute-start | bytes 1572872 | tf_op jit(solution)/shard_map/ppermute | solution.py:157
  69.1 4.5 %collective-permute-start.5 = (f32[4,256,128]{2,1,0:T(8,128)}, f32[4,256,128]{2,1,0:T(8,128)S(1)}, u32[]{:S(2)}, u32[]{:S(2)}) collective-permute-start(f32[4,256,128]{2,1,0:T(8,128)} %get-tuple-element.44), channel_id=1, source_target_pairs={{0,120},{1,9},{8,0},{9,17},{16,8},{17,25},{24,16},{25,33},{32,24},... | collective-permute-start | bytes 1572872 | tf_op jit(solution)/shard_map/ppermute | solution.py:157
  73.7 1.9 %collective-permute-start.3 = (f32[4,256,128]{2,1,0:T(8,128)}, f32[4,256,128]{2,1,0:T(8,128)S(1)}, u32[]{:S(2)}, u32[]{:S(2)}) collective-permute-start(f32[4,256,128]{2,1,0:T(8,128)} %gather_more.2), channel_id=1, source_target_pairs={{0,16},{1,113},{8,24},{9,121},{16,32},{17,1},{24,40},{25,9},{32,48... | collective-permute-start | bytes 1572872 | tf_op jit(solution)/shard_map/ppermute | solution.py:157
  75.6 0.0 all-to-all-done.1
  75.6 0.1 reduce_sum.9
  75.7 4.1 %collective-permute-start.6 = (f32[256,128]{1,0:T(8,128)S(1)}, f32[256,128]{1,0:T(8,128)S(1)}, u32[]{:S(2)}, u32[]{:S(2)}) collective-permute-start(f32[256,128]{1,0:T(8,128)S(1)} %reduce_sum.9), channel_id=1, source_target_pairs={{0,504},{8,496},{16,488},{24,480},{32,472},{40,464},{48,456},{56,4... | collective-permute-start | bytes 393224 | tf_op jit(solution)/shard_map/ppermute | solution.py:221
  79.8 2.9 %collective-permute-done.4 = f32[4,256,128]{2,1,0:T(8,128)S(1)} collective-permute-done((f32[4,256,128]{2,1,0:T(8,128)}, f32[4,256,128]{2,1,0:T(8,128)S(1)}, u32[]{:S(2)}, u32[]{:S(2)}) %collective-permute-start.4) | collective-permute-done | bytes 524320 | tf_op jit(solution)/shard_map/ppermute | solution.py:157
  82.7 17.6 %collective-permute-done.5 = f32[4,256,128]{2,1,0:T(8,128)S(1)} collective-permute-done((f32[4,256,128]{2,1,0:T(8,128)}, f32[4,256,128]{2,1,0:T(8,128)S(1)}, u32[]{:S(2)}, u32[]{:S(2)}) %collective-permute-start.5) | collective-permute-done | bytes 524320 | tf_op jit(solution)/shard_map/ppermute | solution.py:157
  100.3 2.9 %collective-permute-done.3 = f32[4,256,128]{2,1,0:T(8,128)S(1)} collective-permute-done((f32[4,256,128]{2,1,0:T(8,128)}, f32[4,256,128]{2,1,0:T(8,128)S(1)}, u32[]{:S(2)}, u32[]{:S(2)}) %collective-permute-start.3) | collective-permute-done | bytes 524320 | tf_op jit(solution)/shard_map/ppermute | solution.py:157
  103.2 0.0 copy-done.3
  103.2 0.9 add_add_fusion
  104.1 0.0 copy-start.4
  104.1 3.3 %collective-permute-done.6 = f32[256,128]{1,0:T(8,128)S(1)} collective-permute-done((f32[256,128]{1,0:T(8,128)S(1)}, f32[256,128]{1,0:T(8,128)S(1)}, u32[]{:S(2)}, u32[]{:S(2)}) %collective-permute-start.6) | collective-permute-done | bytes 131104 | tf_op jit(solution)/shard_map/ppermute | solution.py:221
  107.4 8.8 %all-to-all-start.2 = ((f32[4,256,128]{2,1,0:T(8,128)}), f32[4,256,128]{2,1,0:T(8,128)S(1)}, u32[]{:S(2)}, u32[]{:S(2)}) async-start(f32[4,256,128]{2,1,0:T(8,128)} %add_add_fusion), calls=%async_computation.2 | async-start | bytes 1048576 | tf_op jit(solution)/shard_map/all_to_all | solution.py:230
  116.2 0.6 gather_fusion
  116.8 0.2 rev.3
  117.0 22.8 %all-to-all-done.2 = f32[4,256,128]{2,1,0:T(8,128)S(1)} async-done(((f32[4,256,128]{2,1,0:T(8,128)}), f32[4,256,128]{2,1,0:T(8,128)S(1)}, u32[]{:S(2)}, u32[]{:S(2)}) %all-to-all-start.2) | async-done | bytes 524320 | tf_op jit(solution)/shard_map/all_to_all | solution.py:230
  139.8 0.0 copy-done.4
  139.8 0.7 fusion.1
  (2 shorter events, 0.0 us)
Async XLA Ops:
  0.0 10.1 %copy-start.5 = (s32[1,2]{1,0:T(1,128)S(1)}, s32[1,2]{1,0:T(1,128)}, u32[]{:S(2)}) copy-start(s32[1,2]{1,0:T(1,128)} %param.18) | copy-start | bytes 28
  3.0 35.3 %collective-permute-start = (f32[2056,128]{1,0:T(8,128)}, f32[2056,128]{1,0:T(8,128)S(1)}, u32[]{:S(2)}, u32[]{:S(2)}) collective-permute-start(f32[2056,128]{1,0:T(8,128)} %products.1.refs_0_), channel_id=1, source_target_pairs={{0,128},{1,385},{128,256},{129,1},{256,384},{257,129},{384,0},{385... | collective-permute-start | bytes 3158024 | tf_op jit(solution)/shard_map/ppermute | solution.py:153
  6.4 31.9 %collective-permute-start.1 = (f32[2056,128]{1,0:T(8,128)}, f32[2056,128]{1,0:T(8,128)S(1)}, u32[]{:S(2)}, u32[]{:S(2)}) collective-permute-start(f32[2056,128]{1,0:T(8,128)} %products.1.refs_0_), channel_id=1, source_target_pairs={{0,384},{1,129},{128,0},{129,257},{256,128},{257,385},{384,256},{3... | collective-permute-start | bytes 3158024 | tf_op jit(solution)/shard_map/ppermute | solution.py:153
  10.7 27.6 %all-to-all-start = ((s32[16,1,2]{2,1,0:T(1,128)}), s32[16,1,2]{2,1,0:T(1,128)S(1)}, u32[]{:S(2)}, u32[]{:S(2)}) async-start(s32[16,1,2]{2,1,0:T(1,128)} %broadcast_in_dim.2), calls=%async_computation | async-start | bytes 16384 | tf_op jit(solution)/shard_map/all_to_all | solution.py:211
  38.3 3.9 %copy-start.1 = (f32[2056,128]{1,0:T(8,128)}, f32[2056,128]{1,0:T(8,128)S(1)}, u32[]{:S(2)}) copy-start(f32[2056,128]{1,0:T(8,128)S(1)} %collective-permute-done.refs_1_) | copy-start | bytes 3158020
  38.3 1.0 copy-start.2
  39.4 17.9 %collective-permute-start.2 = (f32[2056,128]{1,0:T(8,128)S(1)}, f32[2056,128]{1,0:T(8,128)S(1)}, u32[]{:S(2)}, u32[]{:S(2)}) collective-permute-start(f32[2056,128]{1,0:T(8,128)S(1)} %collective-permute-done.refs_1_), channel_id=1, source_target_pairs={{0,128},{1,385},{128,256},{129,1},{256,384},{257,129},{384,0},{385... | collective-permute-start | bytes 3158024 | tf_op jit(solution)/shard_map/ppermute | solution.py:153
  49.4 26.2 %all-to-all-start.1 = ((f32[8,256,128]{2,1,0:T(8,128)}), f32[8,256,128]{2,1,0:T(8,128)S(1)}, u32[]{:S(2)}, u32[]{:S(2)}) async-start(f32[8,256,128]{2,1,0:T(8,128)} %ladder.1), calls=%async_computation.1 | async-start | bytes 2097152 | tf_op jit(solution)/shard_map/all_to_all | solution.py:217
  57.3 1.0 copy-start
  66.5 36.7 %copy-start.3 = (f32[4,256,128]{2,1,0:T(8,128)S(1)}, f32[4,256,128]{2,1,0:T(8,128)}, u32[]{:S(2)}) copy-start(f32[4,256,128]{2,1,0:T(8,128)} %get-tuple-element.42) | copy-start | bytes 1572868
  66.5 16.2 %collective-permute-start.4 = (f32[4,256,128]{2,1,0:T(8,128)}, f32[4,256,128]{2,1,0:T(8,128)S(1)}, u32[]{:S(2)}, u32[]{:S(2)}) collective-permute-start(f32[4,256,128]{2,1,0:T(8,128)} %get-tuple-element.43), channel_id=1, source_target_pairs={{0,8},{1,121},{8,16},{9,1},{16,24},{17,9},{24,32},{25,17},{32,40},... | collective-permute-start | bytes 1572872 | tf_op jit(solution)/shard_map/ppermute | solution.py:157
  69.1 31.1 %collective-permute-start.5 = (f32[4,256,128]{2,1,0:T(8,128)}, f32[4,256,128]{2,1,0:T(8,128)S(1)}, u32[]{:S(2)}, u32[]{:S(2)}) collective-permute-start(f32[4,256,128]{2,1,0:T(8,128)} %get-tuple-element.44), channel_id=1, source_target_pairs={{0,120},{1,9},{8,0},{9,17},{16,8},{17,25},{24,16},{25,33},{32,24},... | collective-permute-start | bytes 1572872 | tf_op jit(solution)/shard_map/ppermute | solution.py:157
  73.7 29.5 %collective-permute-start.3 = (f32[4,256,128]{2,1,0:T(8,128)}, f32[4,256,128]{2,1,0:T(8,128)S(1)}, u32[]{:S(2)}, u32[]{:S(2)}) collective-permute-start(f32[4,256,128]{2,1,0:T(8,128)} %gather_more.2), channel_id=1, source_target_pairs={{0,16},{1,113},{8,24},{9,121},{16,32},{17,1},{24,40},{25,9},{32,48... | collective-permute-start | bytes 1572872 | tf_op jit(solution)/shard_map/ppermute | solution.py:157
  75.7 31.7 %collective-permute-start.6 = (f32[256,128]{1,0:T(8,128)S(1)}, f32[256,128]{1,0:T(8,128)S(1)}, u32[]{:S(2)}, u32[]{:S(2)}) collective-permute-start(f32[256,128]{1,0:T(8,128)S(1)} %reduce_sum.9), channel_id=1, source_target_pairs={{0,504},{8,496},{16,488},{24,480},{32,472},{40,464},{48,456},{56,4... | collective-permute-start | bytes 393224 | tf_op jit(solution)/shard_map/ppermute | solution.py:221
  104.1 35.7 %copy-start.4 = (f32[256,128]{1,0:T(8,128)S(1)}, f32[256,128]{1,0:T(8,128)}, u32[]{:S(2)}) copy-start(f32[256,128]{1,0:T(8,128)} %param.19) | copy-start | bytes 393220
  107.4 32.4 %all-to-all-start.2 = ((f32[4,256,128]{2,1,0:T(8,128)}), f32[4,256,128]{2,1,0:T(8,128)S(1)}, u32[]{:S(2)}, u32[]{:S(2)}) async-start(f32[4,256,128]{2,1,0:T(8,128)} %add_add_fusion), calls=%async_computation.2 | async-start | bytes 1048576 | tf_op jit(solution)/shard_map/all_to_all | solution.py:230

commit v4 on v3

--- a/solution.py
+++ b/solution.py
@@ -88,13 +88,14 @@
     return jnp.concatenate(parts, axis=0)
 
 
-def gather_kernel(sources, nears, more, slots, *refs):
+def gather_kernel(sources, more, slots, *refs):
     tiles = refs[:sources]
     refs = refs[sources:]
-    befores = refs[: len(nears)] if more else (None,) * len(nears)
-    refs = refs[len(nears) :] if more else refs
-    outs = refs[: len(nears)]
-    tables, sems = refs[len(nears) :]
+    cells = [(near, s) for near in NEAR for s in range(OWN)]
+    befores = refs[: len(cells)] if more else (None,) * len(cells)
+    refs = refs[len(cells) :] if more else refs
+    outs = refs[: len(cells)]
+    tables, sems = refs[len(cells) :]
     copies = [
         pltpu.make_async_copy(tile.at[pl.ds(PAIRS * EDGE, TABLE)], tables.at[i], sems.at[i])
         for i, tile in enumerate(tiles)
@@ -106,10 +107,10 @@
     sign = 1 - 2 * lax.axis_index("c")
     for copy in copies:
         copy.wait()
-    for near, before, out in zip(nears, befores, outs):
+    for j, near in enumerate(NEAR):
         low = jnp.bitwise_and(z + sign * near + NZ, LOW - 1)
 
-        def dest(a, carry, low=low, before=before, out=out):
+        def dest(a, carry, low=low, j=j):
             target = a * LOW + low
             owner = base + target
             sums = []
@@ -130,11 +131,11 @@
                             acc[s] = acc[s] + val * (slot == want).astype(jnp.float32)
                 sums.append(acc)
             for s in range(OWN):
-                rows = pl.ds(s * EDGE, EDGE)
                 total = sums[0][s] + flipped(sums[1][s])
+                before = befores[j * OWN + s]
                 if before is not None:
-                    total = total + before[a, rows, :]
-                out[a, rows, :] = total
+                    total = total + before[a]
+                outs[j * OWN + s][a] = total
             return carry
 
         lax.fori_loop(0, HIGH, dest, 0)
@@ -157,16 +158,17 @@
     return lax.ppermute(array, ("h", "l", "c"), signed(NZ, distance))
 
 
-def gather(nears, slots, arrays, before=()):
+def gather(slots, arrays, before=()):
     n = len(arrays)
+    cells = OWN * len(NEAR)
     return pl.pallas_call(
-        functools.partial(gather_kernel, n, nears, len(before) > 0),
-        out_shape=[jax.ShapeDtypeStruct((HIGH, OWN * EDGE, EDGE), jnp.float32)] * len(nears),
+        functools.partial(gather_kernel, n, len(before) > 0),
+        out_shape=[jax.ShapeDtypeStruct((HIGH, EDGE, EDGE), jnp.float32)] * cells,
         in_specs=sm(1) + vm(n + len(before)),
-        out_specs=vm(len(nears)),
+        out_specs=vm(cells),
         scratch_shapes=[pltpu.SMEM((n, TABLE, EDGE), jnp.float32), pltpu.SemaphoreType.DMA((n,))],
         name="gather_more" if before else "gather",
-    )(slots, *arrays, *before)
+    )(slots, *[pltpu.with_memory_space_constraint(a, VMEM) for a in (*arrays, *before)])
 
 
 def vm(n):
@@ -207,12 +209,15 @@
         out_specs=pl.BlockSpec(memory_space=VMEM),
         name="ladder",
     )(ladder_mask, lam_ladder, ladder_ints)
-    own_slots = jnp.broadcast_to(partner_slot, (NZ, OWN))
+    own_slots = jnp.broadcast_to(partner_slot[0], (NZ, 32, OWN)) if 32 == 1 else jnp.broadcast_to(
+        jnp.pad(partner_slot, ((0, 0), (0, EDGE - OWN))), (NZ, 32, EDGE)
+    )
     slots = lax.all_to_all(own_slots, ("h", "l"), split_axis=0, concat_axis=0, tiled=True)
-    got_a, got_b, slots, partial = lax.optimization_barrier((got_a, got_b, slots, partial))
+    slots = slots[:, 0, :OWN]
+    got_a, got_b, partial = lax.optimization_barrier((got_a, got_b, partial))
     got_c = move_x(got_a, 1)
 
-    near = gather(NEAR, slots, (payload, got_a, got_b))
+    near = gather(slots, (payload, got_a, got_b))
     near, partial = lax.optimization_barrier((near, partial))
     spread = lax.all_to_all(partial, ("y", "c"), split_axis=0, concat_axis=0, tiled=True)
     ladder = jnp.sum(spread, axis=0)
@@ -220,17 +225,20 @@
     mirror = [(i, n_occ - 1 - i) for i in range(n_occ)]
     other = lax.ppermute(ladder, ("x", "h", "l"), mirror)
 
-    first = gather(NEAR[:1], slots, (got_c,), near[:1])
-    moved = [move_z(first[0], NEAR[0])]
-    first, others = lax.optimization_barrier((first, near[1:]))
-    rest = gather(NEAR[1:], slots, (got_c,), others)
-    moved += [move_z(rest[j], NEAR[1 + j]) for j in range(2)]
-    far = rest[2] + moved[0] + moved[1] + moved[2]
-    far, other = lax.optimization_barrier((far, other))
-    far = lax.all_to_all(far, "h", split_axis=0, concat_axis=0, tiled=True)
+    near = gather(slots, (got_c,), near)
+    halves_done = []
+    for s in range(OWN):
+        cells = near[s::OWN]
+        far = cells[3]
+        for j in range(3):
+            far = far + move_z(cells[j], NEAR[j])
+        if s == OWN - 1:
+            far, other = lax.optimization_barrier((far, other))
+        far = lax.all_to_all(far, "h", split_axis=0, concat_axis=0, tiled=True)
+        halves_done.append(far[0] + far[1] + far[2] + far[3])
     other = other.reshape(OWN, EDGE, EDGE)[partner_slot[0]][:, ::-1, ::-1]
     ladder = ladder + other.reshape(OWN * EDGE, EDGE)
-    return (ladder + far[0] + far[1] + far[2] + far[3]) / denom
+    return (ladder + jnp.concatenate(halves_done, axis=0)) / denom
 
 
 def solution(mesh):

time: 142 us -> 155 us (1.092)
  starting transfers between devices: 51.1 us -> 72 us
  waiting for transfers between devices: 61.1 us -> 56.8 us
  Pallas kernels: 22.4 us -> 18.2 us
  other arithmetic: 1.69 us -> 4.51 us
  local copies, waits for them, and re-layouts: 4.1 us -> 2.14 us
    ppermute x3 -> x6, starting transfers between devices: 9.1 us -> 21.1 us  [move_z(): return lax.ppermute(array, ('h', 'l', 'c'), signed(NZ, distance))]
    all_to_all x1 -> x2, starting transfers between devices: 8.82 us -> 15.2 us  [body(): far = lax.all_to_all(far, 'h', split_axis=0, concat_axis=0, tiled=True)]
    all_to_all x1 -> x2, waiting for transfers between devices: 22.8 us -> 17.6 us  [body(): far = lax.all_to_all(far, 'h', split_axis=0, concat_axis=0, tiled=True)]
    pallas_call x3 -> x2, Pallas kernels: 15.4 us -> 11.2 us  [gather(): pl.pallas_call(functools.partial(gather_kernel, n, len(before) > 0), out_...]
    ppermute x3 -> x6, waiting for transfers between devices: 23.4 us -> 26.2 us  [move_z(): return lax.ppermute(array, ('h', 'l', 'c'), signed(NZ, distance))]
    ppermute x3, waiting for transfers between devices: 3.16 us -> 0.41 us  [move_x(): return lax.ppermute(array, ('x', 'c'), signed(NX, distance))]
    all_to_all x1, waiting for transfers between devices: 8.41 us -> 10.4 us  [body(): lax.all_to_all(own_slots, ('h', 'l'), split_axis=0, concat_axis=0, tiled=...]
    unnamed x12 -> x30, local copies, waits for them, and re-layouts: 2 us -> 0.06 us
  transfers between devices with their start and end apart: 10 -> 14, of which waited for: 7 -> 7; matrix products, arithmetic and copies ran while one was open for 2% -> 4% of each run, Pallas kernels for 14% -> 10%
where the time goes in v4:
time: 155 us; the launch traced here: 154 us
  starting transfers between devices  72 us (46%)
  waiting for transfers between devices  56.8 us (37%)
  Pallas kernels  18.2 us (12%)
  other arithmetic  4.51 us (3%)
  local copies, waits for them, and re-layouts  2.14 us (1%)
    ppermute x6, waiting for transfers between devices, move_z(): return lax.ppermute(array, ('h', 'l', 'c'), signed(NZ, distance))  26.2 us
    ppermute x6, starting transfers between devices, move_z(): return lax.ppermute(array, ('h', 'l', 'c'), signed(NZ, distance))  21.1 us
    all_to_all x2, waiting for transfers between devices, body(): far = lax.all_to_all(far, 'h', split_axis=0, concat_axis=0, tiled=True)  17.6 us
    all_to_all x1, starting transfers between devices, body(): lax.all_to_all(own_slots, ('h', 'l'), split_axis=0, concat_axis=0, tiled=...  15.2 us
    all_to_all x2, starting transfers between devices, body(): far = lax.all_to_all(far, 'h', split_axis=0, concat_axis=0, tiled=True)  15.2 us
    pallas_call x2, Pallas kernels, gather(): pl.pallas_call(functools.partial(gather_kernel, n, len(before) > 0), out_...  11.2 us
    all_to_all x1, waiting for transfers between devices, body(): lax.all_to_all(own_slots, ('h', 'l'), split_axis=0, concat_axis=0, tiled=...  10.4 us
    ppermute x3, starting transfers between devices, move_x(): return lax.ppermute(array, ('x', 'c'), signed(NX, distance))  10 us
  transfers between devices with their start and end apart: 14, of which 7 were waited for; matrix products, arithmetic and copies ran while one was open for 4% of the time, Pallas kernels for 10%

profile of v4, /device:TPU:24, one launch (start us, length us, event | category | flops | bytes accessed | tf_op | source)
XLA Modules:
  0.0 154.0 jit_solution(16074918841210797137)
XLA Ops:
  0.0 3.0 %products.1.refs_0_ = f32[2056,128]{1,0:T(8,128)} custom-call(s32[96]{0:T(128)} %bitcast.26, s32[96]{0:T(128)} %bitcast.27, s32[96]{0:T(128)} %bitcast.28, f32[4,128,256]{2,1,0:T(8,128)} %bitcast.21, f32[4,256,128]{2,1,0:T(8,128)} %bitcast.22), custom_call_target="tpu_custom_call" | custom-call | tf_op jit(solution)/shard_map/products/pallas_call | solution.py:195
  3.0 3.4 %collective-permute-start = (f32[2056,128]{1,0:T(8,128)}, f32[2056,128]{1,0:T(8,128)S(1)}, u32[]{:S(2)}, u32[]{:S(2)}) collective-permute-start(f32[2056,128]{1,0:T(8,128)} %products.1.refs_0_), channel_id=1, source_target_pairs={{0,128},{1,385},{128,256},{129,1},{256,384},{257,129},{384,0},{385... | collective-permute-start | bytes 3158024 | tf_op jit(solution)/shard_map/ppermute | solution.py:154
  6.4 3.7 %collective-permute-start.1 = (f32[2056,128]{1,0:T(8,128)}, f32[2056,128]{1,0:T(8,128)S(1)}, u32[]{:S(2)}, u32[]{:S(2)}) collective-permute-start(f32[2056,128]{1,0:T(8,128)} %products.1.refs_0_), channel_id=1, source_target_pairs={{0,384},{1,129},{128,0},{129,257},{256,128},{257,385},{384,256},{3... | collective-permute-start | bytes 3158024 | tf_op jit(solution)/shard_map/ppermute | solution.py:154
  10.1 0.0 copy-done.14
  10.1 0.7 broadcast_in_dim.2
  10.8 15.2 %all-to-all-start = ((s32[16,32,128]{2,1,0:T(8,128)}), s32[16,32,128]{2,1,0:T(8,128)S(1)}, u32[]{:S(2)}, u32[]{:S(2)}) async-start(s32[16,32,128]{2,1,0:T(8,128)} %broadcast_in_dim.2), calls=%async_computation | async-start | bytes 524288 | tf_op jit(solution)/shard_map/all_to_all | solution.py:215
  26.0 4.0 %ladder.1 = f32[8,256,128]{2,1,0:T(8,128)} custom-call(s32[2,4]{1,0:T(2,128)} %mask.1, f32[256,512]{1,0:T(8,128)} %lam_ref.1, f32[512,1024]{1,0:T(8,128)} %ints_ref.1), custom_call_target="tpu_custom_call" | custom-call | tf_op jit(solution)/shard_map/ladder/pallas_call | solution.py:205
  30.1 0.0 collective-permute-done.refs_1_
  30.1 0.4 collective-permute-done.1.refs_2_
  30.5 3.0 %collective-permute-start.2 = (f32[2056,128]{1,0:T(8,128)S(1)}, f32[2056,128]{1,0:T(8,128)}, u32[]{:S(2)}, u32[]{:S(2)}) collective-permute-start(f32[2056,128]{1,0:T(8,128)S(1)} %collective-permute-done.refs_1_), channel_id=1, source_target_pairs={{0,128},{1,385},{128,256},{129,1},{256,384},{257,129},{384,0},{385... | collective-permute-start | bytes 3158024 | tf_op jit(solution)/shard_map/ppermute | solution.py:154
  33.5 10.4 %all-to-all-done = s32[16,32,128]{2,1,0:T(8,128)S(1)} async-done(((s32[16,32,128]{2,1,0:T(8,128)}), s32[16,32,128]{2,1,0:T(8,128)S(1)}, u32[]{:S(2)}, u32[]{:S(2)}) %all-to-all-start) | async-done | bytes 262176 | tf_op jit(solution)/shard_map/all_to_all | solution.py:215
  43.9 0.6 slice.38
  44.5 6.0 %gather.7 = (f32[4,128,128]{2,1,0:T(8,128)}, f32[4,128,128]{2,1,0:T(8,128)}, f32[4,128,128]{2,1,0:T(8,128)}, f32[4,128,128]{2,1,0:T(8,128)}, f32[4,128,128]{2,1,...) custom-call(s32[16,2]{1,0:T(8,128)} %bitcast.24, f32[2056,128]{1,0:T(8,128)S(1)} %copy-done, ...), custom_call_target="tpu_custom_call" | custom-call | tf_op jit(solution)/shard_map/gather/pallas_call | solution.py:164
  50.5 4.8 %all-to-all-start.1 = ((f32[8,256,128]{2,1,0:T(8,128)}), f32[8,256,128]{2,1,0:T(8,128)}, u32[]{:S(2)}, u32[]{:S(2)}) async-start(f32[8,256,128]{2,1,0:T(8,128)} %ladder.1), calls=%async_computation.1 | async-start | bytes 2097152 | tf_op jit(solution)/shard_map/all_to_all | solution.py:222
  55.4 0.0 collective-permute-done.2.refs_0_
  55.4 0.0 copy-done.1
  55.4 0.0 copy-done.2
  55.4 0.0 copy-done.3
  55.4 0.0 copy-done.4
  55.4 0.0 copy-done.5
  55.4 0.0 copy-done.6
  55.4 0.0 copy-done.7
  55.5 5.2 %gather_more.1 = (f32[4,128,128]{2,1,0:T(8,128)}, f32[4,128,128]{2,1,0:T(8,128)}, f32[4,128,128]{2,1,0:T(8,128)}, f32[4,128,128]{2,1,0:T(8,128)}, f32[4,128,128]...) custom-call(s32[16,2]{1,0:T(8,128)} %bitcast.25, ...), custom_call_target="tpu_custom_call" | custom-call | tf_op jit(solution)/shard_map/gather_more/pallas_call | solution.py:164
  60.7 4.8 %collective-permute-start.7 = (f32[4,128,128]{2,1,0:T(8,128)}, f32[4,128,128]{2,1,0:T(8,128)S(1)}, u32[]{:S(2)}, u32[]{:S(2)}) collective-permute-start(f32[4,128,128]{2,1,0:T(8,128)} %get-tuple-element.61), channel_id=1, source_target_pairs={{0,16},{1,113},{8,24},{9,121},{16,32},{17,1},{24,40},{25,9},{32,48... | collective-permute-start | bytes 786440 | tf_op jit(solution)/shard_map/ppermute | solution.py:158
  65.6 2.9 %collective-permute-start.8 = (f32[4,128,128]{2,1,0:T(8,128)}, f32[4,128,128]{2,1,0:T(8,128)S(1)}, u32[]{:S(2)}, u32[]{:S(2)}) collective-permute-start(f32[4,128,128]{2,1,0:T(8,128)} %get-tuple-element.62), channel_id=1, source_target_pairs={{0,8},{1,121},{8,16},{9,1},{16,24},{17,9},{24,32},{25,17},{32,40},... | collective-permute-start | bytes 786440 | tf_op jit(solution)/shard_map/ppermute | solution.py:158
  68.5 4.1 %collective-permute-start.9 = (f32[4,128,128]{2,1,0:T(8,128)}, f32[4,128,128]{2,1,0:T(8,128)S(1)}, u32[]{:S(2)}, u32[]{:S(2)}) collective-permute-start(f32[4,128,128]{2,1,0:T(8,128)} %get-tuple-element.63), channel_id=1, source_target_pairs={{0,120},{1,9},{8,0},{9,17},{16,8},{17,25},{24,16},{25,33},{32,24},... | collective-permute-start | bytes 786440 | tf_op jit(solution)/shard_map/ppermute | solution.py:158
  72.6 0.0 collective-permute-done.7
  72.6 6.9 %collective-permute-done.8 = f32[4,128,128]{2,1,0:T(8,128)S(1)} collective-permute-done((f32[4,128,128]{2,1,0:T(8,128)}, f32[4,128,128]{2,1,0:T(8,128)S(1)}, u32[]{:S(2)}, u32[]{:S(2)}) %collective-permute-start.8) | collective-permute-done | bytes 262176 | tf_op jit(solution)/shard_map/ppermute | solution.py:158
  79.6 0.0 collective-permute-done.9
  79.6 1.7 %add_add_fusion = f32[4,128,128]{2,1,0:T(8,128)} fusion(f32[4,128,128]{2,1,0:T(8,128)S(1)} %collective-permute-done.9, f32[4,128,128]{2,1,0:T(8,128)S(1)} %collective-permute-done.8, f32[4,128,128]{2,1,0:T(8,128)} %get-tuple-element.60, f32[4,128,128]{2,1,0:T(8,128)S(1)} %collective-permute-done.7), kind=kLoop, calls=%fused_computation.1 | loop fusion | flops 196608 | bytes 1310720 | tf_op jit(solution)/shard_map/add | solution.py:234
  81.3 0.0 all-to-all-done.1
  81.3 8.6 %all-to-all-start.2 = ((f32[4,128,128]{2,1,0:T(8,128)}), f32[4,128,128]{2,1,0:T(8,128)S(1)}, u32[]{:S(2)}, u32[]{:S(2)}) async-start(f32[4,128,128]{2,1,0:T(8,128)} %add_add_fusion), calls=%async_computation.2 | async-start | bytes 524288 | tf_op jit(solution)/shard_map/all_to_all | solution.py:237
  89.9 2.2 %collective-permute-start.3 = (f32[4,128,128]{2,1,0:T(8,128)S(1)}, f32[4,128,128]{2,1,0:T(8,128)S(1)}, u32[]{:S(2)}, u32[]{:S(2)}) collective-permute-start(f32[4,128,128]{2,1,0:T(8,128)S(1)} %copy-done.13), channel_id=1, source_target_pairs={{0,16},{1,113},{8,24},{9,121},{16,32},{17,1},{24,40},{25,9},{32,48... | collective-permute-start | bytes 786440 | tf_op jit(solution)/shard_map/ppermute | solution.py:158
  92.1 2.8 %collective-permute-start.4 = (f32[4,128,128]{2,1,0:T(8,128)S(1)}, f32[4,128,128]{2,1,0:T(8,128)S(1)}, u32[]{:S(2)}, u32[]{:S(2)}) collective-permute-start(f32[4,128,128]{2,1,0:T(8,128)S(1)} %copy-done.12), channel_id=1, source_target_pairs={{0,8},{1,121},{8,16},{9,1},{16,24},{17,9},{24,32},{25,17},{32,40},... | collective-permute-start | bytes 786440 | tf_op jit(solution)/shard_map/ppermute | solution.py:158
  94.9 4.2 %collective-permute-start.5 = (f32[4,128,128]{2,1,0:T(8,128)S(1)}, f32[4,128,128]{2,1,0:T(8,128)S(1)}, u32[]{:S(2)}, u32[]{:S(2)}) collective-permute-start(f32[4,128,128]{2,1,0:T(8,128)S(1)} %copy-done.11), channel_id=1, source_target_pairs={{0,120},{1,9},{8,0},{9,17},{16,8},{17,25},{24,16},{25,33},{32,24},... | collective-permute-start | bytes 786440 | tf_op jit(solution)/shard_map/ppermute | solution.py:158
  99.1 1.3 reduce_sum.9
  100.4 5.6 %collective-permute-start.6 = (f32[256,128]{1,0:T(8,128)S(1)}, f32[256,128]{1,0:T(8,128)S(1)}, u32[]{:S(2)}, u32[]{:S(2)}) collective-permute-start(f32[256,128]{1,0:T(8,128)S(1)} %reduce_sum.9), channel_id=1, source_target_pairs={{0,504},{8,496},{16,488},{24,480},{32,472},{40,464},{48,456},{56,4... | collective-permute-start | bytes 393224 | tf_op jit(solution)/shard_map/ppermute | solution.py:226
  106.0 3.5 %collective-permute-done.3 = f32[4,128,128]{2,1,0:T(8,128)S(1)} collective-permute-done((f32[4,128,128]{2,1,0:T(8,128)S(1)}, f32[4,128,128]{2,1,0:T(8,128)S(1)}, u32[]{:S(2)}, u32[]{:S(2)}) %collective-permute-start.3) | collective-permute-done | bytes 262176 | tf_op jit(solution)/shard_map/ppermute | solution.py:158
  109.5 15.8 %collective-permute-done.4 = f32[4,128,128]{2,1,0:T(8,128)S(1)} collective-permute-done((f32[4,128,128]{2,1,0:T(8,128)S(1)}, f32[4,128,128]{2,1,0:T(8,128)S(1)}, u32[]{:S(2)}, u32[]{:S(2)}) %collective-permute-start.4) | collective-permute-done | bytes 262176 | tf_op jit(solution)/shard_map/ppermute | solution.py:158
  125.3 0.0 collective-permute-done.5
  125.3 0.7 add_add_fusion.1
  126.1 2.2 %collective-permute-done.6 = f32[256,128]{1,0:T(8,128)S(1)} collective-permute-done((f32[256,128]{1,0:T(8,128)S(1)}, f32[256,128]{1,0:T(8,128)S(1)}, u32[]{:S(2)}, u32[]{:S(2)}) %collective-permute-start.6) | collective-permute-done | bytes 131104 | tf_op jit(solution)/shard_map/ppermute | solution.py:226
  128.3 0.0 all-to-all-done.2
  128.3 6.6 %all-to-all-start.3 = ((f32[4,128,128]{2,1,0:T(8,128)}), f32[4,128,128]{2,1,0:T(8,128)S(1)}, u32[]{:S(2)}, u32[]{:S(2)}) async-start(f32[4,128,128]{2,1,0:T(8,128)} %add_add_fusion.1), calls=%async_computation.3 | async-start | bytes 524288 | tf_op jit(solution)/shard_map/all_to_all | solution.py:237
  134.9 0.6 gather_fusion
  135.4 0.2 rev.3
  135.7 17.6 %all-to-all-done.3 = f32[4,128,128]{2,1,0:T(8,128)S(1)} async-done(((f32[4,128,128]{2,1,0:T(8,128)}), f32[4,128,128]{2,1,0:T(8,128)S(1)}, u32[]{:S(2)}, u32[]{:S(2)}) %all-to-all-start.3) | async-done | bytes 262176 | tf_op jit(solution)/shard_map/all_to_all | solution.py:237
  153.3 0.7 fusion
  (27 shorter events, 0.1 us)
Async XLA Ops:
  0.0 10.1 %copy-start.14 = (s32[1,2]{1,0:T(1,128)S(1)}, s32[1,2]{1,0:T(1,128)}, u32[]{:S(2)}) copy-start(s32[1,2]{1,0:T(1,128)} %param.18) | copy-start | bytes 28
  3.0 27.1 %collective-permute-start = (f32[2056,128]{1,0:T(8,128)}, f32[2056,128]{1,0:T(8,128)S(1)}, u32[]{:S(2)}, u32[]{:S(2)}) collective-permute-start(f32[2056,128]{1,0:T(8,128)} %products.1.refs_0_), channel_id=1, source_target_pairs={{0,128},{1,385},{128,256},{129,1},{256,384},{257,129},{384,0},{385... | collective-permute-start | bytes 3158024 | tf_op jit(solution)/shard_map/ppermute | solution.py:154
  6.4 24.1 %collective-permute-start.1 = (f32[2056,128]{1,0:T(8,128)}, f32[2056,128]{1,0:T(8,128)S(1)}, u32[]{:S(2)}, u32[]{:S(2)}) collective-permute-start(f32[2056,128]{1,0:T(8,128)} %products.1.refs_0_), channel_id=1, source_target_pairs={{0,384},{1,129},{128,0},{129,257},{256,128},{257,385},{384,256},{3... | collective-permute-start | bytes 3158024 | tf_op jit(solution)/shard_map/ppermute | solution.py:154
  10.8 33.1 %all-to-all-start = ((s32[16,32,128]{2,1,0:T(8,128)}), s32[16,32,128]{2,1,0:T(8,128)S(1)}, u32[]{:S(2)}, u32[]{:S(2)}) async-start(s32[16,32,128]{2,1,0:T(8,128)} %broadcast_in_dim.2), calls=%async_computation | async-start | bytes 524288 | tf_op jit(solution)/shard_map/all_to_all | solution.py:215
  26.0 18.5 %copy-start = (f32[2056,128]{1,0:T(8,128)S(1)}, f32[2056,128]{1,0:T(8,128)}, u32[]{:S(2)}) copy-start(f32[2056,128]{1,0:T(8,128)} %products.1.refs_0_) | copy-start | bytes 3158020
  30.5 24.9 %collective-permute-start.2 = (f32[2056,128]{1,0:T(8,128)S(1)}, f32[2056,128]{1,0:T(8,128)}, u32[]{:S(2)}, u32[]{:S(2)}) collective-permute-start(f32[2056,128]{1,0:T(8,128)S(1)} %collective-permute-done.refs_1_), channel_id=1, source_target_pairs={{0,128},{1,385},{128,256},{129,1},{256,384},{257,129},{384,0},{385... | collective-permute-start | bytes 3158024 | tf_op jit(solution)/shard_map/ppermute | solution.py:154
  50.5 4.9 %copy-start.1 = (f32[4,128,128]{2,1,0:T(8,128)S(1)}, f32[4,128,128]{2,1,0:T(8,128)}, u32[]{:S(2)}) copy-start(f32[4,128,128]{2,1,0:T(8,128)} %get-tuple-element.47.refs_1_) | copy-start | bytes 786436
  50.5 4.9 %copy-start.2 = (f32[4,128,128]{2,1,0:T(8,128)S(1)}, f32[4,128,128]{2,1,0:T(8,128)}, u32[]{:S(2)}) copy-start(f32[4,128,128]{2,1,0:T(8,128)} %get-tuple-element.48.refs_2_) | copy-start | bytes 786436
  50.5 4.9 %copy-start.3 = (f32[4,128,128]{2,1,0:T(8,128)S(1)}, f32[4,128,128]{2,1,0:T(8,128)}, u32[]{:S(2)}) copy-start(f32[4,128,128]{2,1,0:T(8,128)} %get-tuple-element.49.refs_3_) | copy-start | bytes 786436
  50.5 4.9 %copy-start.4 = (f32[4,128,128]{2,1,0:T(8,128)S(1)}, f32[4,128,128]{2,1,0:T(8,128)}, u32[]{:S(2)}) copy-start(f32[4,128,128]{2,1,0:T(8,128)} %get-tuple-element.50.refs_4_) | copy-start | bytes 786436
  50.5 4.9 %copy-start.5 = (f32[4,128,128]{2,1,0:T(8,128)S(1)}, f32[4,128,128]{2,1,0:T(8,128)}, u32[]{:S(2)}) copy-start(f32[4,128,128]{2,1,0:T(8,128)} %get-tuple-element.51.refs_5_) | copy-start | bytes 786436
  50.5 4.9 %copy-start.6 = (f32[4,128,128]{2,1,0:T(8,128)S(1)}, f32[4,128,128]{2,1,0:T(8,128)}, u32[]{:S(2)}) copy-start(f32[4,128,128]{2,1,0:T(8,128)} %get-tuple-element.52.refs_6_) | copy-start | bytes 786436
  50.5 4.9 %copy-start.7 = (f32[4,128,128]{2,1,0:T(8,128)S(1)}, f32[4,128,128]{2,1,0:T(8,128)}, u32[]{:S(2)}) copy-start(f32[4,128,128]{2,1,0:T(8,128)} %get-tuple-element.53.refs_7_) | copy-start | bytes 786436
  50.5 4.9 %copy-start.8 = (f32[4,128,128]{2,1,0:T(8,128)S(1)}, f32[4,128,128]{2,1,0:T(8,128)}, u32[]{:S(2)}) copy-start(f32[4,128,128]{2,1,0:T(8,128)} %get-tuple-element.54.refs_8_) | copy-start | bytes 786436
  50.5 30.8 %all-to-all-start.1 = ((f32[8,256,128]{2,1,0:T(8,128)}), f32[8,256,128]{2,1,0:T(8,128)}, u32[]{:S(2)}, u32[]{:S(2)}) async-start(f32[8,256,128]{2,1,0:T(8,128)} %ladder.1), calls=%async_computation.1 | async-start | bytes 2097152 | tf_op jit(solution)/shard_map/all_to_all | solution.py:222
  60.7 29.2 %copy-start.13 = (f32[4,128,128]{2,1,0:T(8,128)S(1)}, f32[4,128,128]{2,1,0:T(8,128)}, u32[]{:S(2)}) copy-start(f32[4,128,128]{2,1,0:T(8,128)} %get-tuple-element.56) | copy-start | bytes 786436
  60.7 31.3 %copy-start.12 = (f32[4,128,128]{2,1,0:T(8,128)S(1)}, f32[4,128,128]{2,1,0:T(8,128)}, u32[]{:S(2)}) copy-start(f32[4,128,128]{2,1,0:T(8,128)} %get-tuple-element.57) | copy-start | bytes 786436
  60.7 34.2 %copy-start.11 = (f32[4,128,128]{2,1,0:T(8,128)S(1)}, f32[4,128,128]{2,1,0:T(8,128)}, u32[]{:S(2)}) copy-start(f32[4,128,128]{2,1,0:T(8,128)} %get-tuple-element.58) | copy-start | bytes 786436
  60.7 11.9 %collective-permute-start.7 = (f32[4,128,128]{2,1,0:T(8,128)}, f32[4,128,128]{2,1,0:T(8,128)S(1)}, u32[]{:S(2)}, u32[]{:S(2)}) collective-permute-start(f32[4,128,128]{2,1,0:T(8,128)} %get-tuple-element.61), channel_id=1, source_target_pairs={{0,16},{1,113},{8,24},{9,121},{16,32},{17,1},{24,40},{25,9},{32,48... | collective-permute-start | bytes 786440 | tf_op jit(solution)/shard_map/ppermute | solution.py:158
  65.6 14.0 %collective-permute-start.8 = (f32[4,128,128]{2,1,0:T(8,128)}, f32[4,128,128]{2,1,0:T(8,128)S(1)}, u32[]{:S(2)}, u32[]{:S(2)}) collective-permute-start(f32[4,128,128]{2,1,0:T(8,128)} %get-tuple-element.62), channel_id=1, source_target_pairs={{0,8},{1,121},{8,16},{9,1},{16,24},{17,9},{24,32},{25,17},{32,40},... | collective-permute-start | bytes 786440 | tf_op jit(solution)/shard_map/ppermute | solution.py:158
  68.5 11.1 %collective-permute-start.9 = (f32[4,128,128]{2,1,0:T(8,128)}, f32[4,128,128]{2,1,0:T(8,128)S(1)}, u32[]{:S(2)}, u32[]{:S(2)}) collective-permute-start(f32[4,128,128]{2,1,0:T(8,128)} %get-tuple-element.63), channel_id=1, source_target_pairs={{0,120},{1,9},{8,0},{9,17},{16,8},{17,25},{24,16},{25,33},{32,24},... | collective-permute-start | bytes 786440 | tf_op jit(solution)/shard_map/ppermute | solution.py:158
  81.3 44.0 %copy-start.9 = (f32[4,128,128]{2,1,0:T(8,128)S(1)}, f32[4,128,128]{2,1,0:T(8,128)}, u32[]{:S(2)}) copy-start(f32[4,128,128]{2,1,0:T(8,128)} %get-tuple-element.55) | copy-start | bytes 786436
  81.3 46.9 %all-to-all-start.2 = ((f32[4,128,128]{2,1,0:T(8,128)}), f32[4,128,128]{2,1,0:T(8,128)S(1)}, u32[]{:S(2)}, u32[]{:S(2)}) async-start(f32[4,128,128]{2,1,0:T(8,128)} %add_add_fusion), calls=%async_computation.2 | async-start | bytes 524288 | tf_op jit(solution)/shard_map/all_to_all | solution.py:237
  89.9 19.6 %collective-permute-start.3 = (f32[4,128,128]{2,1,0:T(8,128)S(1)}, f32[4,128,128]{2,1,0:T(8,128)S(1)}, u32[]{:S(2)}, u32[]{:S(2)}) collective-permute-start(f32[4,128,128]{2,1,0:T(8,128)S(1)} %copy-done.13), channel_id=1, source_target_pairs={{0,16},{1,113},{8,24},{9,121},{16,32},{17,1},{24,40},{25,9},{32,48... | collective-permute-start | bytes 786440 | tf_op jit(solution)/shard_map/ppermute | solution.py:158
  92.1 33.3 %collective-permute-start.4 = (f32[4,128,128]{2,1,0:T(8,128)S(1)}, f32[4,128,128]{2,1,0:T(8,128)S(1)}, u32[]{:S(2)}, u32[]{:S(2)}) collective-permute-start(f32[4,128,128]{2,1,0:T(8,128)S(1)} %copy-done.12), channel_id=1, source_target_pairs={{0,8},{1,121},{8,16},{9,1},{16,24},{17,9},{24,32},{25,17},{32,40},... | collective-permute-start | bytes 786440 | tf_op jit(solution)/shard_map/ppermute | solution.py:158
  94.9 30.4 %collective-permute-start.5 = (f32[4,128,128]{2,1,0:T(8,128)S(1)}, f32[4,128,128]{2,1,0:T(8,128)S(1)}, u32[]{:S(2)}, u32[]{:S(2)}) collective-permute-start(f32[4,128,128]{2,1,0:T(8,128)S(1)} %copy-done.11), channel_id=1, source_target_pairs={{0,120},{1,9},{8,0},{9,17},{16,8},{17,25},{24,16},{25,33},{32,24},... | collective-permute-start | bytes 786440 | tf_op jit(solution)/shard_map/ppermute | solution.py:158
  100.4 27.8 %collective-permute-start.6 = (f32[256,128]{1,0:T(8,128)S(1)}, f32[256,128]{1,0:T(8,128)S(1)}, u32[]{:S(2)}, u32[]{:S(2)}) collective-permute-start(f32[256,128]{1,0:T(8,128)S(1)} %reduce_sum.9), channel_id=1, source_target_pairs={{0,504},{8,496},{16,488},{24,480},{32,472},{40,464},{48,456},{56,4... | collective-permute-start | bytes 393224 | tf_op jit(solution)/shard_map/ppermute | solution.py:226
  126.1 27.2 %copy-start.10 = (f32[256,128]{1,0:T(8,128)S(1)}, f32[256,128]{1,0:T(8,128)}, u32[]{:S(2)}) copy-start(f32[256,128]{1,0:T(8,128)} %param.19) | copy-start | bytes 393220
  128.3 25.0 %all-to-all-start.3 = ((f32[4,128,128]{2,1,0:T(8,128)}), f32[4,128,128]{2,1,0:T(8,128)S(1)}, u32[]{:S(2)}, u32[]{:S(2)}) async-start(f32[4,128,128]{2,1,0:T(8,128)} %add_add_fusion.1), calls=%async_computation.3 | async-start | bytes 524288 | tf_op jit(solution)/shard_map/all_to_all | solution.py:237

commit v5 on v4

--- a/solution.py
+++ b/solution.py
@@ -91,7 +91,7 @@
 def gather_kernel(sources, more, slots, *refs):
     tiles = refs[:sources]
     refs = refs[sources:]
-    cells = [(near, s) for near in NEAR for s in range(OWN)]
+    cells = NEAR
     befores = refs[: len(cells)] if more else (None,) * len(cells)
     refs = refs[len(cells) :] if more else refs
     outs = refs[: len(cells)]
@@ -132,10 +132,10 @@
                 sums.append(acc)
             for s in range(OWN):
                 total = sums[0][s] + flipped(sums[1][s])
-                before = befores[j * OWN + s]
-                if before is not None:
-                    total = total + before[a]
-                outs[j * OWN + s][a] = total
+                rows = pl.ds(s * EDGE, EDGE)
+                if befores[j] is not None:
+                    total = total + befores[j][a, rows, :]
+                outs[j][a, rows, :] = total
             return carry
 
         lax.fori_loop(0, HIGH, dest, 0)
@@ -160,10 +160,10 @@
 
 def gather(slots, arrays, before=()):
     n = len(arrays)
-    cells = OWN * len(NEAR)
+    cells = len(NEAR)
     return pl.pallas_call(
         functools.partial(gather_kernel, n, len(before) > 0),
-        out_shape=[jax.ShapeDtypeStruct((HIGH, EDGE, EDGE), jnp.float32)] * cells,
+        out_shape=[jax.ShapeDtypeStruct((HIGH, OWN * EDGE, EDGE), jnp.float32)] * cells,
         in_specs=sm(1) + vm(n + len(before)),
         out_specs=vm(cells),
         scratch_shapes=[pltpu.SMEM((n, TABLE, EDGE), jnp.float32), pltpu.SemaphoreType.DMA((n,))],
@@ -209,36 +209,29 @@
         out_specs=pl.BlockSpec(memory_space=VMEM),
         name="ladder",
     )(ladder_mask, lam_ladder, ladder_ints)
-    own_slots = jnp.broadcast_to(partner_slot[0], (NZ, 32, OWN)) if 32 == 1 else jnp.broadcast_to(
-        jnp.pad(partner_slot, ((0, 0), (0, EDGE - OWN))), (NZ, 32, EDGE)
-    )
+    own_slots = jnp.pad(partner_slot, ((0, 0), (0, EDGE - OWN)))
+    own_slots = jnp.broadcast_to(own_slots, (NZ, 32, EDGE))
     slots = lax.all_to_all(own_slots, ("h", "l"), split_axis=0, concat_axis=0, tiled=True)
     slots = slots[:, 0, :OWN]
     got_a, got_b, partial = lax.optimization_barrier((got_a, got_b, partial))
     got_c = move_x(got_a, 1)
 
+    spread = lax.all_to_all(partial, ("y", "c"), split_axis=0, concat_axis=0, tiled=True)
     near = gather(slots, (payload, got_a, got_b))
-    near, partial = lax.optimization_barrier((near, partial))
-    spread = lax.all_to_all(partial, ("y", "c"), split_axis=0, concat_axis=0, tiled=True)
+    near, spread = lax.optimization_barrier((near, spread))
     ladder = jnp.sum(spread, axis=0)
     n_occ = NX * NZ
     mirror = [(i, n_occ - 1 - i) for i in range(n_occ)]
     other = lax.ppermute(ladder, ("x", "h", "l"), mirror)
-
+    near, ladder = lax.optimization_barrier((near, ladder))
     near = gather(slots, (got_c,), near)
-    halves_done = []
-    for s in range(OWN):
-        cells = near[s::OWN]
-        far = cells[3]
-        for j in range(3):
-            far = far + move_z(cells[j], NEAR[j])
-        if s == OWN - 1:
-            far, other = lax.optimization_barrier((far, other))
-        far = lax.all_to_all(far, "h", split_axis=0, concat_axis=0, tiled=True)
-        halves_done.append(far[0] + far[1] + far[2] + far[3])
+    near, other = lax.optimization_barrier((near, other))
+    moved = [move_z(near[j], NEAR[j]) for j in range(3)]
+    far = near[3] + moved[0] + moved[1] + moved[2]
+    far = lax.all_to_all(far, "h", split_axis=0, concat_axis=0, tiled=True)
     other = other.reshape(OWN, EDGE, EDGE)[partner_slot[0]][:, ::-1, ::-1]
     ladder = ladder + other.reshape(OWN * EDGE, EDGE)
-    return (ladder + jnp.concatenate(halves_done, axis=0)) / denom
+    return (ladder + far[0] + far[1] + far[2] + far[3]) / denom
 
 
 def solution(mesh):

time: 155 us -> 151 us (0.974)
  the two profiles are of different devices: /device:TPU:24 before, /device:TPU:6 now
where the time goes in v5:
time: 151 us; the launch traced here: 150 us
  waiting for transfers between devices  73.4 us (49%)
  starting transfers between devices  50.5 us (33%)
  Pallas kernels  18.1 us (12%)
  local copies, waits for them, and re-layouts  4.17 us (3%)
  other arithmetic  3.95 us (3%)
    all_to_all x1, waiting for transfers between devices, body(): far = lax.all_to_all(far, 'h', split_axis=0, concat_axis=0, tiled=True)  27.5 us
    ppermute x3, waiting for transfers between devices, move_z(): return lax.ppermute(array, ('h', 'l', 'c'), signed(NZ, distance))  20.3 us
    ppermute x3, starting transfers between devices, move_x(): return lax.ppermute(array, ('x', 'c'), signed(NX, distance))  15.2 us
    all_to_all x1, starting transfers between devices, body(): lax.all_to_all(own_slots, ('h', 'l'), split_axis=0, concat_axis=0, tiled=...  11.4 us
    pallas_call x2, Pallas kernels, gather(): pl.pallas_call(functools.partial(gather_kernel, n, len(before) > 0), out_...  11.1 us
    ppermute x3, starting transfers between devices, move_z(): return lax.ppermute(array, ('h', 'l', 'c'), signed(NZ, distance))  9.92 us
    all_to_all x1, waiting for transfers between devices, body(): lax.all_to_all(partial, ('y', 'c'), split_axis=0, concat_axis=0, tiled=True)  9.47 us
    ppermute x1, waiting for transfers between devices, body(): other = lax.ppermute(ladder, ('x', 'h', 'l'), mirror)  6.71 us
  transfers between devices with their start and end apart: 10, of which 7 were waited for; matrix products, arithmetic and copies ran while one was open for 2% of the time, Pallas kernels for 10%

profile of v5, /device:TPU:6, one launch (start us, length us, event | category | flops | bytes accessed | tf_op | source)
XLA Modules:
  0.0 150.3 jit_solution(985308081656521878)
XLA Ops:
  0.0 0.0 copy-start.6
  0.0 3.0 %products.1.refs_0_ = f32[2056,128]{1,0:T(8,128)} custom-call(s32[96]{0:T(128)} %bitcast.46, s32[96]{0:T(128)} %bitcast.47, s32[96]{0:T(128)} %bitcast.48, f32[4,128,256]{2,1,0:T(8,128)} %bitcast.41, f32[4,256,128]{2,1,0:T(8,128)} %bitcast.42), custom_call_target="tpu_custom_call" | custom-call | tf_op jit(solution)/shard_map/products/pallas_call | solution.py:195
  3.0 7.7 %collective-permute-start = (f32[2056,128]{1,0:T(8,128)}, f32[2056,128]{1,0:T(8,128)S(1)}, u32[]{:S(2)}, u32[]{:S(2)}) collective-permute-start(f32[2056,128]{1,0:T(8,128)} %products.1.refs_0_), channel_id=1, source_target_pairs={{0,128},{1,385},{128,256},{129,1},{256,384},{257,129},{384,0},{385... | collective-permute-start | bytes 3158024 | tf_op jit(solution)/shard_map/ppermute | solution.py:154
  10.8 1.9 %collective-permute-start.1 = (f32[2056,128]{1,0:T(8,128)}, f32[2056,128]{1,0:T(8,128)S(1)}, u32[]{:S(2)}, u32[]{:S(2)}) collective-permute-start(f32[2056,128]{1,0:T(8,128)} %products.1.refs_0_), channel_id=1, source_target_pairs={{0,384},{1,129},{128,0},{129,257},{256,128},{257,385},{384,256},{3... | collective-permute-start | bytes 3158024 | tf_op jit(solution)/shard_map/ppermute | solution.py:154
  12.7 0.0 copy-done.6
  12.7 0.7 broadcast_in_dim.2
  13.4 11.4 %all-to-all-start = ((s32[16,32,128]{2,1,0:T(8,128)}), s32[16,32,128]{2,1,0:T(8,128)S(1)}, u32[]{:S(2)}, u32[]{:S(2)}) async-start(s32[16,32,128]{2,1,0:T(8,128)} %broadcast_in_dim.2), calls=%async_computation | async-start | bytes 524288 | tf_op jit(solution)/shard_map/all_to_all | solution.py:214
  24.8 4.0 %ladder.1 = f32[8,256,128]{2,1,0:T(8,128)} custom-call(s32[2,4]{1,0:T(2,128)} %mask.1, f32[256,512]{1,0:T(8,128)} %lam_ref.1, f32[512,1024]{1,0:T(8,128)} %ints_ref.1), custom_call_target="tpu_custom_call" | custom-call | tf_op jit(solution)/shard_map/ladder/pallas_call | solution.py:205
  28.8 0.0 copy-start
  28.8 3.8 %collective-permute-done.refs_1_ = f32[2056,128]{1,0:T(8,128)S(1)} collective-permute-done((f32[2056,128]{1,0:T(8,128)}, f32[2056,128]{1,0:T(8,128)S(1)}, u32[]{:S(2)}, u32[]{:S(2)}) %collective-permute-start) | collective-permute-done | bytes 1052704 | tf_op jit(solution)/shard_map/ppermute | solution.py:154
  32.6 0.0 collective-permute-done.1.refs_2_
  32.6 5.5 %collective-permute-start.2 = (f32[2056,128]{1,0:T(8,128)S(1)}, f32[2056,128]{1,0:T(8,128)}, u32[]{:S(2)}, u32[]{:S(2)}) collective-permute-start(f32[2056,128]{1,0:T(8,128)S(1)} %collective-permute-done.refs_1_), channel_id=1, source_target_pairs={{0,128},{1,385},{128,256},{129,1},{256,384},{257,129},{384,0},{385... | collective-permute-start | bytes 3158024 | tf_op jit(solution)/shard_map/ppermute | solution.py:154
  38.1 5.6 %all-to-all-done = s32[16,32,128]{2,1,0:T(8,128)S(1)} async-done(((s32[16,32,128]{2,1,0:T(8,128)}), s32[16,32,128]{2,1,0:T(8,128)S(1)}, u32[]{:S(2)}, u32[]{:S(2)}) %all-to-all-start) | async-done | bytes 262176 | tf_op jit(solution)/shard_map/all_to_all | solution.py:214
  43.7 4.5 %all-to-all-start.1 = ((f32[8,256,128]{2,1,0:T(8,128)}), f32[8,256,128]{2,1,0:T(8,128)}, u32[]{:S(2)}, u32[]{:S(2)}) async-start(f32[8,256,128]{2,1,0:T(8,128)} %ladder.1), calls=%async_computation.1 | async-start | bytes 2097152 | tf_op jit(solution)/shard_map/all_to_all | solution.py:219
  48.1 0.6 slice.22
  48.8 0.0 copy-done
  48.8 6.0 %gather.7 = (f32[4,256,128]{2,1,0:T(8,128)}, f32[4,256,128]{2,1,0:T(8,128)}, f32[4,256,128]{2,1,0:T(8,128)}, f32[4,256,128]{2,1,0:T(8,128)}) custom-call(s32[16,2]{1,0:T(8,128)} %bitcast.44, f32[2056,128]{1,0:T(8,128)S(1)} %copy-done, f32[2056,128]{1,0:T(8,128)S(1)} %collective-permute-done.refs_1_, f32[2056,128]{1,0:T(8,128)S(1)} %collective-permute-done.1.refs_2_), custom_call_target="tpu_custom_call" | custom-call | tf_op jit(solution)/shard_map/gather/pallas_call | solution.py:164
  54.7 0.0 copy-start.1
  54.7 0.0 copy-start.2
  54.7 9.5 %all-to-all-done.1 = f32[8,256,128]{2,1,0:T(8,128)} async-done(((f32[8,256,128]{2,1,0:T(8,128)}), f32[8,256,128]{2,1,0:T(8,128)}, u32[]{:S(2)}, u32[]{:S(2)}) %all-to-all-start.1) | async-done | bytes 1048608 | tf_op jit(solution)/shard_map/all_to_all | solution.py:219
  64.2 1.3 reduce_sum.9
  65.5 4.7 %collective-permute-start.3 = (f32[256,128]{1,0:T(8,128)S(1)}, f32[256,128]{1,0:T(8,128)S(1)}, u32[]{:S(2)}, u32[]{:S(2)}) collective-permute-start(f32[256,128]{1,0:T(8,128)S(1)} %reduce_sum.9), channel_id=1, source_target_pairs={{0,504},{8,496},{16,488},{24,480},{32,472},{40,464},{48,456},{56,4... | collective-permute-start | bytes 393224 | tf_op jit(solution)/shard_map/ppermute | solution.py:225
  70.2 0.0 collective-permute-done.2.refs_0_
  70.2 0.0 copy-done.1
  70.2 0.0 copy-done.2
  70.2 0.0 copy-start.3
  70.2 1.0 copy-done.3
  71.3 0.0 copy-start.4
  71.3 1.0 copy-done.4
  72.3 5.2 %gather_more.1 = (f32[4,256,128]{2,1,0:T(8,128)}, f32[4,256,128]{2,1,0:T(8,128)}, f32[4,256,128]{2,1,0:T(8,128)}, f32[4,256,128]{2,1,0:T(8,128)}) custom-call(s32[16,2]{1,0:T(8,128)} %bitcast.45, f32[2056,128]{1,0:T(8,128)} %collective-permute-done.2.refs_0_, f32[4,256,128]{2,1,0:T(8,128)S(1)} %copy-done.1, f32[4,256,128]{2,1,0:T(8,128)S(1)} %copy-done.2, ...), custom_call_target="tpu_custom_call" | custom-call | tf_op jit(solution)/shard_map/gather_more/pallas_call | solution.py:164
  77.5 6.7 %collective-permute-done.3 = f32[256,128]{1,0:T(8,128)S(1)} collective-permute-done((f32[256,128]{1,0:T(8,128)S(1)}, f32[256,128]{1,0:T(8,128)S(1)}, u32[]{:S(2)}, u32[]{:S(2)}) %collective-permute-start.3) | collective-permute-done | bytes 131104 | tf_op jit(solution)/shard_map/ppermute | solution.py:225
  84.2 1.9 %collective-permute-start.4 = (f32[4,256,128]{2,1,0:T(8,128)}, f32[4,256,128]{2,1,0:T(8,128)S(1)}, u32[]{:S(2)}, u32[]{:S(2)}) collective-permute-start(f32[4,256,128]{2,1,0:T(8,128)} %get-tuple-element.54), channel_id=1, source_target_pairs={{0,16},{1,113},{8,24},{9,121},{16,32},{17,1},{24,40},{25,9},{32,48... | collective-permute-start | bytes 1572872 | tf_op jit(solution)/shard_map/ppermute | solution.py:158
  86.1 3.0 %collective-permute-start.5 = (f32[4,256,128]{2,1,0:T(8,128)}, f32[4,256,128]{2,1,0:T(8,128)S(1)}, u32[]{:S(2)}, u32[]{:S(2)}) collective-permute-start(f32[4,256,128]{2,1,0:T(8,128)} %get-tuple-element.55), channel_id=1, source_target_pairs={{0,8},{1,121},{8,16},{9,1},{16,24},{17,9},{24,32},{25,17},{32,40},... | collective-permute-start | bytes 1572872 | tf_op jit(solution)/shard_map/ppermute | solution.py:158
  89.1 5.0 %collective-permute-start.6 = (f32[4,256,128]{2,1,0:T(8,128)}, f32[4,256,128]{2,1,0:T(8,128)S(1)}, u32[]{:S(2)}, u32[]{:S(2)}) collective-permute-start(f32[4,256,128]{2,1,0:T(8,128)} %get-tuple-element.56), channel_id=1, source_target_pairs={{0,120},{1,9},{8,0},{9,17},{16,8},{17,25},{24,16},{25,33},{32,24},... | collective-permute-start | bytes 1572872 | tf_op jit(solution)/shard_map/ppermute | solution.py:158
  94.1 8.1 %collective-permute-done.4 = f32[4,256,128]{2,1,0:T(8,128)S(1)} collective-permute-done((f32[4,256,128]{2,1,0:T(8,128)}, f32[4,256,128]{2,1,0:T(8,128)S(1)}, u32[]{:S(2)}, u32[]{:S(2)}) %collective-permute-start.4) | collective-permute-done | bytes 524320 | tf_op jit(solution)/shard_map/ppermute | solution.py:158
  102.2 12.2 %collective-permute-done.5 = f32[4,256,128]{2,1,0:T(8,128)S(1)} collective-permute-done((f32[4,256,128]{2,1,0:T(8,128)}, f32[4,256,128]{2,1,0:T(8,128)S(1)}, u32[]{:S(2)}, u32[]{:S(2)}) %collective-permute-start.5) | collective-permute-done | bytes 524320 | tf_op jit(solution)/shard_map/ppermute | solution.py:158
  114.4 0.0 collective-permute-done.6
  114.4 1.9 %add_add_fusion = f32[4,256,128]{2,1,0:T(8,128)} fusion(f32[4,256,128]{2,1,0:T(8,128)S(1)} %collective-permute-done.6, f32[4,256,128]{2,1,0:T(8,128)S(1)} %collective-permute-done.5, f32[4,256,128]{2,1,0:T(8,128)} %get-tuple-element.53, f32[4,256,128]{2,1,0:T(8,128)S(1)} %collective-permute-done.4), kind=kLoop, calls=%fused_computation.1 | loop fusion | flops 393216 | bytes 2621440 | tf_op jit(solution)/shard_map/add | solution.py:230
  116.4 0.0 copy-start.5
  116.4 4.9 %all-to-all-start.2 = ((f32[4,256,128]{2,1,0:T(8,128)}), f32[4,256,128]{2,1,0:T(8,128)S(1)}, u32[]{:S(2)}, u32[]{:S(2)}) async-start(f32[4,256,128]{2,1,0:T(8,128)} %add_add_fusion), calls=%async_computation.2 | async-start | bytes 1048576 | tf_op jit(solution)/shard_map/all_to_all | solution.py:231
  121.3 0.6 gather_fusion
  121.9 0.2 rev.3
  122.1 27.5 %all-to-all-done.2 = f32[4,256,128]{2,1,0:T(8,128)S(1)} async-done(((f32[4,256,128]{2,1,0:T(8,128)}), f32[4,256,128]{2,1,0:T(8,128)S(1)}, u32[]{:S(2)}, u32[]{:S(2)}) %all-to-all-start.2) | async-done | bytes 524320 | tf_op jit(solution)/shard_map/all_to_all | solution.py:231
  149.6 0.0 copy-done.5
  149.6 0.7 fusion.1
  (3 shorter events, 0.0 us)
Async XLA Ops:
  0.0 12.7 %copy-start.6 = (s32[1,2]{1,0:T(1,128)S(1)}, s32[1,2]{1,0:T(1,128)}, u32[]{:S(2)}) copy-start(s32[1,2]{1,0:T(1,128)} %param.18) | copy-start | bytes 28
  3.0 29.6 %collective-permute-start = (f32[2056,128]{1,0:T(8,128)}, f32[2056,128]{1,0:T(8,128)S(1)}, u32[]{:S(2)}, u32[]{:S(2)}) collective-permute-start(f32[2056,128]{1,0:T(8,128)} %products.1.refs_0_), channel_id=1, source_target_pairs={{0,128},{1,385},{128,256},{129,1},{256,384},{257,129},{384,0},{385... | collective-permute-start | bytes 3158024 | tf_op jit(solution)/shard_map/ppermute | solution.py:154
  10.8 21.8 %collective-permute-start.1 = (f32[2056,128]{1,0:T(8,128)}, f32[2056,128]{1,0:T(8,128)S(1)}, u32[]{:S(2)}, u32[]{:S(2)}) collective-permute-start(f32[2056,128]{1,0:T(8,128)} %products.1.refs_0_), channel_id=1, source_target_pairs={{0,384},{1,129},{128,0},{129,257},{256,128},{257,385},{384,256},{3... | collective-permute-start | bytes 3158024 | tf_op jit(solution)/shard_map/ppermute | solution.py:154
  13.4 30.2 %all-to-all-start = ((s32[16,32,128]{2,1,0:T(8,128)}), s32[16,32,128]{2,1,0:T(8,128)S(1)}, u32[]{:S(2)}, u32[]{:S(2)}) async-start(s32[16,32,128]{2,1,0:T(8,128)} %broadcast_in_dim.2), calls=%async_computation | async-start | bytes 524288 | tf_op jit(solution)/shard_map/all_to_all | solution.py:214
  28.8 20.0 %copy-start = (f32[2056,128]{1,0:T(8,128)S(1)}, f32[2056,128]{1,0:T(8,128)}, u32[]{:S(2)}) copy-start(f32[2056,128]{1,0:T(8,128)} %products.1.refs_0_) | copy-start | bytes 3158020
  32.6 37.6 %collective-permute-start.2 = (f32[2056,128]{1,0:T(8,128)S(1)}, f32[2056,128]{1,0:T(8,128)}, u32[]{:S(2)}, u32[]{:S(2)}) collective-permute-start(f32[2056,128]{1,0:T(8,128)S(1)} %collective-permute-done.refs_1_), channel_id=1, source_target_pairs={{0,128},{1,385},{128,256},{129,1},{256,384},{257,129},{384,0},{385... | collective-permute-start | bytes 3158024 | tf_op jit(solution)/shard_map/ppermute | solution.py:154
  43.7 20.5 %all-to-all-start.1 = ((f32[8,256,128]{2,1,0:T(8,128)}), f32[8,256,128]{2,1,0:T(8,128)}, u32[]{:S(2)}, u32[]{:S(2)}) async-start(f32[8,256,128]{2,1,0:T(8,128)} %ladder.1), calls=%async_computation.1 | async-start | bytes 2097152 | tf_op jit(solution)/shard_map/all_to_all | solution.py:219
  54.7 15.5 %copy-start.1 = (f32[4,256,128]{2,1,0:T(8,128)S(1)}, f32[4,256,128]{2,1,0:T(8,128)}, u32[]{:S(2)}) copy-start(f32[4,256,128]{2,1,0:T(8,128)} %get-tuple-element.44.refs_1_) | copy-start | bytes 1572868
  54.7 15.5 %copy-start.2 = (f32[4,256,128]{2,1,0:T(8,128)S(1)}, f32[4,256,128]{2,1,0:T(8,128)}, u32[]{:S(2)}) copy-start(f32[4,256,128]{2,1,0:T(8,128)} %get-tuple-element.45.refs_2_) | copy-start | bytes 1572868
  65.5 18.7 %collective-permute-start.3 = (f32[256,128]{1,0:T(8,128)S(1)}, f32[256,128]{1,0:T(8,128)S(1)}, u32[]{:S(2)}, u32[]{:S(2)}) collective-permute-start(f32[256,128]{1,0:T(8,128)S(1)} %reduce_sum.9), channel_id=1, source_target_pairs={{0,504},{8,496},{16,488},{24,480},{32,472},{40,464},{48,456},{56,4... | collective-permute-start | bytes 393224 | tf_op jit(solution)/shard_map/ppermute | solution.py:225
  70.2 1.0 copy-start.3
  71.3 1.0 copy-start.4
  84.2 18.1 %collective-permute-start.4 = (f32[4,256,128]{2,1,0:T(8,128)}, f32[4,256,128]{2,1,0:T(8,128)S(1)}, u32[]{:S(2)}, u32[]{:S(2)}) collective-permute-start(f32[4,256,128]{2,1,0:T(8,128)} %get-tuple-element.54), channel_id=1, source_target_pairs={{0,16},{1,113},{8,24},{9,121},{16,32},{17,1},{24,40},{25,9},{32,48... | collective-permute-start | bytes 1572872 | tf_op jit(solution)/shard_map/ppermute | solution.py:158
  86.1 28.3 %collective-permute-start.5 = (f32[4,256,128]{2,1,0:T(8,128)}, f32[4,256,128]{2,1,0:T(8,128)S(1)}, u32[]{:S(2)}, u32[]{:S(2)}) collective-permute-start(f32[4,256,128]{2,1,0:T(8,128)} %get-tuple-element.55), channel_id=1, source_target_pairs={{0,8},{1,121},{8,16},{9,1},{16,24},{17,9},{24,32},{25,17},{32,40},... | collective-permute-start | bytes 1572872 | tf_op jit(solution)/shard_map/ppermute | solution.py:158
  89.1 25.3 %collective-permute-start.6 = (f32[4,256,128]{2,1,0:T(8,128)}, f32[4,256,128]{2,1,0:T(8,128)S(1)}, u32[]{:S(2)}, u32[]{:S(2)}) collective-permute-start(f32[4,256,128]{2,1,0:T(8,128)} %get-tuple-element.56), channel_id=1, source_target_pairs={{0,120},{1,9},{8,0},{9,17},{16,8},{17,25},{24,16},{25,33},{32,24},... | collective-permute-start | bytes 1572872 | tf_op jit(solution)/shard_map/ppermute | solution.py:158
  116.4 33.2 %copy-start.5 = (f32[256,128]{1,0:T(8,128)S(1)}, f32[256,128]{1,0:T(8,128)}, u32[]{:S(2)}) copy-start(f32[256,128]{1,0:T(8,128)} %param.19) | copy-start | bytes 393220
  116.4 33.2 %all-to-all-start.2 = ((f32[4,256,128]{2,1,0:T(8,128)}), f32[4,256,128]{2,1,0:T(8,128)S(1)}, u32[]{:S(2)}, u32[]{:S(2)}) async-start(f32[4,256,128]{2,1,0:T(8,128)} %add_add_fusion), calls=%async_computation.2 | async-start | bytes 1048576 | tf_op jit(solution)/shard_map/all_to_all | solution.py:231

commit v6 on v5

--- a/solution.py
+++ b/solution.py
@@ -108,10 +108,10 @@
     for copy in copies:
         copy.wait()
     for j, near in enumerate(NEAR):
-        low = jnp.bitwise_and(z + sign * near + NZ, LOW - 1)
-
-        def dest(a, carry, low=low, j=j):
-            target = a * LOW + low
+        via = jnp.bitwise_and(z + sign * near + NZ, NZ - 1)
+
+        def dest(a, carry, via=via, j=j):
+            target = jnp.bitwise_and(via + sign * LOW * a + NZ, NZ - 1)
             owner = base + target
             sums = []
             for flip in range(2):
@@ -216,19 +216,19 @@
     got_a, got_b, partial = lax.optimization_barrier((got_a, got_b, partial))
     got_c = move_x(got_a, 1)
 
+    near = gather(slots, (payload, got_a, got_b))
+    near, partial = lax.optimization_barrier((near, partial))
     spread = lax.all_to_all(partial, ("y", "c"), split_axis=0, concat_axis=0, tiled=True)
-    near = gather(slots, (payload, got_a, got_b))
-    near, spread = lax.optimization_barrier((near, spread))
     ladder = jnp.sum(spread, axis=0)
     n_occ = NX * NZ
     mirror = [(i, n_occ - 1 - i) for i in range(n_occ)]
     other = lax.ppermute(ladder, ("x", "h", "l"), mirror)
-    near, ladder = lax.optimization_barrier((near, ladder))
+
     near = gather(slots, (got_c,), near)
-    near, other = lax.optimization_barrier((near, other))
     moved = [move_z(near[j], NEAR[j]) for j in range(3)]
     far = near[3] + moved[0] + moved[1] + moved[2]
-    far = lax.all_to_all(far, "h", split_axis=0, concat_axis=0, tiled=True)
+    far, other = lax.optimization_barrier((far, other))
+    far = [far[0]] + [move_z(far[a], LOW * a) for a in (2, 1, 3)]
     other = other.reshape(OWN, EDGE, EDGE)[partner_slot[0]][:, ::-1, ::-1]
     ladder = ladder + other.reshape(OWN * EDGE, EDGE)
     return (ladder + far[0] + far[1] + far[2] + far[3]) / denom

time: 151 us -> 134 us (0.89)
  the two profiles are of different devices: /device:TPU:6 before, /device:TPU:47 now
where the time goes in v6:
time: 134 us
  starting transfers between devices  60.1 us (45%)
  waiting for transfers between devices  50.8 us (38%)
  Pallas kernels  18.3 us (14%)
  local copies, waits for them, and re-layouts  2.15 us (2%)
  other arithmetic  2.1 us (2%)
    ppermute x6, waiting for transfers between devices, move_z(): return lax.ppermute(array, ('h', 'l', 'c'), signed(NZ, distance))  37.7 us
    ppermute x6, starting transfers between devices, move_z(): return lax.ppermute(array, ('h', 'l', 'c'), signed(NZ, distance))  28.4 us
    all_to_all x1, starting transfers between devices, body(): lax.all_to_all(own_slots, ('h', 'l'), split_axis=0, concat_axis=0, tiled=...  14.7 us
    pallas_call x2, Pallas kernels, gather(): pl.pallas_call(functools.partial(gather_kernel, n, len(before) > 0), out_...  11.2 us
    all_to_all x1, waiting for transfers between devices, body(): lax.all_to_all(own_slots, ('h', 'l'), split_axis=0, concat_axis=0, tiled=...  9.02 us
    ppermute x3, starting transfers between devices, move_x(): return lax.ppermute(array, ('x', 'c'), signed(NX, distance))  8.92 us
    all_to_all x1, starting transfers between devices, body(): lax.all_to_all(partial, ('y', 'c'), split_axis=0, concat_axis=0, tiled=True)  5.95 us
    pallas_call x1, Pallas kernels, body(): pl.pallas_call(ladder_kernel, out_shape=jax.ShapeDtypeStruct((8, OWN * ED...  4.05 us
  transfers between devices with their start and end apart: 12, of which 8 were waited for; matrix products, arithmetic and copies ran while one was open for 3% of the time, Pallas kernels for 11%

profile of v6, /device:TPU:47, one launch (start us, length us, event | category | flops | bytes accessed | tf_op | source)
XLA Modules:
  0.0 133.7 jit_solution(11386944278987714466)
XLA Ops:
  0.0 3.0 %products.1.refs_0_ = f32[2056,128]{1,0:T(8,128)} custom-call(s32[96]{0:T(128)} %bitcast.38, s32[96]{0:T(128)} %bitcast.39, s32[96]{0:T(128)} %bitcast.40, f32[4,128,256]{2,1,0:T(8,128)} %bitcast.33, f32[4,256,128]{2,1,0:T(8,128)} %bitcast.34), custom_call_target="tpu_custom_call" | custom-call | tf_op jit(solution)/shard_map/products/pallas_call | solution.py:195
  3.0 2.4 %collective-permute-start = (f32[2056,128]{1,0:T(8,128)}, f32[2056,128]{1,0:T(8,128)S(1)}, u32[]{:S(2)}, u32[]{:S(2)}) collective-permute-start(f32[2056,128]{1,0:T(8,128)} %products.1.refs_0_), channel_id=1, source_target_pairs={{0,128},{1,385},{128,256},{129,1},{256,384},{257,129},{384,0},{385... | collective-permute-start | bytes 3158024 | tf_op jit(solution)/shard_map/ppermute | solution.py:154
  5.5 4.0 %collective-permute-start.1 = (f32[2056,128]{1,0:T(8,128)}, f32[2056,128]{1,0:T(8,128)S(1)}, u32[]{:S(2)}, u32[]{:S(2)}) collective-permute-start(f32[2056,128]{1,0:T(8,128)} %products.1.refs_0_), channel_id=1, source_target_pairs={{0,384},{1,129},{128,0},{129,257},{256,128},{257,385},{384,256},{3... | collective-permute-start | bytes 3158024 | tf_op jit(solution)/shard_map/ppermute | solution.py:154
  9.5 0.0 copy-done.7
  9.5 0.7 broadcast_in_dim.2
  10.3 14.7 %all-to-all-start = ((s32[16,32,128]{2,1,0:T(8,128)}), s32[16,32,128]{2,1,0:T(8,128)S(1)}, u32[]{:S(2)}, u32[]{:S(2)}) async-start(s32[16,32,128]{2,1,0:T(8,128)} %broadcast_in_dim.2), calls=%async_computation | async-start | bytes 524288 | tf_op jit(solution)/shard_map/all_to_all | solution.py:214
  24.9 4.0 %ladder.1 = f32[8,256,128]{2,1,0:T(8,128)} custom-call(s32[2,4]{1,0:T(2,128)} %mask.1, f32[256,512]{1,0:T(8,128)} %lam_ref.1, f32[512,1024]{1,0:T(8,128)} %ints_ref.1), custom_call_target="tpu_custom_call" | custom-call | tf_op jit(solution)/shard_map/ladder/pallas_call | solution.py:205
  29.0 0.0 collective-permute-done.refs_1_
  29.0 2.5 %collective-permute-done.1.refs_2_ = f32[2056,128]{1,0:T(8,128)S(1)} collective-permute-done((f32[2056,128]{1,0:T(8,128)}, f32[2056,128]{1,0:T(8,128)S(1)}, u32[]{:S(2)}, u32[]{:S(2)}) %collective-permute-start.1) | collective-permute-done | bytes 1052704 | tf_op jit(solution)/shard_map/ppermute | solution.py:154
  31.5 2.4 %collective-permute-start.2 = (f32[2056,128]{1,0:T(8,128)S(1)}, f32[2056,128]{1,0:T(8,128)}, u32[]{:S(2)}, u32[]{:S(2)}) collective-permute-start(f32[2056,128]{1,0:T(8,128)S(1)} %collective-permute-done.refs_1_), channel_id=1, source_target_pairs={{0,128},{1,385},{128,256},{129,1},{256,384},{257,129},{384,0},{385... | collective-permute-start | bytes 3158024 | tf_op jit(solution)/shard_map/ppermute | solution.py:154
  34.0 9.0 %all-to-all-done = s32[16,32,128]{2,1,0:T(8,128)S(1)} async-done(((s32[16,32,128]{2,1,0:T(8,128)}), s32[16,32,128]{2,1,0:T(8,128)S(1)}, u32[]{:S(2)}, u32[]{:S(2)}) %all-to-all-start) | async-done | bytes 262176 | tf_op jit(solution)/shard_map/all_to_all | solution.py:214
  43.0 0.6 slice.22
  43.6 0.0 copy-done
  43.6 6.0 %gather.7 = (f32[4,256,128]{2,1,0:T(8,128)}, f32[4,256,128]{2,1,0:T(8,128)}, f32[4,256,128]{2,1,0:T(8,128)}, f32[4,256,128]{2,1,0:T(8,128)}) custom-call(s32[16,2]{1,0:T(8,128)} %bitcast.36, f32[2056,128]{1,0:T(8,128)S(1)} %copy-done, f32[2056,128]{1,0:T(8,128)S(1)} %collective-permute-done.refs_1_, f32[2056,128]{1,0:T(8,128)S(1)} %collective-permute-done.1.refs_2_), custom_call_target="tpu_custom_call" | custom-call | tf_op jit(solution)/shard_map/gather/pallas_call | solution.py:164
  49.6 0.0 copy-start.1
  49.6 0.0 copy-start.2
  49.6 0.0 copy-start.3
  49.6 0.0 copy-start.4
  49.6 6.0 %all-to-all-start.1 = ((f32[8,256,128]{2,1,0:T(8,128)}), f32[8,256,128]{2,1,0:T(8,128)}, u32[]{:S(2)}, u32[]{:S(2)}) async-start(f32[8,256,128]{2,1,0:T(8,128)} %ladder.1), calls=%async_computation.1 | async-start | bytes 2097152 | tf_op jit(solution)/shard_map/all_to_all | solution.py:221
  55.6 0.0 collective-permute-done.2.refs_0_
  55.6 0.0 copy-done.1
  55.6 0.0 copy-done.2
  55.6 0.0 copy-done.3
  55.6 0.0 copy-done.4
  55.6 5.2 %gather_more.1 = (f32[4,256,128]{2,1,0:T(8,128)}, f32[4,256,128]{2,1,0:T(8,128)}, f32[4,256,128]{2,1,0:T(8,128)}, f32[4,256,128]{2,1,0:T(8,128)}) custom-call(s32[16,2]{1,0:T(8,128)} %bitcast.37, f32[2056,128]{1,0:T(8,128)} %collective-permute-done.2.refs_0_, f32[4,256,128]{2,1,0:T(8,128)S(1)} %copy-done.1, f32[4,256,128]{2,1,0:T(8,128)S(1)} %copy-done.2, ...), custom_call_target="tpu_custom_call" | custom-call | tf_op jit(solution)/shard_map/gather_more/pallas_call | solution.py:164
  60.8 0.0 copy-start.5
  60.8 5.6 %collective-permute-start.3 = (f32[4,256,128]{2,1,0:T(8,128)}, f32[4,256,128]{2,1,0:T(8,128)S(1)}, u32[]{:S(2)}, u32[]{:S(2)}) collective-permute-start(f32[4,256,128]{2,1,0:T(8,128)} %get-tuple-element.36), channel_id=1, source_target_pairs={{0,16},{1,113},{8,24},{9,121},{16,32},{17,1},{24,40},{25,9},{32,48... | collective-permute-start | bytes 1572872 | tf_op jit(solution)/shard_map/ppermute | solution.py:158
  66.5 1.9 %collective-permute-start.4 = (f32[4,256,128]{2,1,0:T(8,128)}, f32[4,256,128]{2,1,0:T(8,128)S(1)}, u32[]{:S(2)}, u32[]{:S(2)}) collective-permute-start(f32[4,256,128]{2,1,0:T(8,128)} %get-tuple-element.37), channel_id=1, source_target_pairs={{0,8},{1,121},{8,16},{9,1},{16,24},{17,9},{24,32},{25,17},{32,40},... | collective-permute-start | bytes 1572872 | tf_op jit(solution)/shard_map/ppermute | solution.py:158
  68.4 3.4 %collective-permute-start.5 = (f32[4,256,128]{2,1,0:T(8,128)}, f32[4,256,128]{2,1,0:T(8,128)S(1)}, u32[]{:S(2)}, u32[]{:S(2)}) collective-permute-start(f32[4,256,128]{2,1,0:T(8,128)} %get-tuple-element.38), channel_id=1, source_target_pairs={{0,120},{1,9},{8,0},{9,17},{16,8},{17,25},{24,16},{25,33},{32,24},... | collective-permute-start | bytes 1572872 | tf_op jit(solution)/shard_map/ppermute | solution.py:158
  71.8 0.0 all-to-all-done.1
  71.8 1.3 reduce_sum.9
  73.1 2.2 %collective-permute-start.6 = (f32[256,128]{1,0:T(8,128)S(1)}, f32[256,128]{1,0:T(8,128)S(1)}, u32[]{:S(2)}, u32[]{:S(2)}) collective-permute-start(f32[256,128]{1,0:T(8,128)S(1)} %reduce_sum.9), channel_id=1, source_target_pairs={{0,504},{8,496},{16,488},{24,480},{32,472},{40,464},{48,456},{56,4... | collective-permute-start | bytes 393224 | tf_op jit(solution)/shard_map/ppermute | solution.py:225
  75.3 4.6 %collective-permute-done.3 = f32[4,256,128]{2,1,0:T(8,128)S(1)} collective-permute-done((f32[4,256,128]{2,1,0:T(8,128)}, f32[4,256,128]{2,1,0:T(8,128)S(1)}, u32[]{:S(2)}, u32[]{:S(2)}) %collective-permute-start.3) | collective-permute-done | bytes 524320 | tf_op jit(solution)/shard_map/ppermute | solution.py:158
  79.9 14.2 %collective-permute-done.4 = f32[4,256,128]{2,1,0:T(8,128)S(1)} collective-permute-done((f32[4,256,128]{2,1,0:T(8,128)}, f32[4,256,128]{2,1,0:T(8,128)S(1)}, u32[]{:S(2)}, u32[]{:S(2)}) %collective-permute-start.4) | collective-permute-done | bytes 524320 | tf_op jit(solution)/shard_map/ppermute | solution.py:158
  94.1 0.0 collective-permute-done.5
  94.1 0.0 copy-done.5
  94.1 0.1 add_add_fusion
  94.2 0.0 copy-start.6
  94.3 1.6 %collective-permute-done.6 = f32[256,128]{1,0:T(8,128)S(1)} collective-permute-done((f32[256,128]{1,0:T(8,128)S(1)}, f32[256,128]{1,0:T(8,128)S(1)}, u32[]{:S(2)}, u32[]{:S(2)}) %collective-permute-start.6) | collective-permute-done | bytes 131104 | tf_op jit(solution)/shard_map/ppermute | solution.py:225
  95.8 8.3 %collective-permute-start.7 = (f32[256,128]{1,0:T(8,128)S(1)}, f32[256,128]{1,0:T(8,128)S(1)}, u32[]{:S(2)}, u32[]{:S(2)}) collective-permute-start(f32[256,128]{1,0:T(8,128)S(1)} %get-tuple-element.41), channel_id=1, source_target_pairs={{0,64},{1,65},{8,72},{9,73},{16,80},{17,81},{24,88},{25,89},{32,96... | collective-permute-start | bytes 393224 | tf_op jit(solution)/shard_map/ppermute | solution.py:158
  104.2 4.6 %collective-permute-start.8 = (f32[256,128]{1,0:T(8,128)S(1)}, f32[256,128]{1,0:T(8,128)S(1)}, u32[]{:S(2)}, u32[]{:S(2)}) collective-permute-start(f32[256,128]{1,0:T(8,128)S(1)} %get-tuple-element.43), channel_id=1, source_target_pairs={{0,32},{1,97},{8,40},{9,105},{16,48},{17,113},{24,56},{25,121},{32... | collective-permute-start | bytes 393224 | tf_op jit(solution)/shard_map/ppermute | solution.py:158
  108.7 4.6 %collective-permute-start.9 = (f32[256,128]{1,0:T(8,128)S(1)}, f32[256,128]{1,0:T(8,128)S(1)}, u32[]{:S(2)}, u32[]{:S(2)}) collective-permute-start(f32[256,128]{1,0:T(8,128)S(1)} %get-tuple-element.42), channel_id=1, source_target_pairs={{0,96},{1,33},{8,104},{9,41},{16,112},{17,49},{24,120},{25,57},{32... | collective-permute-start | bytes 393224 | tf_op jit(solution)/shard_map/ppermute | solution.py:158
  113.4 0.6 gather_fusion
  114.0 0.2 rev.3
  114.1 2.2 %collective-permute-done.7 = f32[256,128]{1,0:T(8,128)S(1)} collective-permute-done((f32[256,128]{1,0:T(8,128)S(1)}, f32[256,128]{1,0:T(8,128)S(1)}, u32[]{:S(2)}, u32[]{:S(2)}) %collective-permute-start.7) | collective-permute-done | bytes 131104 | tf_op jit(solution)/shard_map/ppermute | solution.py:158
  116.4 0.9 collective-permute-done.8
  117.2 15.8 %collective-permute-done.9 = f32[256,128]{1,0:T(8,128)S(1)} collective-permute-done((f32[256,128]{1,0:T(8,128)S(1)}, f32[256,128]{1,0:T(8,128)S(1)}, u32[]{:S(2)}, u32[]{:S(2)}) %collective-permute-start.9) | collective-permute-done | bytes 131104 | tf_op jit(solution)/shard_map/ppermute | solution.py:158
  133.0 0.7 fusion.3
  (7 shorter events, 0.0 us)
Async XLA Ops:
  0.0 9.5 %copy-start.7 = (s32[1,2]{1,0:T(1,128)S(1)}, s32[1,2]{1,0:T(1,128)}, u32[]{:S(2)}) copy-start(s32[1,2]{1,0:T(1,128)} %param.18) | copy-start | bytes 28
  3.0 26.0 %collective-permute-start = (f32[2056,128]{1,0:T(8,128)}, f32[2056,128]{1,0:T(8,128)S(1)}, u32[]{:S(2)}, u32[]{:S(2)}) collective-permute-start(f32[2056,128]{1,0:T(8,128)} %products.1.refs_0_), channel_id=1, source_target_pairs={{0,128},{1,385},{128,256},{129,1},{256,384},{257,129},{384,0},{385... | collective-permute-start | bytes 3158024 | tf_op jit(solution)/shard_map/ppermute | solution.py:154
  5.5 26.0 %collective-permute-start.1 = (f32[2056,128]{1,0:T(8,128)}, f32[2056,128]{1,0:T(8,128)S(1)}, u32[]{:S(2)}, u32[]{:S(2)}) collective-permute-start(f32[2056,128]{1,0:T(8,128)} %products.1.refs_0_), channel_id=1, source_target_pairs={{0,384},{1,129},{128,0},{129,257},{256,128},{257,385},{384,256},{3... | collective-permute-start | bytes 3158024 | tf_op jit(solution)/shard_map/ppermute | solution.py:154
  10.3 32.7 %all-to-all-start = ((s32[16,32,128]{2,1,0:T(8,128)}), s32[16,32,128]{2,1,0:T(8,128)S(1)}, u32[]{:S(2)}, u32[]{:S(2)}) async-start(s32[16,32,128]{2,1,0:T(8,128)} %broadcast_in_dim.2), calls=%async_computation | async-start | bytes 524288 | tf_op jit(solution)/shard_map/all_to_all | solution.py:214
  24.9 18.7 %copy-start = (f32[2056,128]{1,0:T(8,128)S(1)}, f32[2056,128]{1,0:T(8,128)}, u32[]{:S(2)}) copy-start(f32[2056,128]{1,0:T(8,128)} %products.1.refs_0_) | copy-start | bytes 3158020
  31.5 24.1 %collective-permute-start.2 = (f32[2056,128]{1,0:T(8,128)S(1)}, f32[2056,128]{1,0:T(8,128)}, u32[]{:S(2)}, u32[]{:S(2)}) collective-permute-start(f32[2056,128]{1,0:T(8,128)S(1)} %collective-permute-done.refs_1_), channel_id=1, source_target_pairs={{0,128},{1,385},{128,256},{129,1},{256,384},{257,129},{384,0},{385... | collective-permute-start | bytes 3158024 | tf_op jit(solution)/shard_map/ppermute | solution.py:154
  49.6 6.0 %copy-start.1 = (f32[4,256,128]{2,1,0:T(8,128)S(1)}, f32[4,256,128]{2,1,0:T(8,128)}, u32[]{:S(2)}) copy-start(f32[4,256,128]{2,1,0:T(8,128)} %get-tuple-element.31.refs_1_) | copy-start | bytes 1572868
  49.6 6.0 %copy-start.2 = (f32[4,256,128]{2,1,0:T(8,128)S(1)}, f32[4,256,128]{2,1,0:T(8,128)}, u32[]{:S(2)}) copy-start(f32[4,256,128]{2,1,0:T(8,128)} %get-tuple-element.32.refs_2_) | copy-start | bytes 1572868
  49.6 6.0 %copy-start.3 = (f32[4,256,128]{2,1,0:T(8,128)S(1)}, f32[4,256,128]{2,1,0:T(8,128)}, u32[]{:S(2)}) copy-start(f32[4,256,128]{2,1,0:T(8,128)} %get-tuple-element.33.refs_3_) | copy-start | bytes 1572868
  49.6 6.0 %copy-start.4 = (f32[4,256,128]{2,1,0:T(8,128)S(1)}, f32[4,256,128]{2,1,0:T(8,128)}, u32[]{:S(2)}) copy-start(f32[4,256,128]{2,1,0:T(8,128)} %get-tuple-element.34.refs_4_) | copy-start | bytes 1572868
  49.6 22.1 %all-to-all-start.1 = ((f32[8,256,128]{2,1,0:T(8,128)}), f32[8,256,128]{2,1,0:T(8,128)}, u32[]{:S(2)}, u32[]{:S(2)}) async-start(f32[8,256,128]{2,1,0:T(8,128)} %ladder.1), calls=%async_computation.1 | async-start | bytes 2097152 | tf_op jit(solution)/shard_map/all_to_all | solution.py:221
  60.8 33.3 %copy-start.5 = (f32[4,256,128]{2,1,0:T(8,128)S(1)}, f32[4,256,128]{2,1,0:T(8,128)}, u32[]{:S(2)}) copy-start(f32[4,256,128]{2,1,0:T(8,128)} %get-tuple-element.35) | copy-start | bytes 1572868
  60.8 19.1 %collective-permute-start.3 = (f32[4,256,128]{2,1,0:T(8,128)}, f32[4,256,128]{2,1,0:T(8,128)S(1)}, u32[]{:S(2)}, u32[]{:S(2)}) collective-permute-start(f32[4,256,128]{2,1,0:T(8,128)} %get-tuple-element.36), channel_id=1, source_target_pairs={{0,16},{1,113},{8,24},{9,121},{16,32},{17,1},{24,40},{25,9},{32,48... | collective-permute-start | bytes 1572872 | tf_op jit(solution)/shard_map/ppermute | solution.py:158
  66.5 27.7 %collective-permute-start.4 = (f32[4,256,128]{2,1,0:T(8,128)}, f32[4,256,128]{2,1,0:T(8,128)S(1)}, u32[]{:S(2)}, u32[]{:S(2)}) collective-permute-start(f32[4,256,128]{2,1,0:T(8,128)} %get-tuple-element.37), channel_id=1, source_target_pairs={{0,8},{1,121},{8,16},{9,1},{16,24},{17,9},{24,32},{25,17},{32,40},... | collective-permute-start | bytes 1572872 | tf_op jit(solution)/shard_map/ppermute | solution.py:158
  68.4 25.7 %collective-permute-start.5 = (f32[4,256,128]{2,1,0:T(8,128)}, f32[4,256,128]{2,1,0:T(8,128)S(1)}, u32[]{:S(2)}, u32[]{:S(2)}) collective-permute-start(f32[4,256,128]{2,1,0:T(8,128)} %get-tuple-element.38), channel_id=1, source_target_pairs={{0,120},{1,9},{8,0},{9,17},{16,8},{17,25},{24,16},{25,33},{32,24},... | collective-permute-start | bytes 1572872 | tf_op jit(solution)/shard_map/ppermute | solution.py:158
  73.1 22.7 %collective-permute-start.6 = (f32[256,128]{1,0:T(8,128)S(1)}, f32[256,128]{1,0:T(8,128)S(1)}, u32[]{:S(2)}, u32[]{:S(2)}) collective-permute-start(f32[256,128]{1,0:T(8,128)S(1)} %reduce_sum.9), channel_id=1, source_target_pairs={{0,504},{8,496},{16,488},{24,480},{32,472},{40,464},{48,456},{56,4... | collective-permute-start | bytes 393224 | tf_op jit(solution)/shard_map/ppermute | solution.py:225
  94.2 38.8 %copy-start.6 = (f32[256,128]{1,0:T(8,128)S(1)}, f32[256,128]{1,0:T(8,128)}, u32[]{:S(2)}) copy-start(f32[256,128]{1,0:T(8,128)} %param.19) | copy-start | bytes 393220
  95.8 20.5 %collective-permute-start.7 = (f32[256,128]{1,0:T(8,128)S(1)}, f32[256,128]{1,0:T(8,128)S(1)}, u32[]{:S(2)}, u32[]{:S(2)}) collective-permute-start(f32[256,128]{1,0:T(8,128)S(1)} %get-tuple-element.41), channel_id=1, source_target_pairs={{0,64},{1,65},{8,72},{9,73},{16,80},{17,81},{24,88},{25,89},{32,96... | collective-permute-start | bytes 393224 | tf_op jit(solution)/shard_map/ppermute | solution.py:158
  104.2 13.1 %collective-permute-start.8 = (f32[256,128]{1,0:T(8,128)S(1)}, f32[256,128]{1,0:T(8,128)S(1)}, u32[]{:S(2)}, u32[]{:S(2)}) collective-permute-start(f32[256,128]{1,0:T(8,128)S(1)} %get-tuple-element.43), channel_id=1, source_target_pairs={{0,32},{1,97},{8,40},{9,105},{16,48},{17,113},{24,56},{25,121},{32... | collective-permute-start | bytes 393224 | tf_op jit(solution)/shard_map/ppermute | solution.py:158
  108.7 24.3 %collective-permute-start.9 = (f32[256,128]{1,0:T(8,128)S(1)}, f32[256,128]{1,0:T(8,128)S(1)}, u32[]{:S(2)}, u32[]{:S(2)}) collective-permute-start(f32[256,128]{1,0:T(8,128)S(1)} %get-tuple-element.42), channel_id=1, source_target_pairs={{0,96},{1,33},{8,104},{9,41},{16,112},{17,49},{24,120},{25,57},{32... | collective-permute-start | bytes 393224 | tf_op jit(solution)/shard_map/ppermute | solution.py:158

commit v7 on v6

--- a/solution.py
+++ b/solution.py
@@ -138,7 +138,7 @@
                 outs[j][a, rows, :] = total
             return carry
 
-        lax.fori_loop(0, HIGH, dest, 0)
+        lax.fori_loop(0, HIGH, dest, 0, unroll=True)
 
 
 def signed(axis_size, distance):
@@ -210,7 +210,7 @@
         name="ladder",
     )(ladder_mask, lam_ladder, ladder_ints)
     own_slots = jnp.pad(partner_slot, ((0, 0), (0, EDGE - OWN)))
-    own_slots = jnp.broadcast_to(own_slots, (NZ, 32, EDGE))
+    own_slots = jnp.broadcast_to(own_slots, (NZ, 24, EDGE))
     slots = lax.all_to_all(own_slots, ("h", "l"), split_axis=0, concat_axis=0, tiled=True)
     slots = slots[:, 0, :OWN]
     got_a, got_b, partial = lax.optimization_barrier((got_a, got_b, partial))

time: 134 us -> 134 us (level)
  the two profiles are of different devices: /device:TPU:47 before, /device:TPU:41 now
where the time goes in v7:
time: 134 us; the launch traced here: 133 us
  starting transfers between devices  64 us (48%)
  waiting for transfers between devices  47.3 us (35%)
  Pallas kernels  17.5 us (13%)
  local copies, waits for them, and re-layouts  2.1 us (2%)
  other arithmetic  2.1 us (2%)
    ppermute x6, waiting for transfers between devices, move_z(): return lax.ppermute(array, ('h', 'l', 'c'), signed(NZ, distance))  34.6 us
    ppermute x6, starting transfers between devices, move_z(): return lax.ppermute(array, ('h', 'l', 'c'), signed(NZ, distance))  24.9 us
    all_to_all x1, starting transfers between devices, body(): lax.all_to_all(own_slots, ('h', 'l'), split_axis=0, concat_axis=0, tiled=...  14.7 us
    pallas_call x2, Pallas kernels, gather(): pl.pallas_call(functools.partial(gather_kernel, n, len(before) > 0), out_...  10.4 us
    ppermute x3, starting transfers between devices, move_x(): return lax.ppermute(array, ('x', 'c'), signed(NX, distance))  9.56 us
    all_to_all x1, starting transfers between devices, body(): lax.all_to_all(partial, ('y', 'c'), split_axis=0, concat_axis=0, tiled=True)  8.63 us
    ppermute x1, starting transfers between devices, body(): other = lax.ppermute(ladder, ('x', 'h', 'l'), mirror)  6.21 us
    ppermute x1, waiting for transfers between devices, body(): other = lax.ppermute(ladder, ('x', 'h', 'l'), mirror)  5.95 us
  transfers between devices with their start and end apart: 12, of which 7 were waited for; matrix products, arithmetic and copies ran while one was open for 3% of the time, Pallas kernels for 11%

profile of v7, /device:TPU:41, one launch (start us, length us, event | category | flops | bytes accessed | tf_op | source)
XLA Modules:
  0.0 133.2 jit_solution(14896191293505178316)
XLA Ops:
  0.0 3.0 %products.1.refs_0_ = f32[2056,128]{1,0:T(8,128)} custom-call(s32[96]{0:T(128)} %bitcast.38, s32[96]{0:T(128)} %bitcast.39, s32[96]{0:T(128)} %bitcast.40, f32[4,128,256]{2,1,0:T(8,128)} %bitcast.33, f32[4,256,128]{2,1,0:T(8,128)} %bitcast.34), custom_call_target="tpu_custom_call" | custom-call | tf_op jit(solution)/shard_map/products/pallas_call | solution.py:195
  3.0 4.4 %collective-permute-start = (f32[2056,128]{1,0:T(8,128)}, f32[2056,128]{1,0:T(8,128)S(1)}, u32[]{:S(2)}, u32[]{:S(2)}) collective-permute-start(f32[2056,128]{1,0:T(8,128)} %products.1.refs_0_), channel_id=1, source_target_pairs={{0,128},{1,385},{128,256},{129,1},{256,384},{257,129},{384,0},{385... | collective-permute-start | bytes 3158024 | tf_op jit(solution)/shard_map/ppermute | solution.py:154
  7.4 1.9 %collective-permute-start.1 = (f32[2056,128]{1,0:T(8,128)}, f32[2056,128]{1,0:T(8,128)S(1)}, u32[]{:S(2)}, u32[]{:S(2)}) collective-permute-start(f32[2056,128]{1,0:T(8,128)} %products.1.refs_0_), channel_id=1, source_target_pairs={{0,384},{1,129},{128,0},{129,257},{256,128},{257,385},{384,256},{3... | collective-permute-start | bytes 3158024 | tf_op jit(solution)/shard_map/ppermute | solution.py:154
  9.3 0.0 copy-done.7
  9.4 0.7 broadcast_in_dim.2
  10.0 14.7 %all-to-all-start = ((s32[16,24,128]{2,1,0:T(8,128)}), s32[16,24,128]{2,1,0:T(8,128)S(1)}, u32[]{:S(2)}, u32[]{:S(2)}) async-start(s32[16,24,128]{2,1,0:T(8,128)} %broadcast_in_dim.2), calls=%async_computation | async-start | bytes 393216 | tf_op jit(solution)/shard_map/all_to_all | solution.py:214
  24.7 4.1 %ladder.1 = f32[8,256,128]{2,1,0:T(8,128)} custom-call(s32[2,4]{1,0:T(2,128)} %mask.1, f32[256,512]{1,0:T(8,128)} %lam_ref.1, f32[512,1024]{1,0:T(8,128)} %ints_ref.1), custom_call_target="tpu_custom_call" | custom-call | tf_op jit(solution)/shard_map/ladder/pallas_call | solution.py:205
  28.8 0.0 collective-permute-done.refs_1_
  28.8 3.9 %collective-permute-done.1.refs_2_ = f32[2056,128]{1,0:T(8,128)S(1)} collective-permute-done((f32[2056,128]{1,0:T(8,128)}, f32[2056,128]{1,0:T(8,128)S(1)}, u32[]{:S(2)}, u32[]{:S(2)}) %collective-permute-start.1) | collective-permute-done | bytes 1052704 | tf_op jit(solution)/shard_map/ppermute | solution.py:154
  32.6 3.3 %collective-permute-start.2 = (f32[2056,128]{1,0:T(8,128)S(1)}, f32[2056,128]{1,0:T(8,128)}, u32[]{:S(2)}, u32[]{:S(2)}) collective-permute-start(f32[2056,128]{1,0:T(8,128)S(1)} %collective-permute-done.refs_1_), channel_id=1, source_target_pairs={{0,128},{1,385},{128,256},{129,1},{256,384},{257,129},{384,0},{385... | collective-permute-start | bytes 3158024 | tf_op jit(solution)/shard_map/ppermute | solution.py:154
  35.9 2.8 %all-to-all-done = s32[16,24,128]{2,1,0:T(8,128)S(1)} async-done(((s32[16,24,128]{2,1,0:T(8,128)}), s32[16,24,128]{2,1,0:T(8,128)S(1)}, u32[]{:S(2)}, u32[]{:S(2)}) %all-to-all-start) | async-done | bytes 196640 | tf_op jit(solution)/shard_map/all_to_all | solution.py:214
  38.7 0.6 slice.22
  39.4 0.0 copy-done
  39.4 6.2 %gather.7 = (f32[4,256,128]{2,1,0:T(8,128)}, f32[4,256,128]{2,1,0:T(8,128)}, f32[4,256,128]{2,1,0:T(8,128)}, f32[4,256,128]{2,1,0:T(8,128)}) custom-call(s32[16,2]{1,0:T(8,128)} %bitcast.36, f32[2056,128]{1,0:T(8,128)S(1)} %copy-done, f32[2056,128]{1,0:T(8,128)S(1)} %collective-permute-done.refs_1_, f32[2056,128]{1,0:T(8,128)S(1)} %collective-permute-done.1.refs_2_), custom_call_target="tpu_custom_call" | custom-call | tf_op jit(solution)/shard_map/gather/pallas_call | solution.py:164
  45.6 0.0 copy-start.1
  45.6 0.0 copy-start.2
  45.6 0.0 copy-start.3
  45.6 0.0 copy-start.4
  45.6 8.6 %all-to-all-start.1 = ((f32[8,256,128]{2,1,0:T(8,128)}), f32[8,256,128]{2,1,0:T(8,128)}, u32[]{:S(2)}, u32[]{:S(2)}) async-start(f32[8,256,128]{2,1,0:T(8,128)} %ladder.1), calls=%async_computation.1 | async-start | bytes 2097152 | tf_op jit(solution)/shard_map/all_to_all | solution.py:221
  54.3 0.0 collective-permute-done.2.refs_0_
  54.3 0.0 copy-done.1
  54.3 0.0 copy-done.2
  54.3 0.0 copy-done.3
  54.3 0.0 copy-done.4
  54.3 4.2 %gather_more.1 = (f32[4,256,128]{2,1,0:T(8,128)}, f32[4,256,128]{2,1,0:T(8,128)}, f32[4,256,128]{2,1,0:T(8,128)}, f32[4,256,128]{2,1,0:T(8,128)}) custom-call(s32[16,2]{1,0:T(8,128)} %bitcast.37, f32[2056,128]{1,0:T(8,128)} %collective-permute-done.2.refs_0_, f32[4,256,128]{2,1,0:T(8,128)S(1)} %copy-done.1, f32[4,256,128]{2,1,0:T(8,128)S(1)} %copy-done.2, ...), custom_call_target="tpu_custom_call" | custom-call | tf_op jit(solution)/shard_map/gather_more/pallas_call | solution.py:164
  58.5 0.0 copy-start.5
  58.5 4.9 %collective-permute-start.3 = (f32[4,256,128]{2,1,0:T(8,128)}, f32[4,256,128]{2,1,0:T(8,128)S(1)}, u32[]{:S(2)}, u32[]{:S(2)}) collective-permute-start(f32[4,256,128]{2,1,0:T(8,128)} %get-tuple-element.36), channel_id=1, source_target_pairs={{0,16},{1,113},{8,24},{9,121},{16,32},{17,1},{24,40},{25,9},{32,48... | collective-permute-start | bytes 1572872 | tf_op jit(solution)/shard_map/ppermute | solution.py:158
  63.4 2.9 %collective-permute-start.4 = (f32[4,256,128]{2,1,0:T(8,128)}, f32[4,256,128]{2,1,0:T(8,128)S(1)}, u32[]{:S(2)}, u32[]{:S(2)}) collective-permute-start(f32[4,256,128]{2,1,0:T(8,128)} %get-tuple-element.37), channel_id=1, source_target_pairs={{0,8},{1,121},{8,16},{9,1},{16,24},{17,9},{24,32},{25,17},{32,40},... | collective-permute-start | bytes 1572872 | tf_op jit(solution)/shard_map/ppermute | solution.py:158
  66.4 2.4 %collective-permute-start.5 = (f32[4,256,128]{2,1,0:T(8,128)}, f32[4,256,128]{2,1,0:T(8,128)S(1)}, u32[]{:S(2)}, u32[]{:S(2)}) collective-permute-start(f32[4,256,128]{2,1,0:T(8,128)} %get-tuple-element.38), channel_id=1, source_target_pairs={{0,120},{1,9},{8,0},{9,17},{16,8},{17,25},{24,16},{25,33},{32,24},... | collective-permute-start | bytes 1572872 | tf_op jit(solution)/shard_map/ppermute | solution.py:158
  68.7 0.0 all-to-all-done.1
  68.7 1.3 reduce_sum.9
  70.0 6.2 %collective-permute-start.6 = (f32[256,128]{1,0:T(8,128)S(1)}, f32[256,128]{1,0:T(8,128)S(1)}, u32[]{:S(2)}, u32[]{:S(2)}) collective-permute-start(f32[256,128]{1,0:T(8,128)S(1)} %reduce_sum.9), channel_id=1, source_target_pairs={{0,504},{8,496},{16,488},{24,480},{32,472},{40,464},{48,456},{56,4... | collective-permute-start | bytes 393224 | tf_op jit(solution)/shard_map/ppermute | solution.py:225
  76.2 0.7 collective-permute-done.3
  77.0 15.3 %collective-permute-done.4 = f32[4,256,128]{2,1,0:T(8,128)S(1)} collective-permute-done((f32[4,256,128]{2,1,0:T(8,128)}, f32[4,256,128]{2,1,0:T(8,128)S(1)}, u32[]{:S(2)}, u32[]{:S(2)}) %collective-permute-start.4) | collective-permute-done | bytes 524320 | tf_op jit(solution)/shard_map/ppermute | solution.py:158
  92.2 0.0 collective-permute-done.5
  92.2 0.0 copy-done.5
  92.3 0.1 add_add_fusion
  92.4 0.0 copy-start.6
  92.4 5.9 %collective-permute-done.6 = f32[256,128]{1,0:T(8,128)S(1)} collective-permute-done((f32[256,128]{1,0:T(8,128)S(1)}, f32[256,128]{1,0:T(8,128)S(1)}, u32[]{:S(2)}, u32[]{:S(2)}) %collective-permute-start.6) | collective-permute-done | bytes 131104 | tf_op jit(solution)/shard_map/ppermute | solution.py:225
  98.3 5.5 %collective-permute-start.7 = (f32[256,128]{1,0:T(8,128)S(1)}, f32[256,128]{1,0:T(8,128)S(1)}, u32[]{:S(2)}, u32[]{:S(2)}) collective-permute-start(f32[256,128]{1,0:T(8,128)S(1)} %get-tuple-element.41), channel_id=1, source_target_pairs={{0,64},{1,65},{8,72},{9,73},{16,80},{17,81},{24,88},{25,89},{32,96... | collective-permute-start | bytes 393224 | tf_op jit(solution)/shard_map/ppermute | solution.py:158
  103.9 5.8 %collective-permute-start.8 = (f32[256,128]{1,0:T(8,128)S(1)}, f32[256,128]{1,0:T(8,128)S(1)}, u32[]{:S(2)}, u32[]{:S(2)}) collective-permute-start(f32[256,128]{1,0:T(8,128)S(1)} %get-tuple-element.43), channel_id=1, source_target_pairs={{0,32},{1,97},{8,40},{9,105},{16,48},{17,113},{24,56},{25,121},{32... | collective-permute-start | bytes 393224 | tf_op jit(solution)/shard_map/ppermute | solution.py:158
  109.7 3.4 %collective-permute-start.9 = (f32[256,128]{1,0:T(8,128)S(1)}, f32[256,128]{1,0:T(8,128)S(1)}, u32[]{:S(2)}, u32[]{:S(2)}) collective-permute-start(f32[256,128]{1,0:T(8,128)S(1)} %get-tuple-element.42), channel_id=1, source_target_pairs={{0,96},{1,33},{8,104},{9,41},{16,112},{17,49},{24,120},{25,57},{32... | collective-permute-start | bytes 393224 | tf_op jit(solution)/shard_map/ppermute | solution.py:158
  113.1 0.6 gather_fusion
  113.7 0.2 rev.3
  113.9 5.2 %collective-permute-done.7 = f32[256,128]{1,0:T(8,128)S(1)} collective-permute-done((f32[256,128]{1,0:T(8,128)S(1)}, f32[256,128]{1,0:T(8,128)S(1)}, u32[]{:S(2)}, u32[]{:S(2)}) %collective-permute-start.7) | collective-permute-done | bytes 131104 | tf_op jit(solution)/shard_map/ppermute | solution.py:158
  119.0 0.0 collective-permute-done.8
  119.0 13.4 %collective-permute-done.9 = f32[256,128]{1,0:T(8,128)S(1)} collective-permute-done((f32[256,128]{1,0:T(8,128)S(1)}, f32[256,128]{1,0:T(8,128)S(1)}, u32[]{:S(2)}, u32[]{:S(2)}) %collective-permute-start.9) | collective-permute-done | bytes 131104 | tf_op jit(solution)/shard_map/ppermute | solution.py:158
  132.5 0.7 fusion.3
  (7 shorter events, 0.0 us)
Async XLA Ops:
  0.0 9.3 %copy-start.7 = (s32[1,2]{1,0:T(1,128)S(1)}, s32[1,2]{1,0:T(1,128)}, u32[]{:S(2)}) copy-start(s32[1,2]{1,0:T(1,128)} %param.18) | copy-start | bytes 28
  3.0 25.7 %collective-permute-start = (f32[2056,128]{1,0:T(8,128)}, f32[2056,128]{1,0:T(8,128)S(1)}, u32[]{:S(2)}, u32[]{:S(2)}) collective-permute-start(f32[2056,128]{1,0:T(8,128)} %products.1.refs_0_), channel_id=1, source_target_pairs={{0,128},{1,385},{128,256},{129,1},{256,384},{257,129},{384,0},{385... | collective-permute-start | bytes 3158024 | tf_op jit(solution)/shard_map/ppermute | solution.py:154
  7.4 25.2 %collective-permute-start.1 = (f32[2056,128]{1,0:T(8,128)}, f32[2056,128]{1,0:T(8,128)S(1)}, u32[]{:S(2)}, u32[]{:S(2)}) collective-permute-start(f32[2056,128]{1,0:T(8,128)} %products.1.refs_0_), channel_id=1, source_target_pairs={{0,384},{1,129},{128,0},{129,257},{256,128},{257,385},{384,256},{3... | collective-permute-start | bytes 3158024 | tf_op jit(solution)/shard_map/ppermute | solution.py:154
  10.0 28.7 %all-to-all-start = ((s32[16,24,128]{2,1,0:T(8,128)}), s32[16,24,128]{2,1,0:T(8,128)S(1)}, u32[]{:S(2)}, u32[]{:S(2)}) async-start(s32[16,24,128]{2,1,0:T(8,128)} %broadcast_in_dim.2), calls=%async_computation | async-start | bytes 393216 | tf_op jit(solution)/shard_map/all_to_all | solution.py:214
  24.7 14.7 %copy-start = (f32[2056,128]{1,0:T(8,128)S(1)}, f32[2056,128]{1,0:T(8,128)}, u32[]{:S(2)}) copy-start(f32[2056,128]{1,0:T(8,128)} %products.1.refs_0_) | copy-start | bytes 3158020
  32.6 21.6 %collective-permute-start.2 = (f32[2056,128]{1,0:T(8,128)S(1)}, f32[2056,128]{1,0:T(8,128)}, u32[]{:S(2)}, u32[]{:S(2)}) collective-permute-start(f32[2056,128]{1,0:T(8,128)S(1)} %collective-permute-done.refs_1_), channel_id=1, source_target_pairs={{0,128},{1,385},{128,256},{129,1},{256,384},{257,129},{384,0},{385... | collective-permute-start | bytes 3158024 | tf_op jit(solution)/shard_map/ppermute | solution.py:154
  45.6 8.7 %copy-start.1 = (f32[4,256,128]{2,1,0:T(8,128)S(1)}, f32[4,256,128]{2,1,0:T(8,128)}, u32[]{:S(2)}) copy-start(f32[4,256,128]{2,1,0:T(8,128)} %get-tuple-element.31.refs_1_) | copy-start | bytes 1572868
  45.6 8.7 %copy-start.2 = (f32[4,256,128]{2,1,0:T(8,128)S(1)}, f32[4,256,128]{2,1,0:T(8,128)}, u32[]{:S(2)}) copy-start(f32[4,256,128]{2,1,0:T(8,128)} %get-tuple-element.32.refs_2_) | copy-start | bytes 1572868
  45.6 8.7 %copy-start.3 = (f32[4,256,128]{2,1,0:T(8,128)S(1)}, f32[4,256,128]{2,1,0:T(8,128)}, u32[]{:S(2)}) copy-start(f32[4,256,128]{2,1,0:T(8,128)} %get-tuple-element.33.refs_3_) | copy-start | bytes 1572868
  45.6 8.7 %copy-start.4 = (f32[4,256,128]{2,1,0:T(8,128)S(1)}, f32[4,256,128]{2,1,0:T(8,128)}, u32[]{:S(2)}) copy-start(f32[4,256,128]{2,1,0:T(8,128)} %get-tuple-element.34.refs_4_) | copy-start | bytes 1572868
  45.6 23.1 %all-to-all-start.1 = ((f32[8,256,128]{2,1,0:T(8,128)}), f32[8,256,128]{2,1,0:T(8,128)}, u32[]{:S(2)}, u32[]{:S(2)}) async-start(f32[8,256,128]{2,1,0:T(8,128)} %ladder.1), calls=%async_computation.1 | async-start | bytes 2097152 | tf_op jit(solution)/shard_map/all_to_all | solution.py:221
  58.5 33.8 %copy-start.5 = (f32[4,256,128]{2,1,0:T(8,128)S(1)}, f32[4,256,128]{2,1,0:T(8,128)}, u32[]{:S(2)}) copy-start(f32[4,256,128]{2,1,0:T(8,128)} %get-tuple-element.35) | copy-start | bytes 1572868
  58.5 18.5 %collective-permute-start.3 = (f32[4,256,128]{2,1,0:T(8,128)}, f32[4,256,128]{2,1,0:T(8,128)S(1)}, u32[]{:S(2)}, u32[]{:S(2)}) collective-permute-start(f32[4,256,128]{2,1,0:T(8,128)} %get-tuple-element.36), channel_id=1, source_target_pairs={{0,16},{1,113},{8,24},{9,121},{16,32},{17,1},{24,40},{25,9},{32,48... | collective-permute-start | bytes 1572872 | tf_op jit(solution)/shard_map/ppermute | solution.py:158
  63.4 28.8 %collective-permute-start.4 = (f32[4,256,128]{2,1,0:T(8,128)}, f32[4,256,128]{2,1,0:T(8,128)S(1)}, u32[]{:S(2)}, u32[]{:S(2)}) collective-permute-start(f32[4,256,128]{2,1,0:T(8,128)} %get-tuple-element.37), channel_id=1, source_target_pairs={{0,8},{1,121},{8,16},{9,1},{16,24},{17,9},{24,32},{25,17},{32,40},... | collective-permute-start | bytes 1572872 | tf_op jit(solution)/shard_map/ppermute | solution.py:158
  66.4 25.9 %collective-permute-start.5 = (f32[4,256,128]{2,1,0:T(8,128)}, f32[4,256,128]{2,1,0:T(8,128)S(1)}, u32[]{:S(2)}, u32[]{:S(2)}) collective-permute-start(f32[4,256,128]{2,1,0:T(8,128)} %get-tuple-element.38), channel_id=1, source_target_pairs={{0,120},{1,9},{8,0},{9,17},{16,8},{17,25},{24,16},{25,33},{32,24},... | collective-permute-start | bytes 1572872 | tf_op jit(solution)/shard_map/ppermute | solution.py:158
  70.0 28.3 %collective-permute-start.6 = (f32[256,128]{1,0:T(8,128)S(1)}, f32[256,128]{1,0:T(8,128)S(1)}, u32[]{:S(2)}, u32[]{:S(2)}) collective-permute-start(f32[256,128]{1,0:T(8,128)S(1)} %reduce_sum.9), channel_id=1, source_target_pairs={{0,504},{8,496},{16,488},{24,480},{32,472},{40,464},{48,456},{56,4... | collective-permute-start | bytes 393224 | tf_op jit(solution)/shard_map/ppermute | solution.py:225
  92.4 40.1 %copy-start.6 = (f32[256,128]{1,0:T(8,128)S(1)}, f32[256,128]{1,0:T(8,128)}, u32[]{:S(2)}) copy-start(f32[256,128]{1,0:T(8,128)} %param.19) | copy-start | bytes 393220
  98.3 20.7 %collective-permute-start.7 = (f32[256,128]{1,0:T(8,128)S(1)}, f32[256,128]{1,0:T(8,128)S(1)}, u32[]{:S(2)}, u32[]{:S(2)}) collective-permute-start(f32[256,128]{1,0:T(8,128)S(1)} %get-tuple-element.41), channel_id=1, source_target_pairs={{0,64},{1,65},{8,72},{9,73},{16,80},{17,81},{24,88},{25,89},{32,96... | collective-permute-start | bytes 393224 | tf_op jit(solution)/shard_map/ppermute | solution.py:158
  103.9 15.1 %collective-permute-start.8 = (f32[256,128]{1,0:T(8,128)S(1)}, f32[256,128]{1,0:T(8,128)S(1)}, u32[]{:S(2)}, u32[]{:S(2)}) collective-permute-start(f32[256,128]{1,0:T(8,128)S(1)} %get-tuple-element.43), channel_id=1, source_target_pairs={{0,32},{1,97},{8,40},{9,105},{16,48},{17,113},{24,56},{25,121},{32... | collective-permute-start | bytes 393224 | tf_op jit(solution)/shard_map/ppermute | solution.py:158
  109.7 22.7 %collective-permute-start.9 = (f32[256,128]{1,0:T(8,128)S(1)}, f32[256,128]{1,0:T(8,128)S(1)}, u32[]{:S(2)}, u32[]{:S(2)}) collective-permute-start(f32[256,128]{1,0:T(8,128)S(1)} %get-tuple-element.42), channel_id=1, source_target_pairs={{0,96},{1,33},{8,104},{9,41},{16,112},{17,49},{24,120},{25,57},{32... | collective-permute-start | bytes 393224 | tf_op jit(solution)/shard_map/ppermute | solution.py:158

commit v8 on v7

--- a/solution.py
+++ b/solution.py
@@ -13,6 +13,7 @@
 OWN = 2
 XT = 4
 NX = 4
+N_VIR = 8
 NZ = 16
 TASKS = 96
 ENTRIES = NX * NZ * CAP
@@ -62,8 +63,15 @@
             out_ref[pl.ds((l * XT + r) * EDGE, EDGE), :] = tile[:, r * EDGE : (r + 1) * EDGE]
 
 
-def ladder_kernel(mask, lam_ref, ints_ref, out_ref):
+def ladder_kernel(mask, behind, ahead, lam_ref, ints_ref, out_ref):
     blocks = lam_ref.shape[1] // EDGE
+    lane = lax.broadcasted_iota(jnp.int32, (TABLE, EDGE), 1)
+    extra = jnp.zeros((TABLE, EDGE), jnp.int32)
+    for s in range(OWN):
+        extra = jnp.where(lane == s, behind[0, s], extra)
+        extra = jnp.where(lane == OWN + s, ahead[0, s], extra)
+    for q in range(out_ref.shape[0]):
+        out_ref[q, pl.ds(OWN * EDGE, TABLE), :] = extra.astype(jnp.float32)
     for s in range(OWN):
         rows = [
             lam_ref[pl.ds(s * EDGE, EDGE), pl.ds(b * EDGE, EDGE)]
@@ -88,7 +96,7 @@
     return jnp.concatenate(parts, axis=0)
 
 
-def gather_kernel(sources, more, slots, *refs):
+def gather_kernel(sources, more, mine, others, *refs):
     tiles = refs[:sources]
     refs = refs[sources:]
     cells = NEAR
@@ -113,6 +121,14 @@
         def dest(a, carry, via=via, j=j):
             target = jnp.bitwise_and(via + sign * LOW * a + NZ, NZ - 1)
             owner = base + target
+            step = jnp.bitwise_and(target - z + NZ, NZ - 1)
+            near_ahead = step <= N_VIR
+            row = jnp.where(near_ahead, jnp.maximum(step - 1, 0), NZ - 1 - step)
+            first = jnp.where(near_ahead, OWN, 0)
+            slots = [
+                jnp.where(step == 0, mine[0, s], others[row, first + s].astype(jnp.int32))
+                for s in range(OWN)
+            ]
             sums = []
             for flip in range(2):
                 start = (NX * NZ - 1 - owner if flip else owner) * CAP
@@ -120,14 +136,14 @@
                 for i, tile in enumerate(tiles):
                     for k in range(CAP):
                         at = start + k
-                        row = lax.shift_right_logical(at, 7)
+                        line = lax.shift_right_logical(at, 7)
                         lane = jnp.bitwise_and(at, EDGE - 1)
-                        entry = tables[i, row, lane].astype(jnp.int32)
+                        entry = tables[i, line, lane].astype(jnp.int32)
                         slot = lax.shift_right_arithmetic(entry, 4)
                         code = jnp.bitwise_and(jnp.maximum(entry, 0), PAIRS - 1)
                         val = tile[pl.ds(pl.multiple_of(code * EDGE, EDGE), EDGE), :]
                         for s in range(OWN):
-                            want = slots[target, s] if flip else s
+                            want = slots[s] if flip else s
                             acc[s] = acc[s] + val * (slot == want).astype(jnp.float32)
                 sums.append(acc)
             for s in range(OWN):
@@ -158,17 +174,25 @@
     return lax.ppermute(array, ("h", "l", "c"), signed(NZ, distance))
 
 
-def gather(slots, arrays, before=()):
+def gather(mine, others, arrays, before=()):
     n = len(arrays)
     cells = len(NEAR)
     return pl.pallas_call(
         functools.partial(gather_kernel, n, len(before) > 0),
         out_shape=[jax.ShapeDtypeStruct((HIGH, OWN * EDGE, EDGE), jnp.float32)] * cells,
-        in_specs=sm(1) + vm(n + len(before)),
+        in_specs=sm(2) + vm(n + len(before)),
         out_specs=vm(cells),
         scratch_shapes=[pltpu.SMEM((n, TABLE, EDGE), jnp.float32), pltpu.SemaphoreType.DMA((n,))],
         name="gather_more" if before else "gather",
-    )(slots, *[pltpu.with_memory_space_constraint(a, VMEM) for a in (*arrays, *before)])
+    )(mine, others, *[pltpu.with_memory_space_constraint(a, VMEM) for a in (*arrays, *before)])
+
+
+def fetch(array, sign):
+    pairs = []
+    for i in range(NZ):
+        for v in range(N_VIR):
+            pairs.append((i * N_VIR + v, (i + sign * (v + 1)) % NZ * N_VIR + v))
+    return lax.ppermute(array, ("h", "l", "y", "c"), pairs)
 
 
 def vm(n):
@@ -202,32 +226,32 @@
     )(cycle_left[0, 0], cycle_right[0, 0], cycle_dest[0, 0], t2_tiles[0, 0], cycle_ints[0, 0])
     got_a = move_x(payload, 1)
     got_b = move_x(payload, -1)
+    row, payload = lax.optimization_barrier((partner_slot, payload))
+    behind = fetch(row, 1)
+    ahead = fetch(row, -1)
     partial = pl.pallas_call(
         ladder_kernel,
-        out_shape=jax.ShapeDtypeStruct((8, OWN * EDGE, EDGE), f32),
-        in_specs=sm(1) + vm(2),
+        out_shape=jax.ShapeDtypeStruct((N_VIR, OWN * EDGE + TABLE, EDGE), f32),
+        in_specs=sm(3) + vm(2),
         out_specs=pl.BlockSpec(memory_space=VMEM),
         name="ladder",
-    )(ladder_mask, lam_ladder, ladder_ints)
-    own_slots = jnp.pad(partner_slot, ((0, 0), (0, EDGE - OWN)))
-    own_slots = jnp.broadcast_to(own_slots, (NZ, 24, EDGE))
-    slots = lax.all_to_all(own_slots, ("h", "l"), split_axis=0, concat_axis=0, tiled=True)
-    slots = slots[:, 0, :OWN]
+    )(ladder_mask, behind, ahead, lam_ladder, ladder_ints)
+    spread = lax.all_to_all(partial, ("y", "c"), split_axis=0, concat_axis=0, tiled=True)
     got_a, got_b, partial = lax.optimization_barrier((got_a, got_b, partial))
     got_c = move_x(got_a, 1)
 
-    near = gather(slots, (payload, got_a, got_b))
-    near, partial = lax.optimization_barrier((near, partial))
-    spread = lax.all_to_all(partial, ("y", "c"), split_axis=0, concat_axis=0, tiled=True)
-    ladder = jnp.sum(spread, axis=0)
+    others = spread[:, OWN * EDGE, :]
+    ladder = jnp.sum(spread[:, : OWN * EDGE], axis=0)
+    got_b, ladder = lax.optimization_barrier((got_b, ladder))
     n_occ = NX * NZ
     mirror = [(i, n_occ - 1 - i) for i in range(n_occ)]
     other = lax.ppermute(ladder, ("x", "h", "l"), mirror)
 
-    near = gather(slots, (got_c,), near)
+    near = gather(partner_slot, others, (payload, got_a, got_b))
+    near = gather(partner_slot, others, (got_c,), near)
+    near, other = lax.optimization_barrier((near, other))
     moved = [move_z(near[j], NEAR[j]) for j in range(3)]
     far = near[3] + moved[0] + moved[1] + moved[2]
-    far, other = lax.optimization_barrier((far, other))
     far = [far[0]] + [move_z(far[a], LOW * a) for a in (2, 1, 3)]
     other = other.reshape(OWN, EDGE, EDGE)[partner_slot[0]][:, ::-1, ::-1]
     ladder = ladder + other.reshape(OWN * EDGE, EDGE)

time: 134 us -> 154 us (1.15)
  the two profiles are of different devices: /device:TPU:41 before, /device:TPU:1 now
where the time goes in v8:
time: 154 us; the launch traced here: 153 us
  starting transfers between devices  75.9 us (49%)
  waiting for transfers between devices  49 us (32%)
  Pallas kernels  17.3 us (11%)
  local copies, waits for them, and re-layouts  6.88 us (4%)
  other arithmetic  3.17 us (2%)
    ppermute x6, waiting for transfers between devices, move_z(): return lax.ppermute(array, ('h', 'l', 'c'), signed(NZ, distance))  37.5 us
    ppermute x6, starting transfers between devices, move_z(): return lax.ppermute(array, ('h', 'l', 'c'), signed(NZ, distance))  27.9 us
    all_to_all x1, starting transfers between devices, body(): lax.all_to_all(partial, ('y', 'c'), split_axis=0, concat_axis=0, tiled=True)  18.6 us
    ppermute x2, starting transfers between devices, fetch(): return lax.ppermute(array, ('h', 'l', 'y', 'c'), pairs)  13.5 us
    ppermute x3, starting transfers between devices, move_x(): return lax.ppermute(array, ('x', 'c'), signed(NX, distance))  11.8 us
    all_to_all x1, waiting for transfers between devices, body(): lax.all_to_all(partial, ('y', 'c'), split_axis=0, concat_axis=0, tiled=True)  10.8 us
    pallas_call x2, Pallas kernels, gather(): pl.pallas_call(functools.partial(gather_kernel, n, len(before) > 0), out_...  10.3 us
    unnamed x20, local copies, waits for them, and re-layouts  4.76 us
  transfers between devices with their start and end apart: 13, of which 6 were waited for; matrix products, arithmetic and copies ran while one was open for 2% of the time, Pallas kernels for 9%

profile of v8, /device:TPU:1, one launch (start us, length us, event | category | flops | bytes accessed | tf_op | source)
XLA Modules:
  0.0 152.6 jit_solution(7087471969970573610)
XLA Ops:
  0.0 3.0 %products.1.refs_0_ = f32[2056,128]{1,0:T(8,128)} custom-call(s32[96]{0:T(128)} %bitcast.40, s32[96]{0:T(128)} %bitcast.41, s32[96]{0:T(128)} %bitcast.42, f32[4,128,256]{2,1,0:T(8,128)} %bitcast.35, f32[4,256,128]{2,1,0:T(8,128)} %bitcast.36), custom_call_target="tpu_custom_call" | custom-call | tf_op jit(solution)/shard_map/products/pallas_call | solution.py:219
  3.0 5.2 %collective-permute-start = (f32[2056,128]{1,0:T(8,128)}, f32[2056,128]{1,0:T(8,128)S(1)}, u32[]{:S(2)}, u32[]{:S(2)}) collective-permute-start(f32[2056,128]{1,0:T(8,128)} %products.1.refs_0_), channel_id=1, source_target_pairs={{0,128},{1,385},{128,256},{129,1},{256,384},{257,129},{384,0},{385... | collective-permute-start | bytes 3158024 | tf_op jit(solution)/shard_map/ppermute | solution.py:170
  8.2 1.9 %collective-permute-start.1 = (f32[2056,128]{1,0:T(8,128)}, f32[2056,128]{1,0:T(8,128)S(1)}, u32[]{:S(2)}, u32[]{:S(2)}) collective-permute-start(f32[2056,128]{1,0:T(8,128)} %products.1.refs_0_), channel_id=1, source_target_pairs={{0,384},{1,129},{128,0},{129,257},{256,128},{257,385},{384,256},{3... | collective-permute-start | bytes 3158024 | tf_op jit(solution)/shard_map/ppermute | solution.py:170
  10.1 0.0 copy-done.6
  10.1 4.9 %collective-permute-start.2 = (s32[1,2]{1,0:T(1,128)S(1)}, s32[1,2]{1,0:T(1,128)S(1)}, u32[]{:S(2)}, u32[]{:S(2)}) collective-permute-start(s32[1,2]{1,0:T(1,128)S(1)} %copy-done.6), channel_id=1, source_target_pairs={{0,8},{1,17},{2,26},{3,35},{4,44},{5,53},{6,62},{7,71},{8,16},{9,2... | collective-permute-start | bytes 32 | tf_op jit(solution)/shard_map/ppermute | solution.py:195
  15.1 8.6 %collective-permute-start.3 = (s32[1,2]{1,0:T(1,128)S(1)}, s32[1,2]{1,0:T(1,128)S(1)}, u32[]{:S(2)}, u32[]{:S(2)}) collective-permute-start(s32[1,2]{1,0:T(1,128)S(1)} %copy-done.6), channel_id=1, source_target_pairs={{0,120},{1,113},{2,106},{3,99},{4,92},{5,85},{6,78},{7,71},{8,0},{... | collective-permute-start | bytes 32 | tf_op jit(solution)/shard_map/ppermute | solution.py:195
  23.6 0.0 collective-permute-done.2.behind
  23.7 0.0 copy-start.8
  23.7 0.7 collective-permute-done.3.ahead
  24.3 0.0 copy-done.8
  24.4 0.6 copy-done.9
  24.9 4.0 %ladder.1 = f32[8,264,128]{2,1,0:T(8,128)} custom-call(s32[2,4]{1,0:T(2,128)} %mask.1, s32[1,2]{1,0:T(1,128)} %copy-done.8, s32[1,2]{1,0:T(1,128)} %copy-done.9, f32[256,512]{1,0:T(8,128)} %lam_ref.1, f32[512,1024]{1,0:T(8,128)} %ints_ref.1), custom_call_target="tpu_custom_call" | custom-call | tf_op jit(solution)/shard_map/ladder/pallas_call | solution.py:232
  28.9 18.6 %all-to-all-start = ((f32[8,264,128]{2,1,0:T(8,128)}), f32[8,264,128]{2,1,0:T(8,128)}, u32[]{:S(2)}, u32[]{:S(2)}) async-start(f32[8,264,128]{2,1,0:T(8,128)} %ladder.1), calls=%async_computation | async-start | bytes 2162688 | tf_op jit(solution)/shard_map/all_to_all | solution.py:239
  47.6 0.0 collective-permute-done.refs_1_
  47.6 0.0 collective-permute-done.1.refs_2_
  47.6 4.7 %collective-permute-start.4 = (f32[2056,128]{1,0:T(8,128)S(1)}, f32[2056,128]{1,0:T(8,128)}, u32[]{:S(2)}, u32[]{:S(2)}) collective-permute-start(f32[2056,128]{1,0:T(8,128)S(1)} %collective-permute-done.refs_1_), channel_id=1, source_target_pairs={{0,128},{1,385},{128,256},{129,1},{256,384},{257,129},{384,0},{385... | collective-permute-start | bytes 3158024 | tf_op jit(solution)/shard_map/ppermute | solution.py:170
  52.3 10.8 %all-to-all-done = f32[8,264,128]{2,1,0:T(8,128)} async-done(((f32[8,264,128]{2,1,0:T(8,128)}), f32[8,264,128]{2,1,0:T(8,128)}, u32[]{:S(2)}, u32[]{:S(2)}) %all-to-all-start) | async-done | bytes 1081376 | tf_op jit(solution)/shard_map/all_to_all | solution.py:239
  63.1 1.3 slice_reduce_fusion
  64.4 4.1 %collective-permute-start.5 = (f32[256,128]{1,0:T(8,128)S(1)}, f32[256,128]{1,0:T(8,128)S(1)}, u32[]{:S(2)}, u32[]{:S(2)}) collective-permute-start(f32[256,128]{1,0:T(8,128)S(1)} %slice_reduce_fusion), channel_id=1, source_target_pairs={{0,504},{8,496},{16,488},{24,480},{32,472},{40,464},{48,456},{56,4... | collective-permute-start | bytes 393224 | tf_op jit(solution)/shard_map/ppermute | solution.py:248
  68.6 1.4 slice.27
  69.9 0.0 copy-done
  69.9 6.1 %gather.7 = (f32[4,256,128]{2,1,0:T(8,128)}, f32[4,256,128]{2,1,0:T(8,128)}, f32[4,256,128]{2,1,0:T(8,128)}, f32[4,256,128]{2,1,0:T(8,128)}) custom-call(s32[1,2]{1,0:T(1,128)} %mine.3, f32[8,128]{1,0:T(8,128)} %bitcast.38, f32[2056,128]{1,0:T(8,128)S(1)} %copy-done, f32[2056,128]{1,0:T(8,128)S(1)} %collective-permute-done.refs_1_, ...), custom_call_target="tpu_custom_call" | custom-call | tf_op jit(solution)/shard_map/gather/pallas_call | solution.py:180
  76.0 0.0 collective-permute-done.4.refs_0_
  76.0 0.0 copy-start.1
  76.0 1.0 copy-done.1
  77.1 1.0 copy-done.2
  78.1 1.0 copy-done.3
  79.2 1.0 copy-done.4
  80.2 4.2 %gather_more.1 = (f32[4,256,128]{2,1,0:T(8,128)}, f32[4,256,128]{2,1,0:T(8,128)}, f32[4,256,128]{2,1,0:T(8,128)}, f32[4,256,128]{2,1,0:T(8,128)}) custom-call(s32[1,2]{1,0:T(1,128)} %mine.3, f32[8,128]{1,0:T(8,128)} %bitcast.39, f32[2056,128]{1,0:T(8,128)} %collective-permute-done.4.refs_0_, f32[4,256,128]{2,1,0:T(8,128)S(1)} %copy-done.1, ...), custom_call_target="tpu_custom_call" | custom-call | tf_op jit(solution)/shard_map/gather_more/pallas_call | solution.py:180
  84.4 0.0 collective-permute-done.5
  84.4 0.0 copy-start.7
  84.4 6.1 %collective-permute-start.6 = (f32[4,256,128]{2,1,0:T(8,128)}, f32[4,256,128]{2,1,0:T(8,128)S(1)}, u32[]{:S(2)}, u32[]{:S(2)}) collective-permute-start(f32[4,256,128]{2,1,0:T(8,128)} %get-tuple-element.40), channel_id=1, source_target_pairs={{0,16},{1,113},{8,24},{9,121},{16,32},{17,1},{24,40},{25,9},{32,48... | collective-permute-start | bytes 1572872 | tf_op jit(solution)/shard_map/ppermute | solution.py:174
  90.6 3.5 %collective-permute-start.7 = (f32[4,256,128]{2,1,0:T(8,128)}, f32[4,256,128]{2,1,0:T(8,128)S(1)}, u32[]{:S(2)}, u32[]{:S(2)}) collective-permute-start(f32[4,256,128]{2,1,0:T(8,128)} %get-tuple-element.41), channel_id=1, source_target_pairs={{0,8},{1,121},{8,16},{9,1},{16,24},{17,9},{24,32},{25,17},{32,40},... | collective-permute-start | bytes 1572872 | tf_op jit(solution)/shard_map/ppermute | solution.py:174
  94.1 1.9 %collective-permute-start.8 = (f32[4,256,128]{2,1,0:T(8,128)}, f32[4,256,128]{2,1,0:T(8,128)S(1)}, u32[]{:S(2)}, u32[]{:S(2)}) collective-permute-start(f32[4,256,128]{2,1,0:T(8,128)} %get-tuple-element.42), channel_id=1, source_target_pairs={{0,120},{1,9},{8,0},{9,17},{16,8},{17,25},{24,16},{25,33},{32,24},... | collective-permute-start | bytes 1572872 | tf_op jit(solution)/shard_map/ppermute | solution.py:174
  96.0 8.7 %collective-permute-done.6 = f32[4,256,128]{2,1,0:T(8,128)S(1)} collective-permute-done((f32[4,256,128]{2,1,0:T(8,128)}, f32[4,256,128]{2,1,0:T(8,128)S(1)}, u32[]{:S(2)}, u32[]{:S(2)}) %collective-permute-start.6) | collective-permute-done | bytes 524320 | tf_op jit(solution)/shard_map/ppermute | solution.py:174
  104.8 9.0 %collective-permute-done.7 = f32[4,256,128]{2,1,0:T(8,128)S(1)} collective-permute-done((f32[4,256,128]{2,1,0:T(8,128)}, f32[4,256,128]{2,1,0:T(8,128)S(1)}, u32[]{:S(2)}, u32[]{:S(2)}) %collective-permute-start.7) | collective-permute-done | bytes 524320 | tf_op jit(solution)/shard_map/ppermute | solution.py:174
  113.8 0.0 collective-permute-done.8
  113.8 1.2 add_add_fusion
  115.0 0.0 copy-start.5
  115.0 7.3 %collective-permute-start.10 = (f32[256,128]{1,0:T(8,128)S(1)}, f32[256,128]{1,0:T(8,128)S(1)}, u32[]{:S(2)}, u32[]{:S(2)}) collective-permute-start(f32[256,128]{1,0:T(8,128)S(1)} %get-tuple-element.45), channel_id=1, source_target_pairs={{0,32},{1,97},{8,40},{9,105},{16,48},{17,113},{24,56},{25,121},{32... | collective-permute-start | bytes 393224 | tf_op jit(solution)/shard_map/ppermute | solution.py:174
  122.4 2.0 %collective-permute-start.11 = (f32[256,128]{1,0:T(8,128)S(1)}, f32[256,128]{1,0:T(8,128)S(1)}, u32[]{:S(2)}, u32[]{:S(2)}) collective-permute-start(f32[256,128]{1,0:T(8,128)S(1)} %get-tuple-element.44), channel_id=1, source_target_pairs={{0,96},{1,33},{8,104},{9,41},{16,112},{17,49},{24,120},{25,57},{32... | collective-permute-start | bytes 393224 | tf_op jit(solution)/shard_map/ppermute | solution.py:174
  124.3 6.9 %collective-permute-start.9 = (f32[256,128]{1,0:T(8,128)S(1)}, f32[256,128]{1,0:T(8,128)S(1)}, u32[]{:S(2)}, u32[]{:S(2)}) collective-permute-start(f32[256,128]{1,0:T(8,128)S(1)} %get-tuple-element.43), channel_id=1, source_target_pairs={{0,64},{1,65},{8,72},{9,73},{16,80},{17,81},{24,88},{25,89},{32,96... | collective-permute-start | bytes 393224 | tf_op jit(solution)/shard_map/ppermute | solution.py:174
  131.3 0.6 gather_fusion
  131.9 0.2 rev.3
  132.1 0.0 collective-permute-done.10
  132.1 5.6 %collective-permute-done.11 = f32[256,128]{1,0:T(8,128)S(1)} collective-permute-done((f32[256,128]{1,0:T(8,128)S(1)}, f32[256,128]{1,0:T(8,128)S(1)}, u32[]{:S(2)}, u32[]{:S(2)}) %collective-permute-start.11) | collective-permute-done | bytes 131104 | tf_op jit(solution)/shard_map/ppermute | solution.py:174
  137.7 14.1 %collective-permute-done.9 = f32[256,128]{1,0:T(8,128)S(1)} collective-permute-done((f32[256,128]{1,0:T(8,128)S(1)}, f32[256,128]{1,0:T(8,128)S(1)}, u32[]{:S(2)}, u32[]{:S(2)}) %collective-permute-start.9) | collective-permute-done | bytes 131104 | tf_op jit(solution)/shard_map/ppermute | solution.py:174
  151.9 0.7 fusion.4
  (11 shorter events, 0.1 us)
Async XLA Ops:
  0.0 10.1 %copy-start.6 = (s32[1,2]{1,0:T(1,128)S(1)}, s32[1,2]{1,0:T(1,128)}, u32[]{:S(2)}) copy-start(s32[1,2]{1,0:T(1,128)} %mine.3) | copy-start | bytes 28
  3.0 44.6 %collective-permute-start = (f32[2056,128]{1,0:T(8,128)}, f32[2056,128]{1,0:T(8,128)S(1)}, u32[]{:S(2)}, u32[]{:S(2)}) collective-permute-start(f32[2056,128]{1,0:T(8,128)} %products.1.refs_0_), channel_id=1, source_target_pairs={{0,128},{1,385},{128,256},{129,1},{256,384},{257,129},{384,0},{385... | collective-permute-start | bytes 3158024 | tf_op jit(solution)/shard_map/ppermute | solution.py:170
  8.2 39.4 %collective-permute-start.1 = (f32[2056,128]{1,0:T(8,128)}, f32[2056,128]{1,0:T(8,128)S(1)}, u32[]{:S(2)}, u32[]{:S(2)}) collective-permute-start(f32[2056,128]{1,0:T(8,128)} %products.1.refs_0_), channel_id=1, source_target_pairs={{0,384},{1,129},{128,0},{129,257},{256,128},{257,385},{384,256},{3... | collective-permute-start | bytes 3158024 | tf_op jit(solution)/shard_map/ppermute | solution.py:170
  10.1 13.5 %collective-permute-start.2 = (s32[1,2]{1,0:T(1,128)S(1)}, s32[1,2]{1,0:T(1,128)S(1)}, u32[]{:S(2)}, u32[]{:S(2)}) collective-permute-start(s32[1,2]{1,0:T(1,128)S(1)} %copy-done.6), channel_id=1, source_target_pairs={{0,8},{1,17},{2,26},{3,35},{4,44},{5,53},{6,62},{7,71},{8,16},{9,2... | collective-permute-start | bytes 32 | tf_op jit(solution)/shard_map/ppermute | solution.py:195
  15.1 9.3 %collective-permute-start.3 = (s32[1,2]{1,0:T(1,128)S(1)}, s32[1,2]{1,0:T(1,128)S(1)}, u32[]{:S(2)}, u32[]{:S(2)}) collective-permute-start(s32[1,2]{1,0:T(1,128)S(1)} %copy-done.6), channel_id=1, source_target_pairs={{0,120},{1,113},{2,106},{3,99},{4,92},{5,85},{6,78},{7,71},{8,0},{... | collective-permute-start | bytes 32 | tf_op jit(solution)/shard_map/ppermute | solution.py:195
  23.7 0.7 copy-start.8
  24.4 0.6 copy-start.9
  28.9 34.2 %all-to-all-start = ((f32[8,264,128]{2,1,0:T(8,128)}), f32[8,264,128]{2,1,0:T(8,128)}, u32[]{:S(2)}, u32[]{:S(2)}) async-start(f32[8,264,128]{2,1,0:T(8,128)} %ladder.1), calls=%async_computation | async-start | bytes 2162688 | tf_op jit(solution)/shard_map/all_to_all | solution.py:239
  47.6 22.3 %copy-start = (f32[2056,128]{1,0:T(8,128)S(1)}, f32[2056,128]{1,0:T(8,128)}, u32[]{:S(2)}) copy-start(f32[2056,128]{1,0:T(8,128)} %products.1.refs_0_) | copy-start | bytes 3158020
  47.6 28.4 %collective-permute-start.4 = (f32[2056,128]{1,0:T(8,128)S(1)}, f32[2056,128]{1,0:T(8,128)}, u32[]{:S(2)}, u32[]{:S(2)}) collective-permute-start(f32[2056,128]{1,0:T(8,128)S(1)} %collective-permute-done.refs_1_), channel_id=1, source_target_pairs={{0,128},{1,385},{128,256},{129,1},{256,384},{257,129},{384,0},{385... | collective-permute-start | bytes 3158024 | tf_op jit(solution)/shard_map/ppermute | solution.py:170
  64.4 20.0 %collective-permute-start.5 = (f32[256,128]{1,0:T(8,128)S(1)}, f32[256,128]{1,0:T(8,128)S(1)}, u32[]{:S(2)}, u32[]{:S(2)}) collective-permute-start(f32[256,128]{1,0:T(8,128)S(1)} %slice_reduce_fusion), channel_id=1, source_target_pairs={{0,504},{8,496},{16,488},{24,480},{32,472},{40,464},{48,456},{56,4... | collective-permute-start | bytes 393224 | tf_op jit(solution)/shard_map/ppermute | solution.py:248
  76.0 1.0 copy-start.1
  77.1 1.0 copy-start.2
  78.1 1.0 copy-start.3
  79.2 1.0 copy-start.4
  84.4 46.9 %copy-start.7 = (s32[1,2]{1,0:T(1,128)S(1)}, s32[1,2]{1,0:T(1,128)}, u32[]{:S(2)}) copy-start(s32[1,2]{1,0:T(1,128)} %mine.3) | copy-start | bytes 28
  84.4 20.3 %collective-permute-start.6 = (f32[4,256,128]{2,1,0:T(8,128)}, f32[4,256,128]{2,1,0:T(8,128)S(1)}, u32[]{:S(2)}, u32[]{:S(2)}) collective-permute-start(f32[4,256,128]{2,1,0:T(8,128)} %get-tuple-element.40), channel_id=1, source_target_pairs={{0,16},{1,113},{8,24},{9,121},{16,32},{17,1},{24,40},{25,9},{32,48... | collective-permute-start | bytes 1572872 | tf_op jit(solution)/shard_map/ppermute | solution.py:174
  90.6 23.2 %collective-permute-start.7 = (f32[4,256,128]{2,1,0:T(8,128)}, f32[4,256,128]{2,1,0:T(8,128)S(1)}, u32[]{:S(2)}, u32[]{:S(2)}) collective-permute-start(f32[4,256,128]{2,1,0:T(8,128)} %get-tuple-element.41), channel_id=1, source_target_pairs={{0,8},{1,121},{8,16},{9,1},{16,24},{17,9},{24,32},{25,17},{32,40},... | collective-permute-start | bytes 1572872 | tf_op jit(solution)/shard_map/ppermute | solution.py:174
  94.1 19.7 %collective-permute-start.8 = (f32[4,256,128]{2,1,0:T(8,128)}, f32[4,256,128]{2,1,0:T(8,128)S(1)}, u32[]{:S(2)}, u32[]{:S(2)}) collective-permute-start(f32[4,256,128]{2,1,0:T(8,128)} %get-tuple-element.42), channel_id=1, source_target_pairs={{0,120},{1,9},{8,0},{9,17},{16,8},{17,25},{24,16},{25,33},{32,24},... | collective-permute-start | bytes 1572872 | tf_op jit(solution)/shard_map/ppermute | solution.py:174
  115.0 36.9 %copy-start.5 = (f32[256,128]{1,0:T(8,128)S(1)}, f32[256,128]{1,0:T(8,128)}, u32[]{:S(2)}) copy-start(f32[256,128]{1,0:T(8,128)} %param.19) | copy-start | bytes 393220
  115.0 17.1 %collective-permute-start.10 = (f32[256,128]{1,0:T(8,128)S(1)}, f32[256,128]{1,0:T(8,128)S(1)}, u32[]{:S(2)}, u32[]{:S(2)}) collective-permute-start(f32[256,128]{1,0:T(8,128)S(1)} %get-tuple-element.45), channel_id=1, source_target_pairs={{0,32},{1,97},{8,40},{9,105},{16,48},{17,113},{24,56},{25,121},{32... | collective-permute-start | bytes 393224 | tf_op jit(solution)/shard_map/ppermute | solution.py:174
  122.4 15.4 %collective-permute-start.11 = (f32[256,128]{1,0:T(8,128)S(1)}, f32[256,128]{1,0:T(8,128)S(1)}, u32[]{:S(2)}, u32[]{:S(2)}) collective-permute-start(f32[256,128]{1,0:T(8,128)S(1)} %get-tuple-element.44), channel_id=1, source_target_pairs={{0,96},{1,33},{8,104},{9,41},{16,112},{17,49},{24,120},{25,57},{32... | collective-permute-start | bytes 393224 | tf_op jit(solution)/shard_map/ppermute | solution.py:174
  124.3 27.5 %collective-permute-start.9 = (f32[256,128]{1,0:T(8,128)S(1)}, f32[256,128]{1,0:T(8,128)S(1)}, u32[]{:S(2)}, u32[]{:S(2)}) collective-permute-start(f32[256,128]{1,0:T(8,128)S(1)} %get-tuple-element.43), channel_id=1, source_target_pairs={{0,64},{1,65},{8,72},{9,73},{16,80},{17,81},{24,88},{25,89},{32,96... | collective-permute-start | bytes 393224 | tf_op jit(solution)/shard_map/ppermute | solution.py:174

commit v9 on v7

--- a/solution.py
+++ b/solution.py
@@ -222,13 +222,13 @@
     ladder = jnp.sum(spread, axis=0)
     n_occ = NX * NZ
     mirror = [(i, n_occ - 1 - i) for i in range(n_occ)]
-    other = lax.ppermute(ladder, ("x", "h", "l"), mirror)
-
     near = gather(slots, (got_c,), near)
     moved = [move_z(near[j], NEAR[j]) for j in range(3)]
     far = near[3] + moved[0] + moved[1] + moved[2]
-    far, other = lax.optimization_barrier((far, other))
+    far, ladder = lax.optimization_barrier((far, ladder))
+    other = lax.ppermute(ladder, ("x", "h", "l"), mirror)
     far = [far[0]] + [move_z(far[a], LOW * a) for a in (2, 1, 3)]
+    far[1], other = lax.optimization_barrier((far[1], other))
     other = other.reshape(OWN, EDGE, EDGE)[partner_slot[0]][:, ::-1, ::-1]
     ladder = ladder + other.reshape(OWN * EDGE, EDGE)
     return (ladder + far[0] + far[1] + far[2] + far[3]) / denom

time: 134 us -> 133 us (level)
  the two profiles are of different devices: /device:TPU:41 before, /device:TPU:24 now
where the time goes in v9:
time: 133 us; the launch traced here: 132 us
  starting transfers between devices  64.3 us (48%)
  waiting for transfers between devices  45.6 us (34%)
  Pallas kernels  17.5 us (13%)
  local copies, waits for them, and re-layouts  2.1 us (2%)
  other arithmetic  2.1 us (2%)
    ppermute x6, starting transfers between devices, move_z(): return lax.ppermute(array, ('h', 'l', 'c'), signed(NZ, distance))  30.3 us
    ppermute x6, waiting for transfers between devices, move_z(): return lax.ppermute(array, ('h', 'l', 'c'), signed(NZ, distance))  22.3 us
    all_to_all x1, starting transfers between devices, body(): lax.all_to_all(own_slots, ('h', 'l'), split_axis=0, concat_axis=0, tiled=...  15.2 us
    ppermute x1, waiting for transfers between devices, body(): other = lax.ppermute(ladder, ('x', 'h', 'l'), mirror)  14.3 us
    pallas_call x2, Pallas kernels, gather(): pl.pallas_call(functools.partial(gather_kernel, n, len(before) > 0), out_...  10.4 us
    ppermute x3, starting transfers between devices, move_x(): return lax.ppermute(array, ('x', 'c'), signed(NX, distance))  10 us
    all_to_all x1, waiting for transfers between devices, body(): lax.all_to_all(own_slots, ('h', 'l'), split_axis=0, concat_axis=0, tiled=...  8.48 us
    all_to_all x1, starting transfers between devices, body(): lax.all_to_all(partial, ('y', 'c'), split_axis=0, concat_axis=0, tiled=True)  4.83 us
  transfers between devices with their start and end apart: 12, of which 6 were waited for; matrix products, arithmetic and copies ran while one was open for 3% of the time, Pallas kernels for 11%

profile of v9, /device:TPU:24, one launch (start us, length us, event | category | flops | bytes accessed | tf_op | source)
XLA Modules:
  0.0 131.9 jit_solution(4851105876220353004)
XLA Ops:
  0.0 3.0 %products.1.refs_0_ = f32[2056,128]{1,0:T(8,128)} custom-call(s32[96]{0:T(128)} %bitcast.38, s32[96]{0:T(128)} %bitcast.39, s32[96]{0:T(128)} %bitcast.40, f32[4,128,256]{2,1,0:T(8,128)} %bitcast.33, f32[4,256,128]{2,1,0:T(8,128)} %bitcast.34), custom_call_target="tpu_custom_call" | custom-call | tf_op jit(solution)/shard_map/products/pallas_call | solution.py:195
  3.0 3.4 %collective-permute-start = (f32[2056,128]{1,0:T(8,128)}, f32[2056,128]{1,0:T(8,128)S(1)}, u32[]{:S(2)}, u32[]{:S(2)}) collective-permute-start(f32[2056,128]{1,0:T(8,128)} %products.1.refs_0_), channel_id=1, source_target_pairs={{0,128},{1,385},{128,256},{129,1},{256,384},{257,129},{384,0},{385... | collective-permute-start | bytes 3158024 | tf_op jit(solution)/shard_map/ppermute | solution.py:154
  6.4 3.7 %collective-permute-start.1 = (f32[2056,128]{1,0:T(8,128)}, f32[2056,128]{1,0:T(8,128)S(1)}, u32[]{:S(2)}, u32[]{:S(2)}) collective-permute-start(f32[2056,128]{1,0:T(8,128)} %products.1.refs_0_), channel_id=1, source_target_pairs={{0,384},{1,129},{128,0},{129,257},{256,128},{257,385},{384,256},{3... | collective-permute-start | bytes 3158024 | tf_op jit(solution)/shard_map/ppermute | solution.py:154
  10.1 0.0 copy-done.7
  10.1 0.7 broadcast_in_dim.2
  10.8 15.2 %all-to-all-start = ((s32[16,24,128]{2,1,0:T(8,128)}), s32[16,24,128]{2,1,0:T(8,128)S(1)}, u32[]{:S(2)}, u32[]{:S(2)}) async-start(s32[16,24,128]{2,1,0:T(8,128)} %broadcast_in_dim.2), calls=%async_computation | async-start | bytes 393216 | tf_op jit(solution)/shard_map/all_to_all | solution.py:214
  26.0 0.0 copy-start
  26.0 4.0 %ladder.1 = f32[8,256,128]{2,1,0:T(8,128)} custom-call(s32[2,4]{1,0:T(2,128)} %mask.1, f32[256,512]{1,0:T(8,128)} %lam_ref.1, f32[512,1024]{1,0:T(8,128)} %ints_ref.1), custom_call_target="tpu_custom_call" | custom-call | tf_op jit(solution)/shard_map/ladder/pallas_call | solution.py:205
  30.1 0.0 collective-permute-done.refs_1_
  30.1 0.4 collective-permute-done.1.refs_2_
  30.5 3.0 %collective-permute-start.2 = (f32[2056,128]{1,0:T(8,128)S(1)}, f32[2056,128]{1,0:T(8,128)}, u32[]{:S(2)}, u32[]{:S(2)}) collective-permute-start(f32[2056,128]{1,0:T(8,128)S(1)} %collective-permute-done.refs_1_), channel_id=1, source_target_pairs={{0,128},{1,385},{128,256},{129,1},{256,384},{257,129},{384,0},{385... | collective-permute-start | bytes 3158024 | tf_op jit(solution)/shard_map/ppermute | solution.py:154
  33.5 8.5 %all-to-all-done = s32[16,24,128]{2,1,0:T(8,128)S(1)} async-done(((s32[16,24,128]{2,1,0:T(8,128)}), s32[16,24,128]{2,1,0:T(8,128)S(1)}, u32[]{:S(2)}, u32[]{:S(2)}) %all-to-all-start) | async-done | bytes 196640 | tf_op jit(solution)/shard_map/all_to_all | solution.py:214
  42.0 0.6 slice.22
  42.6 0.0 copy-done
  42.6 6.2 %gather.7 = (f32[4,256,128]{2,1,0:T(8,128)}, f32[4,256,128]{2,1,0:T(8,128)}, f32[4,256,128]{2,1,0:T(8,128)}, f32[4,256,128]{2,1,0:T(8,128)}) custom-call(s32[16,2]{1,0:T(8,128)} %bitcast.36, f32[2056,128]{1,0:T(8,128)S(1)} %copy-done, f32[2056,128]{1,0:T(8,128)S(1)} %collective-permute-done.refs_1_, f32[2056,128]{1,0:T(8,128)S(1)} %collective-permute-done.1.refs_2_), custom_call_target="tpu_custom_call" | custom-call | tf_op jit(solution)/shard_map/gather/pallas_call | solution.py:164
  48.8 0.0 copy-start.1
  48.8 0.0 copy-start.2
  48.9 0.0 copy-start.3
  48.9 0.0 copy-start.4
  48.9 4.8 %all-to-all-start.1 = ((f32[8,256,128]{2,1,0:T(8,128)}), f32[8,256,128]{2,1,0:T(8,128)}, u32[]{:S(2)}, u32[]{:S(2)}) async-start(f32[8,256,128]{2,1,0:T(8,128)} %ladder.1), calls=%async_computation.1 | async-start | bytes 2097152 | tf_op jit(solution)/shard_map/all_to_all | solution.py:221
  53.7 0.0 collective-permute-done.2.refs_0_
  53.7 0.0 copy-done.1
  53.7 0.0 copy-done.2
  53.7 0.0 copy-done.3
  53.7 0.0 copy-done.4
  53.7 4.2 %gather_more.1 = (f32[4,256,128]{2,1,0:T(8,128)}, f32[4,256,128]{2,1,0:T(8,128)}, f32[4,256,128]{2,1,0:T(8,128)}, f32[4,256,128]{2,1,0:T(8,128)}) custom-call(s32[16,2]{1,0:T(8,128)} %bitcast.37, f32[2056,128]{1,0:T(8,128)} %collective-permute-done.2.refs_0_, f32[4,256,128]{2,1,0:T(8,128)S(1)} %copy-done.1, f32[4,256,128]{2,1,0:T(8,128)S(1)} %copy-done.2, ...), custom_call_target="tpu_custom_call" | custom-call | tf_op jit(solution)/shard_map/gather_more/pallas_call | solution.py:164
  57.9 0.0 copy-start.5
  57.9 3.5 %collective-permute-start.3 = (f32[4,256,128]{2,1,0:T(8,128)}, f32[4,256,128]{2,1,0:T(8,128)S(1)}, u32[]{:S(2)}, u32[]{:S(2)}) collective-permute-start(f32[4,256,128]{2,1,0:T(8,128)} %get-tuple-element.37), channel_id=1, source_target_pairs={{0,16},{1,113},{8,24},{9,121},{16,32},{17,1},{24,40},{25,9},{32,48... | collective-permute-start | bytes 1572872 | tf_op jit(solution)/shard_map/ppermute | solution.py:158
  61.4 3.5 %collective-permute-start.4 = (f32[4,256,128]{2,1,0:T(8,128)}, f32[4,256,128]{2,1,0:T(8,128)S(1)}, u32[]{:S(2)}, u32[]{:S(2)}) collective-permute-start(f32[4,256,128]{2,1,0:T(8,128)} %get-tuple-element.38), channel_id=1, source_target_pairs={{0,8},{1,121},{8,16},{9,1},{16,24},{17,9},{24,32},{25,17},{32,40},... | collective-permute-start | bytes 1572872 | tf_op jit(solution)/shard_map/ppermute | solution.py:158
  64.9 3.6 %collective-permute-start.5 = (f32[4,256,128]{2,1,0:T(8,128)}, f32[4,256,128]{2,1,0:T(8,128)S(1)}, u32[]{:S(2)}, u32[]{:S(2)}) collective-permute-start(f32[4,256,128]{2,1,0:T(8,128)} %get-tuple-element.39), channel_id=1, source_target_pairs={{0,120},{1,9},{8,0},{9,17},{16,8},{17,25},{24,16},{25,33},{32,24},... | collective-permute-start | bytes 1572872 | tf_op jit(solution)/shard_map/ppermute | solution.py:158
  68.5 0.0 all-to-all-done.1
  68.5 1.3 reduce_sum.9
  69.8 6.2 %collective-permute-done.3 = f32[4,256,128]{2,1,0:T(8,128)S(1)} collective-permute-done((f32[4,256,128]{2,1,0:T(8,128)}, f32[4,256,128]{2,1,0:T(8,128)S(1)}, u32[]{:S(2)}, u32[]{:S(2)}) %collective-permute-start.3) | collective-permute-done | bytes 524320 | tf_op jit(solution)/shard_map/ppermute | solution.py:158
  76.0 12.9 %collective-permute-done.4 = f32[4,256,128]{2,1,0:T(8,128)S(1)} collective-permute-done((f32[4,256,128]{2,1,0:T(8,128)}, f32[4,256,128]{2,1,0:T(8,128)S(1)}, u32[]{:S(2)}, u32[]{:S(2)}) %collective-permute-start.4) | collective-permute-done | bytes 524320 | tf_op jit(solution)/shard_map/ppermute | solution.py:158
  88.9 0.0 collective-permute-done.5
  88.9 0.1 add_add_fusion
  89.0 0.0 copy-start.6
  89.0 10.0 %collective-permute-start.6 = (f32[256,128]{1,0:T(8,128)S(1)}, f32[256,128]{1,0:T(8,128)S(1)}, u32[]{:S(2)}, u32[]{:S(2)}) collective-permute-start(f32[256,128]{1,0:T(8,128)S(1)} %get-tuple-element.45), channel_id=1, source_target_pairs={{0,64},{1,65},{8,72},{9,73},{16,80},{17,81},{24,88},{25,89},{32,96... | collective-permute-start | bytes 393224 | tf_op jit(solution)/shard_map/ppermute | solution.py:158
  99.1 3.9 %collective-permute-start.7 = (f32[256,128]{1,0:T(8,128)S(1)}, f32[256,128]{1,0:T(8,128)S(1)}, u32[]{:S(2)}, u32[]{:S(2)}) collective-permute-start(f32[256,128]{1,0:T(8,128)S(1)} %reduce_sum.9), channel_id=1, source_target_pairs={{0,504},{8,496},{16,488},{24,480},{32,472},{40,464},{48,456},{56,4... | collective-permute-start | bytes 393224 | tf_op jit(solution)/shard_map/ppermute | solution.py:229
  103.0 4.9 %collective-permute-start.8 = (f32[256,128]{1,0:T(8,128)S(1)}, f32[256,128]{1,0:T(8,128)S(1)}, u32[]{:S(2)}, u32[]{:S(2)}) collective-permute-start(f32[256,128]{1,0:T(8,128)S(1)} %get-tuple-element.47), channel_id=1, source_target_pairs={{0,32},{1,97},{8,40},{9,105},{16,48},{17,113},{24,56},{25,121},{32... | collective-permute-start | bytes 393224 | tf_op jit(solution)/shard_map/ppermute | solution.py:158
  107.9 4.9 %collective-permute-start.9 = (f32[256,128]{1,0:T(8,128)S(1)}, f32[256,128]{1,0:T(8,128)S(1)}, u32[]{:S(2)}, u32[]{:S(2)}) collective-permute-start(f32[256,128]{1,0:T(8,128)S(1)} %get-tuple-element.46), channel_id=1, source_target_pairs={{0,96},{1,33},{8,104},{9,41},{16,112},{17,49},{24,120},{25,57},{32... | collective-permute-start | bytes 393224 | tf_op jit(solution)/shard_map/ppermute | solution.py:158
  112.8 0.0 collective-permute-done.6
  112.8 14.3 %collective-permute-done.7 = f32[256,128]{1,0:T(8,128)S(1)} collective-permute-done((f32[256,128]{1,0:T(8,128)S(1)}, f32[256,128]{1,0:T(8,128)S(1)}, u32[]{:S(2)}, u32[]{:S(2)}) %collective-permute-start.7) | collective-permute-done | bytes 131104 | tf_op jit(solution)/shard_map/ppermute | solution.py:229
  127.1 0.6 gather_fusion
  127.7 0.2 rev.3
  127.9 0.0 collective-permute-done.8
  127.9 3.3 %collective-permute-done.9 = f32[256,128]{1,0:T(8,128)S(1)} collective-permute-done((f32[256,128]{1,0:T(8,128)S(1)}, f32[256,128]{1,0:T(8,128)S(1)}, u32[]{:S(2)}, u32[]{:S(2)}) %collective-permute-start.9) | collective-permute-done | bytes 131104 | tf_op jit(solution)/shard_map/ppermute | solution.py:158
  131.2 0.7 fusion.3
  (7 shorter events, 0.0 us)
Async XLA Ops:
  0.0 10.1 %copy-start.7 = (s32[1,2]{1,0:T(1,128)S(1)}, s32[1,2]{1,0:T(1,128)}, u32[]{:S(2)}) copy-start(s32[1,2]{1,0:T(1,128)} %param.18) | copy-start | bytes 28
  3.0 27.0 %collective-permute-start = (f32[2056,128]{1,0:T(8,128)}, f32[2056,128]{1,0:T(8,128)S(1)}, u32[]{:S(2)}, u32[]{:S(2)}) collective-permute-start(f32[2056,128]{1,0:T(8,128)} %products.1.refs_0_), channel_id=1, source_target_pairs={{0,128},{1,385},{128,256},{129,1},{256,384},{257,129},{384,0},{385... | collective-permute-start | bytes 3158024 | tf_op jit(solution)/shard_map/ppermute | solution.py:154
  6.4 24.1 %collective-permute-start.1 = (f32[2056,128]{1,0:T(8,128)}, f32[2056,128]{1,0:T(8,128)S(1)}, u32[]{:S(2)}, u32[]{:S(2)}) collective-permute-start(f32[2056,128]{1,0:T(8,128)} %products.1.refs_0_), channel_id=1, source_target_pairs={{0,384},{1,129},{128,0},{129,257},{256,128},{257,385},{384,256},{3... | collective-permute-start | bytes 3158024 | tf_op jit(solution)/shard_map/ppermute | solution.py:154
  10.8 31.2 %all-to-all-start = ((s32[16,24,128]{2,1,0:T(8,128)}), s32[16,24,128]{2,1,0:T(8,128)S(1)}, u32[]{:S(2)}, u32[]{:S(2)}) async-start(s32[16,24,128]{2,1,0:T(8,128)} %broadcast_in_dim.2), calls=%async_computation | async-start | bytes 393216 | tf_op jit(solution)/shard_map/all_to_all | solution.py:214
  26.0 16.6 %copy-start = (f32[2056,128]{1,0:T(8,128)S(1)}, f32[2056,128]{1,0:T(8,128)}, u32[]{:S(2)}) copy-start(f32[2056,128]{1,0:T(8,128)} %products.1.refs_0_) | copy-start | bytes 3158020
  30.5 23.2 %collective-permute-start.2 = (f32[2056,128]{1,0:T(8,128)S(1)}, f32[2056,128]{1,0:T(8,128)}, u32[]{:S(2)}, u32[]{:S(2)}) collective-permute-start(f32[2056,128]{1,0:T(8,128)S(1)} %collective-permute-done.refs_1_), channel_id=1, source_target_pairs={{0,128},{1,385},{128,256},{129,1},{256,384},{257,129},{384,0},{385... | collective-permute-start | bytes 3158024 | tf_op jit(solution)/shard_map/ppermute | solution.py:154
  48.8 4.9 %copy-start.1 = (f32[4,256,128]{2,1,0:T(8,128)S(1)}, f32[4,256,128]{2,1,0:T(8,128)}, u32[]{:S(2)}) copy-start(f32[4,256,128]{2,1,0:T(8,128)} %get-tuple-element.32.refs_1_) | copy-start | bytes 1572868
  48.8 4.9 %copy-start.2 = (f32[4,256,128]{2,1,0:T(8,128)S(1)}, f32[4,256,128]{2,1,0:T(8,128)}, u32[]{:S(2)}) copy-start(f32[4,256,128]{2,1,0:T(8,128)} %get-tuple-element.33.refs_2_) | copy-start | bytes 1572868
  48.9 4.9 %copy-start.3 = (f32[4,256,128]{2,1,0:T(8,128)S(1)}, f32[4,256,128]{2,1,0:T(8,128)}, u32[]{:S(2)}) copy-start(f32[4,256,128]{2,1,0:T(8,128)} %get-tuple-element.34.refs_3_) | copy-start | bytes 1572868
  48.9 4.9 %copy-start.4 = (f32[4,256,128]{2,1,0:T(8,128)S(1)}, f32[4,256,128]{2,1,0:T(8,128)}, u32[]{:S(2)}) copy-start(f32[4,256,128]{2,1,0:T(8,128)} %get-tuple-element.35.refs_4_) | copy-start | bytes 1572868
  48.9 19.6 %all-to-all-start.1 = ((f32[8,256,128]{2,1,0:T(8,128)}), f32[8,256,128]{2,1,0:T(8,128)}, u32[]{:S(2)}, u32[]{:S(2)}) async-start(f32[8,256,128]{2,1,0:T(8,128)} %ladder.1), calls=%async_computation.1 | async-start | bytes 2097152 | tf_op jit(solution)/shard_map/all_to_all | solution.py:221
  57.9 30.9 %copy-start.5 = (f32[4,256,128]{2,1,0:T(8,128)S(1)}, f32[4,256,128]{2,1,0:T(8,128)}, u32[]{:S(2)}) copy-start(f32[4,256,128]{2,1,0:T(8,128)} %get-tuple-element.36) | copy-start | bytes 1572868
  57.9 18.0 %collective-permute-start.3 = (f32[4,256,128]{2,1,0:T(8,128)}, f32[4,256,128]{2,1,0:T(8,128)S(1)}, u32[]{:S(2)}, u32[]{:S(2)}) collective-permute-start(f32[4,256,128]{2,1,0:T(8,128)} %get-tuple-element.37), channel_id=1, source_target_pairs={{0,16},{1,113},{8,24},{9,121},{16,32},{17,1},{24,40},{25,9},{32,48... | collective-permute-start | bytes 1572872 | tf_op jit(solution)/shard_map/ppermute | solution.py:158
  61.4 27.4 %collective-permute-start.4 = (f32[4,256,128]{2,1,0:T(8,128)}, f32[4,256,128]{2,1,0:T(8,128)S(1)}, u32[]{:S(2)}, u32[]{:S(2)}) collective-permute-start(f32[4,256,128]{2,1,0:T(8,128)} %get-tuple-element.38), channel_id=1, source_target_pairs={{0,8},{1,121},{8,16},{9,1},{16,24},{17,9},{24,32},{25,17},{32,40},... | collective-permute-start | bytes 1572872 | tf_op jit(solution)/shard_map/ppermute | solution.py:158
  64.9 24.0 %collective-permute-start.5 = (f32[4,256,128]{2,1,0:T(8,128)}, f32[4,256,128]{2,1,0:T(8,128)S(1)}, u32[]{:S(2)}, u32[]{:S(2)}) collective-permute-start(f32[4,256,128]{2,1,0:T(8,128)} %get-tuple-element.39), channel_id=1, source_target_pairs={{0,120},{1,9},{8,0},{9,17},{16,8},{17,25},{24,16},{25,33},{32,24},... | collective-permute-start | bytes 1572872 | tf_op jit(solution)/shard_map/ppermute | solution.py:158
  89.0 42.2 %copy-start.6 = (f32[256,128]{1,0:T(8,128)S(1)}, f32[256,128]{1,0:T(8,128)}, u32[]{:S(2)}) copy-start(f32[256,128]{1,0:T(8,128)} %param.19) | copy-start | bytes 393220
  89.0 23.8 %collective-permute-start.6 = (f32[256,128]{1,0:T(8,128)S(1)}, f32[256,128]{1,0:T(8,128)S(1)}, u32[]{:S(2)}, u32[]{:S(2)}) collective-permute-start(f32[256,128]{1,0:T(8,128)S(1)} %get-tuple-element.45), channel_id=1, source_target_pairs={{0,64},{1,65},{8,72},{9,73},{16,80},{17,81},{24,88},{25,89},{32,96... | collective-permute-start | bytes 393224 | tf_op jit(solution)/shard_map/ppermute | solution.py:158
  99.1 28.1 %collective-permute-start.7 = (f32[256,128]{1,0:T(8,128)S(1)}, f32[256,128]{1,0:T(8,128)S(1)}, u32[]{:S(2)}, u32[]{:S(2)}) collective-permute-start(f32[256,128]{1,0:T(8,128)S(1)} %reduce_sum.9), channel_id=1, source_target_pairs={{0,504},{8,496},{16,488},{24,480},{32,472},{40,464},{48,456},{56,4... | collective-permute-start | bytes 393224 | tf_op jit(solution)/shard_map/ppermute | solution.py:229
  103.0 24.9 %collective-permute-start.8 = (f32[256,128]{1,0:T(8,128)S(1)}, f32[256,128]{1,0:T(8,128)S(1)}, u32[]{:S(2)}, u32[]{:S(2)}) collective-permute-start(f32[256,128]{1,0:T(8,128)S(1)} %get-tuple-element.47), channel_id=1, source_target_pairs={{0,32},{1,97},{8,40},{9,105},{16,48},{17,113},{24,56},{25,121},{32... | collective-permute-start | bytes 393224 | tf_op jit(solution)/shard_map/ppermute | solution.py:158
  107.9 23.3 %collective-permute-start.9 = (f32[256,128]{1,0:T(8,128)S(1)}, f32[256,128]{1,0:T(8,128)S(1)}, u32[]{:S(2)}, u32[]{:S(2)}) collective-permute-start(f32[256,128]{1,0:T(8,128)S(1)} %get-tuple-element.46), channel_id=1, source_target_pairs={{0,96},{1,33},{8,104},{9,41},{16,112},{17,49},{24,120},{25,57},{32... | collective-permute-start | bytes 393224 | tf_op jit(solution)/shard_map/ppermute | solution.py:158

commit v10 on v9

--- a/solution.py
+++ b/solution.py
@@ -228,7 +228,7 @@
     far, ladder = lax.optimization_barrier((far, ladder))
     other = lax.ppermute(ladder, ("x", "h", "l"), mirror)
     far = [far[0]] + [move_z(far[a], LOW * a) for a in (2, 1, 3)]
-    far[1], other = lax.optimization_barrier((far[1], other))
+    far[3], other = lax.optimization_barrier((far[3], other))
     other = other.reshape(OWN, EDGE, EDGE)[partner_slot[0]][:, ::-1, ::-1]
     ladder = ladder + other.reshape(OWN * EDGE, EDGE)
     return (ladder + far[0] + far[1] + far[2] + far[3]) / denom

time: 133 us -> 132 us (level)
    ppermute x1, waiting for transfers between devices: 14.3 us -> 6.29 us  [body(): other = lax.ppermute(ladder, ('x', 'h', 'l'), mirror)]
    ppermute x6, waiting for transfers between devices: 22.3 us -> 29.5 us  [move_z(): return lax.ppermute(array, ('h', 'l', 'c'), signed(NZ, distance))]
where the time goes in v10:
time: 132 us
  starting transfers between devices  64.9 us (49%)
  waiting for transfers between devices  44.7 us (34%)
  Pallas kernels  17.5 us (13%)
  other arithmetic  2.11 us (2%)
  local copies, waits for them, and re-layouts  2.1 us (2%)
    ppermute x6, starting transfers between devices, move_z(): return lax.ppermute(array, ('h', 'l', 'c'), signed(NZ, distance))  30.5 us
    ppermute x6, waiting for transfers between devices, move_z(): return lax.ppermute(array, ('h', 'l', 'c'), signed(NZ, distance))  29.5 us
    all_to_all x1, starting transfers between devices, body(): lax.all_to_all(own_slots, ('h', 'l'), split_axis=0, concat_axis=0, tiled=...  15.2 us
    pallas_call x2, Pallas kernels, gather(): pl.pallas_call(functools.partial(gather_kernel, n, len(before) > 0), out_...  10.4 us
    ppermute x3, starting transfers between devices, move_x(): return lax.ppermute(array, ('x', 'c'), signed(NX, distance))  10 us
    all_to_all x1, waiting for transfers between devices, body(): lax.all_to_all(own_slots, ('h', 'l'), split_axis=0, concat_axis=0, tiled=...  8.48 us
    ppermute x1, waiting for transfers between devices, body(): other = lax.ppermute(ladder, ('x', 'h', 'l'), mirror)  6.29 us
    all_to_all x1, starting transfers between devices, body(): lax.all_to_all(partial, ('y', 'c'), split_axis=0, concat_axis=0, tiled=True)  4.83 us
  transfers between devices with their start and end apart: 12, of which 6 were waited for; matrix products, arithmetic and copies ran while one was open for 3% of the time, Pallas kernels for 11%

profile of v10, /device:TPU:24, one launch (start us, length us, event | category | flops | bytes accessed | tf_op | source)
XLA Modules:
  0.0 131.5 jit_solution(9693587516577053355)
XLA Ops:
  0.0 3.0 %products.1.refs_0_ = f32[2056,128]{1,0:T(8,128)} custom-call(s32[96]{0:T(128)} %bitcast.38, s32[96]{0:T(128)} %bitcast.39, s32[96]{0:T(128)} %bitcast.40, f32[4,128,256]{2,1,0:T(8,128)} %bitcast.33, f32[4,256,128]{2,1,0:T(8,128)} %bitcast.34), custom_call_target="tpu_custom_call" | custom-call | tf_op jit(solution)/shard_map/products/pallas_call | solution.py:195
  3.0 3.4 %collective-permute-start = (f32[2056,128]{1,0:T(8,128)}, f32[2056,128]{1,0:T(8,128)S(1)}, u32[]{:S(2)}, u32[]{:S(2)}) collective-permute-start(f32[2056,128]{1,0:T(8,128)} %products.1.refs_0_), channel_id=1, source_target_pairs={{0,128},{1,385},{128,256},{129,1},{256,384},{257,129},{384,0},{385... | collective-permute-start | bytes 3158024 | tf_op jit(solution)/shard_map/ppermute | solution.py:154
  6.4 3.7 %collective-permute-start.1 = (f32[2056,128]{1,0:T(8,128)}, f32[2056,128]{1,0:T(8,128)S(1)}, u32[]{:S(2)}, u32[]{:S(2)}) collective-permute-start(f32[2056,128]{1,0:T(8,128)} %products.1.refs_0_), channel_id=1, source_target_pairs={{0,384},{1,129},{128,0},{129,257},{256,128},{257,385},{384,256},{3... | collective-permute-start | bytes 3158024 | tf_op jit(solution)/shard_map/ppermute | solution.py:154
  10.1 0.0 copy-done.7
  10.1 0.7 broadcast_in_dim.2
  10.8 15.2 %all-to-all-start = ((s32[16,24,128]{2,1,0:T(8,128)}), s32[16,24,128]{2,1,0:T(8,128)S(1)}, u32[]{:S(2)}, u32[]{:S(2)}) async-start(s32[16,24,128]{2,1,0:T(8,128)} %broadcast_in_dim.2), calls=%async_computation | async-start | bytes 393216 | tf_op jit(solution)/shard_map/all_to_all | solution.py:214
  26.0 0.0 copy-start
  26.0 4.0 %ladder.1 = f32[8,256,128]{2,1,0:T(8,128)} custom-call(s32[2,4]{1,0:T(2,128)} %mask.1, f32[256,512]{1,0:T(8,128)} %lam_ref.1, f32[512,1024]{1,0:T(8,128)} %ints_ref.1), custom_call_target="tpu_custom_call" | custom-call | tf_op jit(solution)/shard_map/ladder/pallas_call | solution.py:205
  30.1 0.0 collective-permute-done.refs_1_
  30.1 0.4 collective-permute-done.1.refs_2_
  30.5 3.0 %collective-permute-start.2 = (f32[2056,128]{1,0:T(8,128)S(1)}, f32[2056,128]{1,0:T(8,128)}, u32[]{:S(2)}, u32[]{:S(2)}) collective-permute-start(f32[2056,128]{1,0:T(8,128)S(1)} %collective-permute-done.refs_1_), channel_id=1, source_target_pairs={{0,128},{1,385},{128,256},{129,1},{256,384},{257,129},{384,0},{385... | collective-permute-start | bytes 3158024 | tf_op jit(solution)/shard_map/ppermute | solution.py:154
  33.5 8.5 %all-to-all-done = s32[16,24,128]{2,1,0:T(8,128)S(1)} async-done(((s32[16,24,128]{2,1,0:T(8,128)}), s32[16,24,128]{2,1,0:T(8,128)S(1)}, u32[]{:S(2)}, u32[]{:S(2)}) %all-to-all-start) | async-done | bytes 196640 | tf_op jit(solution)/shard_map/all_to_all | solution.py:214
  42.0 0.6 slice.22
  42.6 0.0 copy-done
  42.6 6.2 %gather.7 = (f32[4,256,128]{2,1,0:T(8,128)}, f32[4,256,128]{2,1,0:T(8,128)}, f32[4,256,128]{2,1,0:T(8,128)}, f32[4,256,128]{2,1,0:T(8,128)}) custom-call(s32[16,2]{1,0:T(8,128)} %bitcast.36, f32[2056,128]{1,0:T(8,128)S(1)} %copy-done, f32[2056,128]{1,0:T(8,128)S(1)} %collective-permute-done.refs_1_, f32[2056,128]{1,0:T(8,128)S(1)} %collective-permute-done.1.refs_2_), custom_call_target="tpu_custom_call" | custom-call | tf_op jit(solution)/shard_map/gather/pallas_call | solution.py:164
  48.8 0.0 copy-start.1
  48.8 0.0 copy-start.2
  48.9 0.0 copy-start.3
  48.9 0.0 copy-start.4
  48.9 4.8 %all-to-all-start.1 = ((f32[8,256,128]{2,1,0:T(8,128)}), f32[8,256,128]{2,1,0:T(8,128)}, u32[]{:S(2)}, u32[]{:S(2)}) async-start(f32[8,256,128]{2,1,0:T(8,128)} %ladder.1), calls=%async_computation.1 | async-start | bytes 2097152 | tf_op jit(solution)/shard_map/all_to_all | solution.py:221
  53.7 0.0 collective-permute-done.2.refs_0_
  53.7 0.0 copy-done.1
  53.7 0.0 copy-done.2
  53.7 0.0 copy-done.3
  53.7 0.0 copy-done.4
  53.7 4.2 %gather_more.1 = (f32[4,256,128]{2,1,0:T(8,128)}, f32[4,256,128]{2,1,0:T(8,128)}, f32[4,256,128]{2,1,0:T(8,128)}, f32[4,256,128]{2,1,0:T(8,128)}) custom-call(s32[16,2]{1,0:T(8,128)} %bitcast.37, f32[2056,128]{1,0:T(8,128)} %collective-permute-done.2.refs_0_, f32[4,256,128]{2,1,0:T(8,128)S(1)} %copy-done.1, f32[4,256,128]{2,1,0:T(8,128)S(1)} %copy-done.2, ...), custom_call_target="tpu_custom_call" | custom-call | tf_op jit(solution)/shard_map/gather_more/pallas_call | solution.py:164
  57.9 0.0 copy-start.5
  57.9 3.5 %collective-permute-start.3 = (f32[4,256,128]{2,1,0:T(8,128)}, f32[4,256,128]{2,1,0:T(8,128)S(1)}, u32[]{:S(2)}, u32[]{:S(2)}) collective-permute-start(f32[4,256,128]{2,1,0:T(8,128)} %get-tuple-element.37), channel_id=1, source_target_pairs={{0,16},{1,113},{8,24},{9,121},{16,32},{17,1},{24,40},{25,9},{32,48... | collective-permute-start | bytes 1572872 | tf_op jit(solution)/shard_map/ppermute | solution.py:158
  61.4 3.5 %collective-permute-start.4 = (f32[4,256,128]{2,1,0:T(8,128)}, f32[4,256,128]{2,1,0:T(8,128)S(1)}, u32[]{:S(2)}, u32[]{:S(2)}) collective-permute-start(f32[4,256,128]{2,1,0:T(8,128)} %get-tuple-element.38), channel_id=1, source_target_pairs={{0,8},{1,121},{8,16},{9,1},{16,24},{17,9},{24,32},{25,17},{32,40},... | collective-permute-start | bytes 1572872 | tf_op jit(solution)/shard_map/ppermute | solution.py:158
  64.9 3.6 %collective-permute-start.5 = (f32[4,256,128]{2,1,0:T(8,128)}, f32[4,256,128]{2,1,0:T(8,128)S(1)}, u32[]{:S(2)}, u32[]{:S(2)}) collective-permute-start(f32[4,256,128]{2,1,0:T(8,128)} %get-tuple-element.39), channel_id=1, source_target_pairs={{0,120},{1,9},{8,0},{9,17},{16,8},{17,25},{24,16},{25,33},{32,24},... | collective-permute-start | bytes 1572872 | tf_op jit(solution)/shard_map/ppermute | solution.py:158
  68.5 0.0 all-to-all-done.1
  68.5 1.3 reduce_sum.9
  69.8 6.2 %collective-permute-done.3 = f32[4,256,128]{2,1,0:T(8,128)S(1)} collective-permute-done((f32[4,256,128]{2,1,0:T(8,128)}, f32[4,256,128]{2,1,0:T(8,128)S(1)}, u32[]{:S(2)}, u32[]{:S(2)}) %collective-permute-start.3) | collective-permute-done | bytes 524320 | tf_op jit(solution)/shard_map/ppermute | solution.py:158
  76.0 12.9 %collective-permute-done.4 = f32[4,256,128]{2,1,0:T(8,128)S(1)} collective-permute-done((f32[4,256,128]{2,1,0:T(8,128)}, f32[4,256,128]{2,1,0:T(8,128)S(1)}, u32[]{:S(2)}, u32[]{:S(2)}) %collective-permute-start.4) | collective-permute-done | bytes 524320 | tf_op jit(solution)/shard_map/ppermute | solution.py:158
  88.9 0.0 collective-permute-done.5
  88.9 0.1 add_add_fusion
  89.0 0.0 copy-start.6
  89.0 7.1 %collective-permute-start.6 = (f32[256,128]{1,0:T(8,128)S(1)}, f32[256,128]{1,0:T(8,128)S(1)}, u32[]{:S(2)}, u32[]{:S(2)}) collective-permute-start(f32[256,128]{1,0:T(8,128)S(1)} %get-tuple-element.47), channel_id=1, source_target_pairs={{0,96},{1,33},{8,104},{9,41},{16,112},{17,49},{24,120},{25,57},{32... | collective-permute-start | bytes 393224 | tf_op jit(solution)/shard_map/ppermute | solution.py:158
  96.1 4.4 %collective-permute-start.7 = (f32[256,128]{1,0:T(8,128)S(1)}, f32[256,128]{1,0:T(8,128)S(1)}, u32[]{:S(2)}, u32[]{:S(2)}) collective-permute-start(f32[256,128]{1,0:T(8,128)S(1)} %reduce_sum.9), channel_id=1, source_target_pairs={{0,504},{8,496},{16,488},{24,480},{32,472},{40,464},{48,456},{56,4... | collective-permute-start | bytes 393224 | tf_op jit(solution)/shard_map/ppermute | solution.py:229
  100.4 4.7 %collective-permute-start.8 = (f32[256,128]{1,0:T(8,128)S(1)}, f32[256,128]{1,0:T(8,128)S(1)}, u32[]{:S(2)}, u32[]{:S(2)}) collective-permute-start(f32[256,128]{1,0:T(8,128)S(1)} %get-tuple-element.45), channel_id=1, source_target_pairs={{0,64},{1,65},{8,72},{9,73},{16,80},{17,81},{24,88},{25,89},{32,96... | collective-permute-start | bytes 393224 | tf_op jit(solution)/shard_map/ppermute | solution.py:158
  105.2 8.1 %collective-permute-start.9 = (f32[256,128]{1,0:T(8,128)S(1)}, f32[256,128]{1,0:T(8,128)S(1)}, u32[]{:S(2)}, u32[]{:S(2)}) collective-permute-start(f32[256,128]{1,0:T(8,128)S(1)} %get-tuple-element.46), channel_id=1, source_target_pairs={{0,32},{1,97},{8,40},{9,105},{16,48},{17,113},{24,56},{25,121},{32... | collective-permute-start | bytes 393224 | tf_op jit(solution)/shard_map/ppermute | solution.py:158
  113.4 10.4 %collective-permute-done.6 = f32[256,128]{1,0:T(8,128)S(1)} collective-permute-done((f32[256,128]{1,0:T(8,128)S(1)}, f32[256,128]{1,0:T(8,128)S(1)}, u32[]{:S(2)}, u32[]{:S(2)}) %collective-permute-start.6) | collective-permute-done | bytes 131104 | tf_op jit(solution)/shard_map/ppermute | solution.py:158
  123.8 6.3 %collective-permute-done.7 = f32[256,128]{1,0:T(8,128)S(1)} collective-permute-done((f32[256,128]{1,0:T(8,128)S(1)}, f32[256,128]{1,0:T(8,128)S(1)}, u32[]{:S(2)}, u32[]{:S(2)}) %collective-permute-start.7) | collective-permute-done | bytes 131104 | tf_op jit(solution)/shard_map/ppermute | solution.py:229
  130.1 0.6 gather_fusion
  130.6 0.2 rev.3
  130.8 0.0 collective-permute-done.8
  130.8 0.0 collective-permute-done.9
  130.8 0.7 fusion.3
  (7 shorter events, 0.0 us)
Async XLA Ops:
  0.0 10.1 %copy-start.7 = (s32[1,2]{1,0:T(1,128)S(1)}, s32[1,2]{1,0:T(1,128)}, u32[]{:S(2)}) copy-start(s32[1,2]{1,0:T(1,128)} %param.18) | copy-start | bytes 28
  3.0 27.0 %collective-permute-start = (f32[2056,128]{1,0:T(8,128)}, f32[2056,128]{1,0:T(8,128)S(1)}, u32[]{:S(2)}, u32[]{:S(2)}) collective-permute-start(f32[2056,128]{1,0:T(8,128)} %products.1.refs_0_), channel_id=1, source_target_pairs={{0,128},{1,385},{128,256},{129,1},{256,384},{257,129},{384,0},{385... | collective-permute-start | bytes 3158024 | tf_op jit(solution)/shard_map/ppermute | solution.py:154
  6.4 24.1 %collective-permute-start.1 = (f32[2056,128]{1,0:T(8,128)}, f32[2056,128]{1,0:T(8,128)S(1)}, u32[]{:S(2)}, u32[]{:S(2)}) collective-permute-start(f32[2056,128]{1,0:T(8,128)} %products.1.refs_0_), channel_id=1, source_target_pairs={{0,384},{1,129},{128,0},{129,257},{256,128},{257,385},{384,256},{3... | collective-permute-start | bytes 3158024 | tf_op jit(solution)/shard_map/ppermute | solution.py:154
  10.8 31.2 %all-to-all-start = ((s32[16,24,128]{2,1,0:T(8,128)}), s32[16,24,128]{2,1,0:T(8,128)S(1)}, u32[]{:S(2)}, u32[]{:S(2)}) async-start(s32[16,24,128]{2,1,0:T(8,128)} %broadcast_in_dim.2), calls=%async_computation | async-start | bytes 393216 | tf_op jit(solution)/shard_map/all_to_all | solution.py:214
  26.0 16.6 %copy-start = (f32[2056,128]{1,0:T(8,128)S(1)}, f32[2056,128]{1,0:T(8,128)}, u32[]{:S(2)}) copy-start(f32[2056,128]{1,0:T(8,128)} %products.1.refs_0_) | copy-start | bytes 3158020
  30.5 23.2 %collective-permute-start.2 = (f32[2056,128]{1,0:T(8,128)S(1)}, f32[2056,128]{1,0:T(8,128)}, u32[]{:S(2)}, u32[]{:S(2)}) collective-permute-start(f32[2056,128]{1,0:T(8,128)S(1)} %collective-permute-done.refs_1_), channel_id=1, source_target_pairs={{0,128},{1,385},{128,256},{129,1},{256,384},{257,129},{384,0},{385... | collective-permute-start | bytes 3158024 | tf_op jit(solution)/shard_map/ppermute | solution.py:154
  48.8 4.9 %copy-start.1 = (f32[4,256,128]{2,1,0:T(8,128)S(1)}, f32[4,256,128]{2,1,0:T(8,128)}, u32[]{:S(2)}) copy-start(f32[4,256,128]{2,1,0:T(8,128)} %get-tuple-element.32.refs_1_) | copy-start | bytes 1572868
  48.8 4.9 %copy-start.2 = (f32[4,256,128]{2,1,0:T(8,128)S(1)}, f32[4,256,128]{2,1,0:T(8,128)}, u32[]{:S(2)}) copy-start(f32[4,256,128]{2,1,0:T(8,128)} %get-tuple-element.33.refs_2_) | copy-start | bytes 1572868
  48.9 4.9 %copy-start.3 = (f32[4,256,128]{2,1,0:T(8,128)S(1)}, f32[4,256,128]{2,1,0:T(8,128)}, u32[]{:S(2)}) copy-start(f32[4,256,128]{2,1,0:T(8,128)} %get-tuple-element.34.refs_3_) | copy-start | bytes 1572868
  48.9 4.9 %copy-start.4 = (f32[4,256,128]{2,1,0:T(8,128)S(1)}, f32[4,256,128]{2,1,0:T(8,128)}, u32[]{:S(2)}) copy-start(f32[4,256,128]{2,1,0:T(8,128)} %get-tuple-element.35.refs_4_) | copy-start | bytes 1572868
  48.9 19.6 %all-to-all-start.1 = ((f32[8,256,128]{2,1,0:T(8,128)}), f32[8,256,128]{2,1,0:T(8,128)}, u32[]{:S(2)}, u32[]{:S(2)}) async-start(f32[8,256,128]{2,1,0:T(8,128)} %ladder.1), calls=%async_computation.1 | async-start | bytes 2097152 | tf_op jit(solution)/shard_map/all_to_all | solution.py:221
  57.9 30.9 %copy-start.5 = (f32[4,256,128]{2,1,0:T(8,128)S(1)}, f32[4,256,128]{2,1,0:T(8,128)}, u32[]{:S(2)}) copy-start(f32[4,256,128]{2,1,0:T(8,128)} %get-tuple-element.36) | copy-start | bytes 1572868
  57.9 18.0 %collective-permute-start.3 = (f32[4,256,128]{2,1,0:T(8,128)}, f32[4,256,128]{2,1,0:T(8,128)S(1)}, u32[]{:S(2)}, u32[]{:S(2)}) collective-permute-start(f32[4,256,128]{2,1,0:T(8,128)} %get-tuple-element.37), channel_id=1, source_target_pairs={{0,16},{1,113},{8,24},{9,121},{16,32},{17,1},{24,40},{25,9},{32,48... | collective-permute-start | bytes 1572872 | tf_op jit(solution)/shard_map/ppermute | solution.py:158
  61.4 27.4 %collective-permute-start.4 = (f32[4,256,128]{2,1,0:T(8,128)}, f32[4,256,128]{2,1,0:T(8,128)S(1)}, u32[]{:S(2)}, u32[]{:S(2)}) collective-permute-start(f32[4,256,128]{2,1,0:T(8,128)} %get-tuple-element.38), channel_id=1, source_target_pairs={{0,8},{1,121},{8,16},{9,1},{16,24},{17,9},{24,32},{25,17},{32,40},... | collective-permute-start | bytes 1572872 | tf_op jit(solution)/shard_map/ppermute | solution.py:158
  64.9 24.0 %collective-permute-start.5 = (f32[4,256,128]{2,1,0:T(8,128)}, f32[4,256,128]{2,1,0:T(8,128)S(1)}, u32[]{:S(2)}, u32[]{:S(2)}) collective-permute-start(f32[4,256,128]{2,1,0:T(8,128)} %get-tuple-element.39), channel_id=1, source_target_pairs={{0,120},{1,9},{8,0},{9,17},{16,8},{17,25},{24,16},{25,33},{32,24},... | collective-permute-start | bytes 1572872 | tf_op jit(solution)/shard_map/ppermute | solution.py:158
  89.0 41.9 %copy-start.6 = (f32[256,128]{1,0:T(8,128)S(1)}, f32[256,128]{1,0:T(8,128)}, u32[]{:S(2)}) copy-start(f32[256,128]{1,0:T(8,128)} %param.19) | copy-start | bytes 393220
  89.0 34.8 %collective-permute-start.6 = (f32[256,128]{1,0:T(8,128)S(1)}, f32[256,128]{1,0:T(8,128)S(1)}, u32[]{:S(2)}, u32[]{:S(2)}) collective-permute-start(f32[256,128]{1,0:T(8,128)S(1)} %get-tuple-element.47), channel_id=1, source_target_pairs={{0,96},{1,33},{8,104},{9,41},{16,112},{17,49},{24,120},{25,57},{32... | collective-permute-start | bytes 393224 | tf_op jit(solution)/shard_map/ppermute | solution.py:158
  96.1 34.0 %collective-permute-start.7 = (f32[256,128]{1,0:T(8,128)S(1)}, f32[256,128]{1,0:T(8,128)S(1)}, u32[]{:S(2)}, u32[]{:S(2)}) collective-permute-start(f32[256,128]{1,0:T(8,128)S(1)} %reduce_sum.9), channel_id=1, source_target_pairs={{0,504},{8,496},{16,488},{24,480},{32,472},{40,464},{48,456},{56,4... | collective-permute-start | bytes 393224 | tf_op jit(solution)/shard_map/ppermute | solution.py:229
  100.4 30.4 %collective-permute-start.8 = (f32[256,128]{1,0:T(8,128)S(1)}, f32[256,128]{1,0:T(8,128)S(1)}, u32[]{:S(2)}, u32[]{:S(2)}) collective-permute-start(f32[256,128]{1,0:T(8,128)S(1)} %get-tuple-element.45), channel_id=1, source_target_pairs={{0,64},{1,65},{8,72},{9,73},{16,80},{17,81},{24,88},{25,89},{32,96... | collective-permute-start | bytes 393224 | tf_op jit(solution)/shard_map/ppermute | solution.py:158
  105.2 25.6 %collective-permute-start.9 = (f32[256,128]{1,0:T(8,128)S(1)}, f32[256,128]{1,0:T(8,128)S(1)}, u32[]{:S(2)}, u32[]{:S(2)}) collective-permute-start(f32[256,128]{1,0:T(8,128)S(1)} %get-tuple-element.46), channel_id=1, source_target_pairs={{0,32},{1,97},{8,40},{9,105},{16,48},{17,113},{24,56},{25,121},{32... | collective-permute-start | bytes 393224 | tf_op jit(solution)/shard_map/ppermute | solution.py:158
